TPU v7x, 32 devices: a whole 2x2x4 slice. The times are simulated.
32 devices in a mesh: grp: 2 (over y), tm: 4 (over z), height: 2 (over core), head: 2 (over x).
Axes of the slice: x: 2, y: 2, z: 4, core: 2. Of those that a mesh axis runs over, the one named last changes fastest.
Arguments:
- query_video: bfloat16 [32, 16, 16, 3072], P('grp', 'height', 'tm', 'head'), parts along dimension 0, may hold values from -20 to 20
- key_video: bfloat16 [32, 16, 16, 3072], P('grp', 'height', 'tm', 'head'), parts along dimension 0, may hold values from -20 to 20
- value_video: bfloat16 [32, 16, 16, 3072], P('grp', 'height', 'tm', 'head'), parts along dimension 0, may hold values from -6 to 6
- query_text: bfloat16 [512, 3072], P('grp', 'head'), parts along dimension 0, may hold values from -20 to 20
- key_text: bfloat16 [512, 3072], P('grp', 'head'), parts along dimension 0, may hold values from -6 to 6
- value_text: bfloat16 [512, 3072], P('grp', 'head'), parts along dimension 0, may hold values from -6 to 6
- text_valid: int32 [512], P('grp'), parts along dimension 0, may hold values from 0 to 1, as said below
Outputs:
- out_video: bfloat16 [32, 16, 16, 3072], P('grp', 'height', 'tm', 'head'), parts along dimension 0
- out_text: bfloat16 [512, 3072], P('grp', 'head'), parts along dimension 0
There are 2 independent parts, one for each index of `grp`. A program takes and returns all parts, laid end to end along the dimension named above; each array names one. Nothing has to cross between parts.
Inputs may be any that keep to these rules, and one draw needn't show every extreme that they name: `text_valid`: 1 on a leading run of at least 64 positions and 0 on the rest; at least one position is 0.
All inputs are finite; a program needn't handle non-finite values.
Results may differ from a plain program's by a relative error of at most 0.0037.
Values may be sent and summed in bfloat16 or wider, within the bound.
No kernel may reach another device: no remote copies, remote signals or barrier semaphores. Data moves between devices by JAX's collectives and lax.ppermute only.
A program may use at most 192 MiB of HBM per device.

v0:
```python
import math

import jax
import jax.numpy as jnp
from jax import lax
from jax.sharding import PartitionSpec as P

HD = 128
TILE = 4


def with_halo(array, sides, width):
    for axis, dim in sides:
        devices, length = (lax.axis_size(axis), array.shape[dim])
        up = [(i, (i + 1) % devices) for i in range(devices - 1)]
        down = [(j, i) for i, j in up]
        last = lax.slice_in_dim(array, length - width, length, axis=dim)
        initial = lax.slice_in_dim(array, 0, width, axis=dim)
        before = lax.ppermute(last, axis, up)
        after = lax.ppermute(initial, axis, down)
        array = jnp.concatenate([before, array, after], axis=dim)
    return array


def into_tiles(field):
    time_tiles = field.shape[0] // TILE
    row_tiles = field.shape[1] // TILE
    col_tiles = field.shape[2] // TILE
    shaped = field.reshape(time_tiles, TILE, row_tiles, TILE, col_tiles, TILE, field.shape[3])
    shaped = shaped.transpose(0, 2, 4, 1, 3, 5, 6)
    return shaped.reshape(time_tiles, row_tiles, col_tiles, TILE**3, field.shape[3])


def from_tiles(tiles, time_tiles, row_tiles, col_tiles):
    shaped = tiles.reshape(time_tiles, row_tiles, col_tiles, TILE, TILE, TILE, tiles.shape[2])
    shaped = shaped.transpose(0, 3, 1, 4, 2, 5, 6)
    return shaped.reshape(time_tiles * TILE, row_tiles * TILE, col_tiles * TILE, tiles.shape[2])


def shards(query_video, key_video, value_video, query_text, key_text, value_text, text_valid):
    frames = query_video.shape[0]
    features = query_video.shape[3]
    head_count = features // HD
    time_tiles = frames // TILE
    row_tiles = query_video.shape[1] // TILE
    col_tiles = query_video.shape[2] // TILE
    tile_count = time_tiles * row_tiles * col_tiles
    volume = TILE**3
    text_count = query_text.shape[0]
    scale_factor = 1.0 / math.sqrt(HD)
    stacked = jnp.concatenate([key_video, value_video], axis=3)
    padded = with_halo(stacked, (("tm", 2), ("height", 1)), TILE)
    padded = jnp.pad(padded, ((TILE, TILE), (0, 0), (0, 0), (0, 0)))
    grid_shape = (time_tiles + 2, row_tiles + 2, col_tiles + 2, volume, head_count, HD)
    key_grid = into_tiles(padded[:, :, :, :features]).reshape(grid_shape)
    value_grid = into_tiles(padded[:, :, :, features:]).reshape(grid_shape)
    query_tiles = into_tiles(query_video).reshape(tile_count, volume, head_count, HD)
    slot_list = jnp.arange(27, dtype=jnp.int32)
    slot_ids = slot_list[None, :]
    numbering = jnp.arange(tile_count, dtype=jnp.int32)
    tile_time = numbering // (row_tiles * col_tiles)
    tile_row = numbering // col_tiles % row_tiles
    tile_col = numbering % col_tiles
    target_time = tile_time[:, None] + slot_ids // 9 - 1
    target_row = tile_row[:, None] + slot_ids // 3 % 3 - 1
    target_col = tile_col[:, None] + slot_ids % 3 - 1
    global_row = lax.axis_index("height") * row_tiles + target_row
    global_col = lax.axis_index("tm") * col_tiles + target_col
    inside = (target_time >= 0) & (target_time < time_tiles)
    inside = inside & (global_row >= 0) & (global_row < row_tiles * lax.axis_size("height"))
    inside = inside & (global_col >= 0) & (global_col < col_tiles * lax.axis_size("tm"))

    def window_block(grid, slot):
        zero = jnp.zeros((), jnp.int32)
        starts = (slot // 9, slot // 3 % 3, slot % 3, zero, zero, zero)
        block = lax.dynamic_slice(
            grid, starts, (time_tiles, row_tiles, col_tiles, volume, head_count, HD)
        )
        return block.reshape(tile_count, volume, head_count, HD)

    text_keys = key_text.reshape(text_count, head_count, HD)
    text_values = value_text.reshape(text_count, head_count, HD)
    text_queries = query_text.reshape(text_count, head_count, HD)
    text_open = text_valid > 0
    cross_scores = (
        jnp.einsum("qahd,khd->qhak", query_tiles, text_keys, preferred_element_type=jnp.float32)
        * scale_factor
    )
    cross_scores = jnp.where(text_open[None, None, None, :], cross_scores, -jnp.inf)

    def slot_scores(slot, allowed):
        picked = window_block(key_grid, slot)
        scores = (
            jnp.einsum("qahd,qbhd->qhab", query_tiles, picked, preferred_element_type=jnp.float32)
            * scale_factor
        )
        return jnp.where(allowed[:, None, None, None], scores, -jnp.inf)

    def peak_slot(peak, operands):
        scores = slot_scores(operands[0], operands[1])
        return (jnp.maximum(peak, jnp.max(scores, axis=3)), None)

    row_peak, unused = lax.scan(peak_slot, jnp.max(cross_scores, axis=3), (slot_list, inside.T))
    cross_probs = jnp.exp(cross_scores - row_peak[..., None])
    cross_weights = cross_probs.astype(jnp.bfloat16)
    text_part = jnp.einsum(
        "qhak,khd->qahd", cross_weights, text_values, preferred_element_type=jnp.float32
    )

    def add_slot(carry, operands):
        running, total = carry
        slot, allowed = operands
        probs = jnp.exp(slot_scores(slot, allowed) - row_peak[..., None])
        picked = window_block(value_grid, slot)
        running = running + jnp.einsum(
            "qhab,qbhd->qahd",
            probs.astype(jnp.bfloat16),
            picked,
            preferred_element_type=jnp.float32,
        )
        total = total + jnp.sum(probs, axis=3)
        return ((running, total), None)

    (summed, video_total), unused = lax.scan(
        add_slot, (text_part, jnp.sum(cross_probs, axis=3)), (slot_list, inside.T)
    )
    video_out = (summed / video_total.transpose(0, 2, 1)[..., None]).astype(jnp.bfloat16)
    out_video = from_tiles(
        video_out.reshape(tile_count, volume, features), time_tiles, row_tiles, col_tiles
    )
    flat_keys = key_video.reshape(-1, head_count, HD)
    flat_values = value_video.reshape(-1, head_count, HD)
    far_scores = (
        jnp.einsum("khd,nhd->hkn", text_queries, flat_keys, preferred_element_type=jnp.float32)
        * scale_factor
    )
    near_scores = (
        jnp.einsum("khd,jhd->hkj", text_queries, text_keys, preferred_element_type=jnp.float32)
        * scale_factor
    )
    near_scores = jnp.where(text_open[None, None, :], near_scores, -jnp.inf)
    far_peak = lax.pmax(jnp.max(far_scores, axis=2), ("tm", "height"))
    text_peak = jnp.maximum(far_peak, jnp.max(near_scores, axis=2))
    far_probs = jnp.exp(far_scores - text_peak[:, :, None])
    near_probs = jnp.exp(near_scores - text_peak[:, :, None])
    far_total = jnp.sum(far_probs, axis=2).T
    near_total = jnp.sum(near_probs, axis=2).T
    far_summed = jnp.einsum(
        "hkn,nhd->khd",
        far_probs.astype(jnp.bfloat16),
        flat_values,
        preferred_element_type=jnp.float32,
    )
    near_summed = jnp.einsum(
        "hkj,jhd->khd",
        near_probs.astype(jnp.bfloat16),
        text_values,
        preferred_element_type=jnp.float32,
    )
    whole_summed, whole_total = lax.psum((far_summed, far_total), ("tm", "height"))
    finished = (whole_summed + near_summed) / (whole_total + near_total)[:, :, None]
    out_text = finished.astype(jnp.bfloat16).reshape(text_count, features)
    return (out_video, out_text)


def solution(mesh):
    placed = (
        P("grp", "height", "tm", "head"),
        P("grp", "height", "tm", "head"),
        P("grp", "height", "tm", "head"),
        P("grp", "head"),
        P("grp", "head"),
        P("grp", "head"),
        P("grp"),
    )
    return jax.shard_map(
        shards,
        mesh=mesh,
        in_specs=placed,
        out_specs=(P("grp", "height", "tm", "head"), P("grp", "head")),
        check_vma=False,
    )
```

profile of v0, /device:TPU:21, one launch (start us, length us, event | category | flops | bytes accessed | tf_op | source)
XLA Modules:
  0.0 901.7 jit_solution(6479953430431862503)
XLA Ops:
  10.2 3.2 collective-permute-start
  15.5 65.6 %collective-permute-done = bf16[16,8,4,3072]{3,2,1,0:T(4,128)(2,1)S(1)} collective-permute-done((bf16[16,8,4,3072]{3,2,1,0:T(4,128)(2,1)S(1)}, bf16[16,8,4,3072]{3,2,1,0:T(4,128)(2,1)S(1)}, u32[]{:S(2)}, u32[]{:S(2)}) %collective-permute-start) | collective-permute-done | bytes 3145760 | tf_op jit(solution)/shard_map/ppermute | solution.py:19
  81.1 2.9 collective-permute-done.1
  85.7 7.0 pad_maximum_fusion
  92.7 5.1 fusion.69
  99.1 9.0 collective-permute-start.3
  108.1 4.2 reshape.186
  112.3 4.2 reshape.187
  121.0 5.9 multiply_reduce_fusion
  126.9 21.4 %pmax.7 = f32[12,256]{1,0:T(8,128)S(1)} all-reduce(f32[12,256]{1,0:T(8,128)S(1)} %get-tuple-element.360), channel_id=1, replica_groups=mesh['grp'=2,'tm'=4,'height'=2,'head'=2] {'tm','height'}, use_global_device_ids=true, to_apply=%region_9.10 | all-reduce | flops 3072 | bytes 24576 | tf_op jit(solution)/shard_map/pmax | solution.py:142
  148.4 4.0 fusion.27
  152.4 5.7 fusion.44
  158.1 3.2 copy.131
  161.3 4.2 reshape_reshape.12
  178.3 26.7 %psum.15 = f32[256,12]{0,1:T(8,128)S(1)} all-reduce(f32[256,12]{0,1:T(8,128)S(1)} %bitcast.156), channel_id=1, replica_groups=mesh['grp'=2,'tm'=4,'height'=2,'head'=2] {'tm','height'}, use_global_device_ids=true, to_apply=%region_13.14 | all-reduce | flops 3072 | bytes 24576 | tf_op jit(solution)/shard_map/psum | solution.py:160
  207.8 13.3 %all-reduce.3.cloned.1.call-done = f32[256,12,128]{2,0,1:T(8,128)} async-done(((f32[256,12,128]{2,0,1:T(8,128)}), f32[256,12,128]{2,0,1:T(8,128)}) %all-reduce.3.cloned.1.call-update) | async-done | bytes 1572880 | tf_op jit(solution)/shard_map/psum | solution.py:160
  221.1 4.8 fusion.36
  230.5 46.5 %select_maximum_fusion = bf16[24,16,12,3072]{3,2,1,0:T(8,128)(2,1)} fusion(bf16[16,4,12,3072]{3,2,1,0:T(8,128)(2,1)} %collective-permute-done.3, bf16[16,4,12,3072]{3,2,1,0:T(8,128)(2,1)} %collective-permute-done.2, bf16[16,8,4,3072]{3,2,1,0:T(4,128)(2,1)} %copy-done.4, bf16[16,8,4,3072]{3,2,1,0:T(4,128)(2,1)S(1)} %constant_dynamic-update-slice_fusion, ...), kind=kLoop, calls=%fused_computation.19 | loop fusion | flops 254803968 | bytes 47185920 | tf_op jit(solution)/shard_map/concatenate | solution.py:21
  277.1 26.4 %fusion.68 = (bf16[24,16,12,1536]{3,2,1,0:T(8,128)(2,1)}, bf16[24,16,12,1536]{3,2,1,0:T(8,128)(2,1)}) fusion(bf16[24,16,12,3072]{3,2,1,0:T(8,128)(2,1)} %select_maximum_fusion), kind=kLoop, calls=%fused_computation.106 | loop fusion | bytes 56623104 | tf_op jit(solution)/shard_map/slice | solution.py:56
  303.4 26.3 %reshape.181 = bf16[6,4,4,4,3,4,1536]{6,5,4,3,2,1,0:T(4,128)(2,1)} reshape(bf16[24,16,12,1536]{3,2,1,0:T(8,128)(2,1)} %get-tuple-element.357) | data formatting | bytes 28311552 | tf_op jit(solution)/shard_map/reshape | solution.py:29
  329.7 12.7 %copy.130 = bf16[6,4,4,4,3,4,1536]{6,5,3,1,4,2,0:T(4,128)(2,1)} copy(bf16[6,4,4,4,3,4,1536]{6,5,4,3,2,1,0:T(4,128)(2,1)} %reshape.181) | data formatting | bytes 28311552 | tf_op jit(solution)/shard_map/reshape | solution.py:29
  342.4 28.4 %reshape_reshape.13 = bf16[6,4,3,64,12,128]{5,4,3,2,1,0:T(8,128)(2,1)} reshape(bf16[6,4,3,4,4,4,1536]{6,5,4,3,2,1,0:T(4,128)(2,1)} %bitcast.134) | data formatting | bytes 28311552 | tf_op jit(solution)/shard_map/reshape;reshape | solution.py:55
  370.8 15.6 %copy.85 = bf16[6,4,3,64,12,128]{5,3,4,1,0,2:T(8,128)(2,1)} copy(bf16[6,4,3,64,12,128]{5,4,3,2,1,0:T(8,128)(2,1)} %reshape_reshape.13) | data formatting | bytes 28311552 | tf_op jit(solution)/shard_map/while | solution.py:103
  386.4 172.4 %while.28 = (s32[]{:T(128)}, f32[8,12,64]{2,1,0:T(8,128)S(1)}, pred[27,8]{1,0:T(8,128)(4,1)S(1)}, s32[27]{0:T(128)S(1)}, bf16[6,4,3,64,12,128]{5,3,4,1,0,2:T(8,1...) while((s32[]{:T(128)}, f32[8,12,64]{2,1,0:T(8,128)S(1)}, ...), condition=%wide.region_3.4_spmd, body=%wide.region_1.3_spmd.sunk | while | flops 101842976 | bytes 6390297 | solution.py:103
  558.9 4.9 fusion.15
  565.4 26.3 %reshape.183 = bf16[6,4,4,4,3,4,1536]{6,5,4,3,2,1,0:T(4,128)(2,1)} reshape(bf16[24,16,12,1536]{3,2,1,0:T(8,128)(2,1)} %get-tuple-element.356) | data formatting | bytes 28311552 | tf_op jit(solution)/shard_map/reshape | solution.py:29
  591.7 12.7 %copy.129 = bf16[6,4,4,4,3,4,1536]{6,5,3,1,4,2,0:T(4,128)(2,1)} copy(bf16[6,4,4,4,3,4,1536]{6,5,4,3,2,1,0:T(4,128)(2,1)} %reshape.183) | data formatting | bytes 28311552 | tf_op jit(solution)/shard_map/reshape | solution.py:29
  604.4 28.4 %reshape_reshape.14 = bf16[6,4,3,64,12,128]{5,4,3,2,1,0:T(8,128)(2,1)} reshape(bf16[6,4,3,4,4,4,1536]{6,5,4,3,2,1,0:T(4,128)(2,1)} %bitcast.135) | data formatting | bytes 28311552 | tf_op jit(solution)/shard_map/reshape;reshape | solution.py:56
  632.8 15.6 %copy.93 = bf16[6,4,3,64,12,128]{5,3,4,1,0,2:T(8,128)(2,1)} copy(bf16[6,4,3,64,12,128]{5,4,3,2,1,0:T(8,128)(2,1)} %reshape_reshape.14) | data formatting | bytes 28311552 | tf_op jit(solution)/shard_map/while | solution.py:124
  648.4 239.0 %while.29 = (s32[]{:T(128)}, f32[8,64,12,128]{3,1,2,0:T(8,128)S(1)}, f32[8,12,64]{2,1,0:T(8,128)S(1)}, s32[27]{0:T(128)S(1)}, bf16[6,4,3,64,12,128]{5,3,4,1,0,2:...) while((s32[]{:T(128)}, ...), condition=%wide.region_7.8_spmd, body=%wide.region_5.7_spmd.sunk | while | flops 205258784 | bytes 26886740 | solution.py:124
  651.8 2.7 constant_dynamic-slice_fusion.6
  660.7 2.7 constant_dynamic-slice_fusion.6
  669.5 2.7 constant_dynamic-slice_fusion.6
  678.4 2.7 constant_dynamic-slice_fusion.6
  687.2 2.7 constant_dynamic-slice_fusion.6
  696.1 2.7 constant_dynamic-slice_fusion.6
  704.9 2.7 constant_dynamic-slice_fusion.6
  713.8 2.7 constant_dynamic-slice_fusion.6
  722.6 2.7 constant_dynamic-slice_fusion.6
  740.3 2.7 constant_dynamic-slice_fusion.6
  749.2 2.7 constant_dynamic-slice_fusion.6
  766.9 2.7 constant_dynamic-slice_fusion.6
  775.7 2.7 constant_dynamic-slice_fusion.6
  802.3 2.7 constant_dynamic-slice_fusion.6
  828.8 2.7 constant_dynamic-slice_fusion.6
  855.4 2.7 constant_dynamic-slice_fusion.6
  881.9 2.7 constant_dynamic-slice_fusion.6
  891.1 3.3 copy.97
  (395 shorter events, 237.3 us)
Async XLA Ops:
  7.2 214.0 %all-reduce.3.cloned.1.call-start = ((), (), s32[]{:S(2)}) async-start(), calls=%async_computation | async-start | bytes 3145728 | tf_op jit(solution)/shard_map/psum | solution.py:160
  7.2 2.2 copy-start.6
  10.2 70.9 %collective-permute-start = (bf16[16,8,4,3072]{3,2,1,0:T(4,128)(2,1)S(1)}, bf16[16,8,4,3072]{3,2,1,0:T(4,128)(2,1)S(1)}, u32[]{:S(2)}, u32[]{:S(2)}) collective-permute-start(bf16[16,8,4,3072]{3,2,1,0:T(4,128)(2,1)S(1)} %constant_dynamic-update-slice_fusion), channel_id=1, source_target_pairs={{0,4},{4,8},{8,12},{1,5},{5,9},{9,13},{2,6},{6,10},{10,14},{3,7},{... | collective-permute-start | bytes 9437192 | tf_op jit(solution)/shard_map/ppermute | solution.py:19
  13.4 70.5 %collective-permute-start.1 = (bf16[16,8,4,3072]{3,2,1,0:T(4,128)(2,1)S(1)}, bf16[16,8,4,3072]{3,2,1,0:T(4,128)(2,1)S(1)}, u32[]{:S(2)}, u32[]{:S(2)}) collective-permute-start(bf16[16,8,4,3072]{3,2,1,0:T(4,128)(2,1)S(1)} %constant_dynamic-update-slice_fusion), channel_id=1, source_target_pairs={{4,0},{8,4},{12,8},{5,1},{9,5},{13,9},{6,2},{10,6},{14,10},{7,3},{... | collective-permute-start | bytes 9437192 | tf_op jit(solution)/shard_map/ppermute | solution.py:20
  81.1 2.9 copy-start.3
  84.0 1.7 copy-start.4
  97.8 132.7 %collective-permute-start.2 = (bf16[16,4,12,3072]{3,2,1,0:T(8,128)(2,1)}, bf16[16,4,12,3072]{3,2,1,0:T(8,128)(2,1)}, u32[]{:S(2)}, u32[]{:S(2)}) collective-permute-start(bf16[16,4,12,3072]{3,2,1,0:T(8,128)(2,1)} %get-tuple-element.358), channel_id=1, source_target_pairs={{0,2},{1,3},{4,6},{5,7},{8,10},{9,11},{12,14},{13,15},{16,18},{17,... | collective-permute-start | bytes 14155784 | tf_op jit(solution)/shard_map/ppermute | solution.py:19
  99.1 131.4 %collective-permute-start.3 = (bf16[16,4,12,3072]{3,2,1,0:T(8,128)(2,1)}, bf16[16,4,12,3072]{3,2,1,0:T(8,128)(2,1)}, u32[]{:S(2)}, u32[]{:S(2)}) collective-permute-start(bf16[16,4,12,3072]{3,2,1,0:T(8,128)(2,1)} %get-tuple-element.359), channel_id=1, source_target_pairs={{2,0},{3,1},{6,4},{7,5},{10,8},{11,9},{14,12},{15,13},{18,16},{19,... | collective-permute-start | bytes 14155784 | tf_op jit(solution)/shard_map/ppermute | solution.py:20
  121.0 27.4 %copy-start.10 = (s32[256]{0:T(256)S(1)}, s32[256]{0:T(256)}, u32[]{:S(2)}) copy-start(s32[256]{0:T(256)} %param.17) | copy-start | bytes 3076
  148.4 4.0 copy-start.5
  165.5 7.2 slice-start
  167.7 5.0 slice-start.1
  170.0 2.8 copy-start
  172.8 1.7 copy-start.2
  370.8 15.6 %copy-start.7 = (bf16[8,64,12,128]{3,1,2,0:T(8,128)(2,1)S(1)}, bf16[8,64,12,128]{3,1,2,0:T(8,128)(2,1)}, u32[]{:S(2)}) copy-start(bf16[8,64,12,128]{3,1,2,0:T(8,128)(2,1)} %copy.86) | copy-start | bytes 4718596
  386.4 177.3 %copy-start.9 = (bf16[256,1536]{0,1:T(8,128)(2,1)S(1)}, bf16[256,1536]{0,1:T(8,128)(2,1)}, u32[]{:S(2)}) copy-start(bf16[256,1536]{0,1:T(8,128)(2,1)} %copy.88) | copy-start | bytes 2359300
  558.9 4.9 copy-start.1
  651.8 2.7 copy-start.8
  660.7 2.7 copy-start.8
  669.5 2.7 copy-start.8
  678.4 2.7 copy-start.8
  687.2 2.7 copy-start.8
  696.1 2.7 copy-start.8
  704.9 2.7 copy-start.8
  713.8 2.7 copy-start.8
  722.6 2.7 copy-start.8
  731.5 2.7 copy-start.8
  740.3 2.7 copy-start.8
  749.2 2.7 copy-start.8
  758.0 2.7 copy-start.8
  766.9 2.7 copy-start.8
  775.7 2.7 copy-start.8
  784.6 2.7 copy-start.8
  793.4 2.7 copy-start.8
  802.3 2.7 copy-start.8
  811.1 2.7 copy-start.8
  820.0 2.7 copy-start.8
  828.8 2.7 copy-start.8
  837.7 2.7 copy-start.8
  846.5 2.7 copy-start.8
  855.4 2.7 copy-start.8
  864.2 2.7 copy-start.8
  873.1 2.7 copy-start.8
  881.9 2.7 copy-start.8
Sparse Core Ops, SparseCore 0:
  158.2 62.8 all-reduce.2
where the time goes:
time: 919 us; the launch traced here: 902 us
  local copies, waits for them, and re-layouts  388 us (42%)
  loops' own time  166 us (18%)
  matrix products  121 us (13%)
  waiting for transfers between devices  81.8 us (9%)
  other arithmetic  65.6 us (7%)
  blocking collectives  48.2 us (5%)
  starting transfers between devices  15.6 us (2%)
  between operations  14.8 us (2%)
    dynamic_slice x54, local copies, waits for them, and re-layouts, window_block(): lax.dynamic_slice(grid, starts, (time_tiles, row_tiles, col_tiles, volume...  114 us
    another operation x1, loops' own time, shards(): lax.scan(peak_slot, jnp.max(cross_scores, axis=3), (slot_list, inside.T))  87.3 us
    reshape x5, local copies, waits for them, and re-layouts, into_tiles(): field.reshape(time_tiles, TILE, row_tiles, TILE, col_tiles, TILE, field.s...  81.3 us
    another operation x1, loops' own time, shards(): lax.scan(add_slot, (text_part, jnp.sum(cross_probs, axis=3)), (slot_list,...  79.1 us
    ppermute x2, waiting for transfers between devices, with_halo(): before = lax.ppermute(last, axis, up)  65.6 us
    concatenate x2, other arithmetic, with_halo(): array = jnp.concatenate([before, array, after], axis=dim)  53.6 us
    dot_general x54, matrix products, slot_scores(): jnp.einsum('qahd,qbhd->qhab', query_tiles, picked, preferred_element_type...  53 us
    dot_general x27, matrix products, add_slot(): jnp.einsum('qhab,qbhd->qahd', probs.astype(jnp.bfloat16), picked, preferr...  44 us
  transfers between devices with their start and end apart: 5, of which 3 were waited for; matrix products, arithmetic and copies ran while one was open for 7% of the time, Pallas kernels for 0%

commit v1 on v0

v1 whole, which is shorter than its diff:
```python
import functools
import math

import jax
import jax.numpy as jnp
from jax import lax
from jax.experimental import pallas as pl
from jax.experimental.pallas import tpu as pltpu
from jax.sharding import PartitionSpec as P

HD = 128
TILE = 4
VOL = TILE**3
BF16 = jnp.bfloat16
F32 = jnp.float32
SCALE = 1.0 / math.sqrt(HD)
SCALE_2 = SCALE * math.log2(math.e)
VMEM = 63 << 20
THIRD = 32


def cost(microseconds):
    return pl.CostEstimate(flops=int(microseconds * 1.15e9), bytes_accessed=1, transcendentals=0)


def head_groups(heads):
    if heads % 6:
        return [(start, 1) for start in range(heads)]
    unit = heads // 6
    return [(4 * unit, unit), (0, 2 * unit), (2 * unit, 2 * unit), (5 * unit, unit)]


def dot_nt(a, b):
    return lax.dot_general(a, b, (((1,), (1,)), ((), ())), preferred_element_type=F32)


def dot_nn(a, b):
    return lax.dot_general(a, b, (((1,), (0,)), ((), ())), preferred_element_type=F32)


def weigh(p, v):
    return dot_nn(p.astype(BF16), jnp.concatenate([v, jnp.ones_like(v)], axis=1))


def pack_body(scal, k_ref, v_ref, *rest):
    kv_ref = rest[-1] if len(rest) == 1 else rest[2]
    for which, ref in enumerate((k_ref, v_ref)):
        for head in range(kv_ref.shape[1]):
            lanes = slice(head * HD, (head + 1) * HD)
            for r in range(ref.shape[1] // TILE):
                kv_ref[which, head, 0, r] = ref[:, r * TILE : (r + 1) * TILE, :, lanes].reshape(VOL, HD)
    if len(rest) > 1:
        rest[3][...] = rest[0][...]
        rest[4][...] = rest[1][...]


def pack_group(scal, key_video, value_video, start, count, give):
    frames, rows, cols, features = key_video.shape
    time_tiles = frames // TILE
    row_tiles = rows // TILE
    block = pl.BlockSpec((TILE, rows, cols, count * HD), lambda t, s: (t, 0, 0, start // count))
    in_specs = [block, block]
    out_specs = [pl.BlockSpec((2, count, 1, row_tiles, VOL, HD), lambda t, s: (0, 0, t, 0, 0, 0))]
    out_shape = [jax.ShapeDtypeStruct((2, count, time_tiles, row_tiles, VOL, HD), BF16)]
    operands = [key_video, value_video]
    if give:
        in_specs += [pl.BlockSpec((TILE, rows, cols, features // 2), lambda t, s: (t, 0, 0, s[0]))] * 2
        out_specs += [pl.BlockSpec((TILE, rows, cols, features // 2), lambda t, s: (t, 0, 0, 0))] * 2
        out_shape += [jax.ShapeDtypeStruct((frames, rows, cols, features // 2), BF16)] * 2
        operands += [key_video, value_video]
    return pl.pallas_call(
        pack_body,
        grid_spec=pltpu.PrefetchScalarGridSpec(
            num_scalar_prefetch=1, grid=(time_tiles,), in_specs=in_specs, out_specs=out_specs
        ),
        out_shape=out_shape,
        compiler_params=pltpu.CompilerParams(vmem_limit_bytes=VMEM),
        cost_estimate=cost(0),
        name="pack",
    )(scal, *operands)


def video_body(scal, valid_ref, q_ref, own, left, right, edge, edge_left, edge_right, tk_ref, tv_ref, *rest):
    out_ref = rest[-1]
    near = scal[0]
    has_left = scal[1] > 0
    has_right = scal[2] > 0
    time_tiles = q_ref.shape[0] // TILE
    open_keys = valid_ref[...] > 0
    far_rows = pl.ds((1 - near) * TILE, TILE)
    near_rows = pl.ds(near * TILE, TILE)

    def load(ref, which, first, last):
        picked = ref[which, 0, first:last]
        return picked.reshape(picked.shape[0] * picked.shape[1] * VOL, HD)

    def scores(t):
        first = max(t - 1, 0)
        last = min(t + 1, time_tiles - 1) + 1
        frames = slice(t * TILE, (t + 1) * TILE)
        q_far = q_ref[frames, far_rows, :, :].reshape(VOL, HD)
        q_near = q_ref[frames, near_rows, :, :].reshape(VOL, HD)
        q_all = jnp.concatenate([q_far, q_near], axis=0)
        s_text = jnp.where(open_keys, dot_nt(q_all, tk_ref[...]), -jnp.inf)
        wide = [(s_text, None, None)]
        for ref, ok in ((own, None), (left, has_left), (right, has_right)):
            wide.append((dot_nt(q_all, load(ref, 0, first, last)), ref, ok))
        thin = []
        for ref, ok in ((edge, None), (edge_left, has_left), (edge_right, has_right)):
            thin.append((dot_nt(q_near, load(ref, 0, first, last)), ref, ok))
        return first, last, wide, thin

    def peak(entries):
        tops = []
        for s, _, ok in entries:
            top = jnp.max(s, axis=1, keepdims=True)
            tops.append(top if ok is None else jnp.where(ok, top, -jnp.inf))
        return functools.reduce(jnp.maximum, tops)

    def gather(entries, m, first, last):
        summed = None
        for s, ref, ok in entries:
            base = m if ok is None else jnp.where(ok, m, jnp.inf)
            v = tv_ref[...] if ref is None else load(ref, 1, first, last)
            part = weigh(jnp.exp2((s - base) * SCALE_2), v)
            summed = part if summed is None else summed + part
        return summed

    def finish(t, state):
        first, last, wide, thin = state
        frames = slice(t * TILE, (t + 1) * TILE)
        m_all = peak(wide)
        m_near = jnp.maximum(m_all[VOL:], peak(thin))
        m_all = jnp.concatenate([m_all[:VOL], m_near], axis=0)
        summed = gather(wide, m_all, first, last)
        far = summed[:VOL]
        close = summed[VOL:] + gather(thin, m_near, first, last)
        for rows, value in ((far_rows, far), (near_rows, close)):
            out = value[:, :HD] / value[:, HD:]
            out_ref[frames, rows, :, :] = out.astype(BF16).reshape(TILE, TILE, TILE, HD)

    state = scores(0)
    for t in range(time_tiles):
        following = scores(t + 1) if t + 1 < time_tiles else None
        finish(t, state)
        state = following


def video_group(scal, valid, query_video, tiles, key_text, value_text, prior, start, count):
    frames, rows, cols, _ = query_video.shape
    tokens = frames * rows * cols
    time_tiles = frames // TILE
    text = key_text.shape[0]
    head = pl.BlockSpec((frames, rows, cols, HD), lambda i, s: (0, 0, 0, start + i))
    wide = pl.BlockSpec((2, 1, time_tiles, 2, VOL, HD), lambda i, s: (0, i, 0, 0, 0, 0))
    thin = pl.BlockSpec((2, 1, time_tiles, 1, VOL, HD), lambda i, s: (0, i, 0, 1 - s[0], 0, 0))
    word = pl.BlockSpec((text, HD), lambda i, s: (0, start + i))
    specs = [pl.BlockSpec((1, text), lambda i, s: (0, 0)), head, wide, wide, wide, thin, thin, thin, word, word]
    operands = [scal, valid, query_video, *tiles, key_text, value_text]
    aliases = {}
    if prior is not None:
        specs.append(pl.BlockSpec(memory_space=pl.ANY))
        aliases = {len(operands): 0}
        operands.append(prior)
    return pl.pallas_call(
        video_body,
        grid_spec=pltpu.PrefetchScalarGridSpec(
            num_scalar_prefetch=1,
            grid=(count,),
            in_specs=specs,
            out_specs=head,
        ),
        out_shape=jax.ShapeDtypeStruct(query_video.shape, BF16),
        input_output_aliases=aliases,
        compiler_params=pltpu.CompilerParams(vmem_limit_bytes=VMEM),
        cost_estimate=cost(0),
        name="video",
    )(*operands)


def lane_of(shape):
    return lax.broadcasted_iota(jnp.int32, shape, len(shape) - 1)


def send_logs(logs):
    high = logs.astype(BF16).astype(F32)
    mid = (logs - high).astype(BF16).astype(F32)
    low = logs - high - mid
    lane = lane_of(logs.shape)
    whole = jnp.where(lane < THIRD, high, 0.0)
    whole = jnp.where((lane >= THIRD) & (lane < 2 * THIRD), pltpu.roll(mid, THIRD, 1), whole)
    whole = jnp.where((lane >= 2 * THIRD) & (lane < 3 * THIRD), pltpu.roll(low, 2 * THIRD, 1), whole)
    return jnp.where(lane == HD - 1, 1.0, whole).astype(BF16)


def read_logs(sent):
    whole = sent.astype(F32)
    logs = whole + pltpu.roll(whole, HD - THIRD, 1) + pltpu.roll(whole, HD - 2 * THIRD, 1)
    return jnp.where(whole[:, HD - 1 :] > 0, logs, -jnp.inf)


def text_body(scal, valid_ref, q_ref, k_ref, v_ref, k2_ref, v2_ref, tk_ref, tv_ref, sum_ref, log_ref, send_ref):
    at = pl.program_id(0)
    heads = pl.num_programs(0) - 1

    @pl.when(at < heads)
    def _():
        tokens = k_ref.shape[0] * k_ref.shape[1] * k_ref.shape[2]
        q = q_ref[...]
        s_own = dot_nt(q, k_ref[...].reshape(tokens, HD))
        s_pair = dot_nt(q, k2_ref[...].reshape(tokens, HD))
        s_near = jnp.where((valid_ref[...] > 0) & (scal[3] > 0), dot_nt(q, tk_ref[...]), -jnp.inf)
        m = functools.reduce(jnp.maximum, [jnp.max(s, axis=1, keepdims=True) for s in (s_own, s_pair, s_near)])
        both = weigh(jnp.exp2((s_own - m) * SCALE_2), v_ref[...].reshape(tokens, HD))
        both = both + weigh(jnp.exp2((s_pair - m) * SCALE_2), v2_ref[...].reshape(tokens, HD))
        both = both + weigh(jnp.exp2((s_near - m) * SCALE_2), tv_ref[...])
        total = both[:, HD:]
        out = both[:, :HD] / total
        sum_ref[0] = out
        send_ref[0] = out.astype(BF16)
        logs = m * SCALE + jnp.log(total)
        prior = jnp.where(at == 0, 0.0, log_ref[...])
        log_ref[...] = jnp.where(lane_of(logs.shape) == at, logs, prior)

    @pl.when(at == heads)
    def _():
        send_ref[0] = send_logs(log_ref[...])


def text_partial(scal, valid, query_text, key_video, value_video, key_pair, value_pair, key_text, value_text):
    frames, rows, cols, features = key_pair.shape
    heads = features // HD
    text = query_text.shape[0]

    def own_head(i, s):
        return s[4] + jnp.minimum(i, heads - 1)

    word = pl.BlockSpec((text, HD), lambda i, s: (0, own_head(i, s)))
    block = pl.BlockSpec((frames, rows, cols, HD), lambda i, s: (0, 0, 0, own_head(i, s)))
    pair = pl.BlockSpec((frames, rows, cols, HD), lambda i, s: (0, 0, 0, jnp.minimum(i, heads - 1)))
    return pl.pallas_call(
        text_body,
        grid_spec=pltpu.PrefetchScalarGridSpec(
            num_scalar_prefetch=1,
            grid=(heads + 1,),
            in_specs=[pl.BlockSpec((1, text), lambda i, s: (0, 0)), word, block, block, pair, pair, word, word],
            out_specs=[
                pl.BlockSpec((1, text, HD), lambda i, s: (jnp.minimum(i, heads - 1), 0, 0)),
                pl.BlockSpec((text, HD), lambda i, s: (0, 0)),
                pl.BlockSpec((1, text, HD), lambda i, s: (i, 0, 0)),
            ],
        ),
        out_shape=[
            jax.ShapeDtypeStruct((heads, text, HD), F32),
            jax.ShapeDtypeStruct((text, HD), F32),
            jax.ShapeDtypeStruct((heads + 1, text, HD), BF16),
        ],
        compiler_params=pltpu.CompilerParams(vmem_limit_bytes=VMEM),
        cost_estimate=cost(0),
        name="text",
    )(scal, valid, query_text, key_video, value_video, key_pair, value_pair, key_text, value_text)


def combine(parts, heads):
    logs = [part[1] for part in parts]
    top = functools.reduce(jnp.maximum, logs)
    weights = [jnp.exp(log - top) for log in logs]
    total = functools.reduce(jnp.add, weights)
    weights = [weight / total for weight in weights]
    outs = []
    for head in range(heads):
        terms = [weight[:, head : head + 1] * part[0](head) for weight, part in zip(weights, parts)]
        outs.append(functools.reduce(jnp.add, terms))
    return outs, top + jnp.log(total)


def join_body(sum_ref, log_ref, got_ref, out_ref):
    heads = sum_ref.shape[0]
    own = (lambda head: sum_ref[head], log_ref[...])
    got = (lambda head: got_ref[head].astype(F32), read_logs(got_ref[heads]))
    outs, logs = combine([own, got], heads)
    for head in range(heads):
        out_ref[head] = outs[head].astype(BF16)
    out_ref[heads] = send_logs(logs)


def join(sums, logs, got):
    return pl.pallas_call(
        join_body,
        out_shape=jax.ShapeDtypeStruct(got.shape, BF16),
        compiler_params=pltpu.CompilerParams(vmem_limit_bytes=VMEM),
        cost_estimate=cost(0),
        name="join",
    )(sums, logs, got)


def finish_body(scal, own_ref, got_ref, out_ref):
    heads = own_ref.shape[0] - 1
    low = scal[5] > 0
    parts = []
    for flag in (low, jnp.logical_not(low)):

        def pick(index, flag=flag):
            return jnp.where(flag, own_ref[index].astype(F32), got_ref[index].astype(F32))

        parts.append((pick, read_logs(pick(heads))))
    outs, _ = combine(parts, heads)
    for head in range(heads):
        out_ref[:, head * HD : (head + 1) * HD] = outs[head].astype(BF16)


def finish(scal, own, got):
    heads, text, _ = own.shape
    return pl.pallas_call(
        finish_body,
        grid_spec=pltpu.PrefetchScalarGridSpec(
            num_scalar_prefetch=1,
            grid=(1,),
            in_specs=[pl.BlockSpec(own.shape, lambda i, s: (0, 0, 0))] * 2,
            out_specs=pl.BlockSpec((text, (heads - 1) * HD), lambda i, s: (0, 0)),
        ),
        out_shape=jax.ShapeDtypeStruct((text, (heads - 1) * HD), BF16),
        compiler_params=pltpu.CompilerParams(vmem_limit_bytes=VMEM),
        cost_estimate=cost(0),
        name="finish",
    )(scal, own, got)


def after(value, *others):
    return lax.optimization_barrier((value, *others))[0]


def shards(query_video, key_video, value_video, query_text, key_text, value_text, text_valid):
    features = query_video.shape[3]
    heads = features // HD
    strips = lax.axis_size("tm")
    strip = lax.axis_index("tm")
    half = lax.axis_index("height")
    half_heads = heads // 2
    half_features = features // 2

    def swap(array):
        return lax.ppermute(array, "height", [(0, 1), (1, 0)])

    up = [(i, i + 1) for i in range(strips - 1)]
    down = [(i + 1, i) for i in range(strips - 1)]
    scal = jnp.stack(
        [1 - half, strip > 0, strip < strips - 1, strip == 0, half * half_heads, strip < strips // 2]
    ).astype(jnp.int32)
    valid = text_valid.reshape(1, -1)
    groups = head_groups(heads)

    def to_neighbours(own):
        return lax.ppermute(own, "tm", up), lax.ppermute(own, "tm", down)

    owns = []
    edges = []
    pairs = []
    for index, (start, count) in enumerate(groups):
        packed = pack_group(scal, key_video, value_video, start, count, index == 0)
        owns.append(packed[0])
        pairs += packed[1:]
    key_pair, value_pair = swap(pairs[0]), swap(pairs[1])
    edges = [swap(own) for own in owns]
    sums, logs, sent = text_partial(
        scal, valid, query_text, key_video, value_video, key_pair, value_pair, key_text, value_text
    )

    middle = strips // 2
    for step in range(1, middle):
        got = lax.ppermute(sent, "tm", [(step - 1, step), (strips - step, strips - step - 1)])
        sent = join(sums, logs, got)
    got = lax.ppermute(sent, "tm", [(middle - 1, middle), (middle, middle - 1)])
    mine = finish(scal, sent, got)
    for step in range(middle - 1, 0, -1):
        got = lax.ppermute(mine, "tm", [(step, step - 1), (strips - step - 1, strips - step)])
        mine = jnp.where((strip == step - 1) | (strip == strips - step), got, mine)
    other = swap(mine)
    first = half == 0
    out_text = jnp.concatenate([jnp.where(first, mine, other), jnp.where(first, other, mine)], axis=1)

    out_video = None
    sides = [to_neighbours(own) for own in owns[:2]]
    for index, (start, count) in enumerate(groups):
        left, right = sides[index]
        if out_video is not None:
            left, right = after(left, out_video), after(right, out_video)
        edge_left, edge_right = swap(left), swap(right)
        if index + 2 < len(groups):
            sides.append(to_neighbours(after(owns[index + 2], edge_left, edge_right)))
        tiles = (owns[index], left, right, edges[index], edge_left, edge_right)
        out_video = video_group(scal, valid, query_video, tiles, key_text, value_text, out_video, start, count)
    return (out_video, out_text)


def solution(mesh):
    if mesh.shape["height"] != 2 or mesh.shape["tm"] % 2:
        raise ValueError("unsupported mesh")
    placed = (
        P("grp", "height", "tm", "head"),
        P("grp", "height", "tm", "head"),
        P("grp", "height", "tm", "head"),
        P("grp", "head"),
        P("grp", "head"),
        P("grp", "head"),
        P("grp"),
    )
    return jax.shard_map(
        shards,
        mesh=mesh,
        in_specs=placed,
        out_specs=(P("grp", "height", "tm", "head"), P("grp", "head")),
        check_vma=False,
    )
```

time: 919 us -> 137 us (0.15)
  the two profiles are of different devices: /device:TPU:21 before, /device:TPU:0 now
where the time goes in v1:
time: 137 us; the launch traced here: 136 us
  Pallas kernels  64.9 us (47%)
  waiting for transfers between devices  32.4 us (24%)
  starting transfers between devices  31.6 us (23%)
  other arithmetic  3.02 us (2%)
  local copies, waits for them, and re-layouts  2.75 us (2%)
    pallas_call x4, Pallas kernels, video_group(): pl.pallas_call(video_body, grid_spec=pltpu.PrefetchScalarGridSpec(num_sca...  32.5 us
    ppermute x8, starting transfers between devices, to_neighbours(): return (lax.ppermute(own, 'tm', up), lax.ppermute(own, 'tm', down))  23.8 us
    pallas_call x4, Pallas kernels, pack_group(): pl.pallas_call(pack_body, grid_spec=pltpu.PrefetchScalarGridSpec(num_scal...  17 us
    ppermute x1, waiting for transfers between devices, shards(): lax.ppermute(mine, 'tm', [(step, step - 1), (strips - step - 1, strips -...  15.9 us
    ppermute x8, waiting for transfers between devices, to_neighbours(): return (lax.ppermute(own, 'tm', up), lax.ppermute(own, 'tm', down))  13.1 us
    pallas_call x1, Pallas kernels, text_partial(): pl.pallas_call(text_body, grid_spec=pltpu.PrefetchScalarGridSpec(num_scal...  9.46 us
    pallas_call x1, Pallas kernels, finish(): pl.pallas_call(finish_body, grid_spec=pltpu.PrefetchScalarGridSpec(num_sc...  3.27 us
    ppermute x15, starting transfers between devices, swap(): return lax.ppermute(array, 'height', [(0, 1), (1, 0)])  3.12 us
  transfers between devices with their start and end apart: 26, of which 8 were waited for; matrix products, arithmetic and copies ran while one was open for 2% of the time, Pallas kernels for 40%

profile of v1, /device:TPU:0, one launch (start us, length us, event | category | flops | bytes accessed | tf_op | source)
XLA Modules:
  0.0 135.6 jit_solution(1802767618072831501)
XLA Ops:
  0.6 0.6 stack.43.scal
  1.3 4.6 %pack.6 = (bf16[2,2,4,2,64,128]{5,4,3,2,1,0:T(8,128)(2,1)}, bf16[16,8,4,768]{3,2,1,0:T(4,128)(2,1)}, bf16[16,8,4,768]{3,2,1,0:T(4,128)(2,1)}) custom-call(s32[6]{0:T(128)} %stack.43.scal, bf16[16,8,4,1536]{3,2,1,0:T(4,128)(2,1)} %k_ref.9, bf16[16,8,4,1536]{3,2,1,0:T(4,128)(2,1)} %v_ref.9, bf16[16,8,4,1536]{3,2,1,0:T(4,128)(2,1)} %k_ref.9, ...), custom_call_target="tpu_custom_call" | custom-call | bytes 1 | tf_op jit(solution)/shard_map/pack/pallas_call | solution.py:71
  5.8 0.5 collective-permute-start.20
  6.3 5.7 %collective-permute-start.1 = (bf16[2,2,4,2,64,128]{5,4,3,2,1,0:T(8,128)(2,1)}, bf16[2,2,4,2,64,128]{5,4,3,2,1,0:T(8,128)(2,1)}, u32[]{:S(2)}, u32[]{:S(2)}) collective-permute-start(bf16[2,2,4,2,64,128]{5,4,3,2,1,0:T(8,128)(2,1)} %get-tuple-element.16.own), channel_id=1, source_target_pairs={{0,4},{4,8},{8,12},{1,5},{5,9},{9,13},{2,6},{6,10},{10,14},{3,7},{... | collective-permute-start | bytes 1572872 | tf_op jit(solution)/shard_map/ppermute | solution.py:354
  12.1 1.3 collective-permute-start.2
  13.4 4.2 %pack.5.own = bf16[2,4,4,2,64,128]{5,4,3,2,1,0:T(8,128)(2,1)} custom-call(s32[6]{0:T(128)} %stack.43.scal, bf16[16,8,4,1536]{3,2,1,0:T(4,128)(2,1)} %k_ref.9, bf16[16,8,4,1536]{3,2,1,0:T(4,128)(2,1)} %v_ref.9), custom_call_target="tpu_custom_call" | custom-call | bytes 1 | tf_op jit(solution)/shard_map/pack/pallas_call | solution.py:71
  17.6 1.3 collective-permute-start.7
  18.9 4.1 %collective-permute-done.1.left = bf16[2,2,4,2,64,128]{5,4,3,2,1,0:T(8,128)(2,1)} collective-permute-done((bf16[2,2,4,2,64,128]{5,4,3,2,1,0:T(8,128)(2,1)}, bf16[2,2,4,2,64,128]{5,4,3,2,1,0:T(8,128)(2,1)}, u32[]{:S(2)}, u32[]{:S(2)}) %collective-permute-start.1) | collective-permute-done | bytes 524320 | tf_op jit(solution)/shard_map/ppermute | solution.py:354
  23.0 5.3 %collective-permute-start = (bf16[2,4,4,2,64,128]{5,4,3,2,1,0:T(8,128)(2,1)}, bf16[2,4,4,2,64,128]{5,4,3,2,1,0:T(8,128)(2,1)}, u32[]{:S(2)}, u32[]{:S(2)}) collective-permute-start(bf16[2,4,4,2,64,128]{5,4,3,2,1,0:T(8,128)(2,1)} %pack.5.own), channel_id=1, source_target_pairs={{0,4},{4,8},{8,12},{1,5},{5,9},{9,13},{2,6},{6,10},{10,14},{3,7},{... | collective-permute-start | bytes 3145736 | tf_op jit(solution)/shard_map/ppermute | solution.py:354
  28.3 0.8 collective-permute-done.2.right
  29.1 0.5 collective-permute-start.4
  29.6 0.1 collective-permute-start.5
  29.7 0.3 copy-done.1
  30.0 9.5 %text.1 = (f32[6,256,128]{2,1,0:T(8,128)}, f32[256,128]{1,0:T(8,128)}, bf16[7,256,128]{2,1,0:T(8,128)(2,1)}) custom-call(s32[6]{0:T(128)} %stack.43.scal, s32[1,256]{1,0:T(1,128)} %bitcast.7, bf16[256,1536]{1,0:T(8,128)(2,1)} %q_ref.9, bf16[16,8,4,1536]{3,2,1,0:T(4,128)(2,1)} %k_ref.9, bf16[16,8,4,1536]{3,2,1,0:T(4,128)(2,1)} %v_ref.9, ...), custom_call_target="tpu_custom_call" | custom-call | bytes 1 | tf_op jit(solution)/shard_map/text/pallas_call | solution.py:241
  39.5 2.7 %collective-permute-start.22 = (bf16[7,256,128]{2,1,0:T(8,128)(2,1)}, bf16[7,256,128]{2,1,0:T(8,128)(2,1)S(1)}, u32[]{:S(2)}, u32[]{:S(2)}) collective-permute-start(bf16[7,256,128]{2,1,0:T(8,128)(2,1)} %get-tuple-element.29), channel_id=1, source_target_pairs={{0,4},{12,8},{1,5},{13,9},{2,6},{14,10},{3,7},{15,11},{16,20},{28,... | collective-permute-start | bytes 1376264 | tf_op jit(solution)/shard_map/ppermute | solution.py:371
  42.2 0.3 collective-permute-start.11
  42.5 6.2 %video.4.rest_0_ = bf16[16,8,4,1536]{3,2,1,0:T(4,128)(2,1)} custom-call(s32[6]{0:T(128)} %stack.43.scal, s32[1,256]{1,0:T(1,128)} %bitcast.8, bf16[16,8,4,1536]{3,2,1,0:T(4,128)(2,1)} %q_ref.8, bf16[2,2,4,2,64,128]{5,4,3,2,1,0:T(8,128)(2,1)} %get-tuple-element.16.own, bf16[2,2,4,2,64,128]{5,4,3,2,1,0:T(8,128)(2,1)} %collective-permute-done.1.left, ...), custom_call_target="tpu_custom_call" | custom-call | bytes 1 | tf_op jit(solution)/shard_map/video/pallas_call | solution.py:165
  48.7 1.6 %collective-permute-done.7.right = bf16[2,4,4,2,64,128]{5,4,3,2,1,0:T(8,128)(2,1)} collective-permute-done((bf16[2,4,4,2,64,128]{5,4,3,2,1,0:T(8,128)(2,1)}, bf16[2,4,4,2,64,128]{5,4,3,2,1,0:T(8,128)(2,1)}, u32[]{:S(2)}, u32[]{:S(2)}) %collective-permute-start.7) | collective-permute-done | bytes 1048608 | tf_op jit(solution)/shard_map/ppermute | solution.py:354
  50.4 4.2 %pack.7.own = bf16[2,4,4,2,64,128]{5,4,3,2,1,0:T(8,128)(2,1)} custom-call(s32[6]{0:T(128)} %stack.43.scal, bf16[16,8,4,1536]{3,2,1,0:T(4,128)(2,1)} %k_ref.9, bf16[16,8,4,1536]{3,2,1,0:T(4,128)(2,1)} %v_ref.9), custom_call_target="tpu_custom_call" | custom-call | bytes 1 | tf_op jit(solution)/shard_map/pack/pallas_call | solution.py:71
  54.6 0.5 collective-permute-start.6
  55.1 1.3 collective-permute-start.12
  56.4 2.9 %collective-permute-done.22.got_ref = bf16[7,256,128]{2,1,0:T(8,128)(2,1)S(1)} collective-permute-done((bf16[7,256,128]{2,1,0:T(8,128)(2,1)}, bf16[7,256,128]{2,1,0:T(8,128)(2,1)S(1)}, u32[]{:S(2)}, u32[]{:S(2)}) %collective-permute-start.22) | collective-permute-done | bytes 458784 | tf_op jit(solution)/shard_map/ppermute | solution.py:371
  59.3 5.3 %collective-permute-start.10 = (bf16[2,4,4,2,64,128]{5,4,3,2,1,0:T(8,128)(2,1)}, bf16[2,4,4,2,64,128]{5,4,3,2,1,0:T(8,128)(2,1)}, u32[]{:S(2)}, u32[]{:S(2)}) collective-permute-start(bf16[2,4,4,2,64,128]{5,4,3,2,1,0:T(8,128)(2,1)} %pack.7.own), channel_id=1, source_target_pairs={{0,4},{4,8},{8,12},{1,5},{5,9},{9,13},{2,6},{6,10},{10,14},{3,7},{... | collective-permute-start | bytes 3145736 | tf_op jit(solution)/shard_map/ppermute | solution.py:354
  64.6 2.8 %join.1.own_ref = bf16[7,256,128]{2,1,0:T(8,128)(2,1)} custom-call(f32[6,256,128]{2,1,0:T(8,128)} %get-tuple-element.27.sum_ref, f32[256,128]{1,0:T(8,128)} %get-tuple-element.28.log_ref, bf16[7,256,128]{2,1,0:T(8,128)(2,1)} %copy-done.3), custom_call_target="tpu_custom_call" | custom-call | bytes 1 | tf_op jit(solution)/shard_map/join/pallas_call | solution.py:288
  67.4 0.7 collective-permute-start.23
  68.1 0.1 collective-permute-start.13
  68.1 10.0 %video.5.rest_0_ = bf16[16,8,4,1536]{3,2,1,0:T(4,128)(2,1)} custom-call(s32[6]{0:T(128)} %stack.43.scal, s32[1,256]{1,0:T(1,128)} %bitcast.9, bf16[16,8,4,1536]{3,2,1,0:T(4,128)(2,1)} %q_ref.8, bf16[2,4,4,2,64,128]{5,4,3,2,1,0:T(8,128)(2,1)} %pack.5.own, bf16[2,4,4,2,64,128]{5,4,3,2,1,0:T(8,128)(2,1)} %collective-permute-done.left, ...), custom_call_target="tpu_custom_call", output_to_operand_aliasing={{}: (11, {})} | custom-call | bytes 1 | tf_op jit(solution)/shard_map/video/pallas_call | solution.py:165
  78.1 4.3 %collective-permute-done.12.right = bf16[2,4,4,2,64,128]{5,4,3,2,1,0:T(8,128)(2,1)} collective-permute-done((bf16[2,4,4,2,64,128]{5,4,3,2,1,0:T(8,128)(2,1)}, bf16[2,4,4,2,64,128]{5,4,3,2,1,0:T(8,128)(2,1)}, u32[]{:S(2)}, u32[]{:S(2)}) %collective-permute-start.12) | collective-permute-done | bytes 1048608 | tf_op jit(solution)/shard_map/ppermute | solution.py:354
  82.4 2.4 %collective-permute-done.10.left = bf16[2,4,4,2,64,128]{5,4,3,2,1,0:T(8,128)(2,1)} collective-permute-done((bf16[2,4,4,2,64,128]{5,4,3,2,1,0:T(8,128)(2,1)}, bf16[2,4,4,2,64,128]{5,4,3,2,1,0:T(8,128)(2,1)}, u32[]{:S(2)}, u32[]{:S(2)}) %collective-permute-start.10) | collective-permute-done | bytes 1048608 | tf_op jit(solution)/shard_map/ppermute | solution.py:354
  84.8 0.8 copy-done.4
  85.5 3.3 %finish.1 = bf16[256,768]{1,0:T(8,128)(2,1)} custom-call(s32[6]{0:T(128)} %stack.43.scal, bf16[7,256,128]{2,1,0:T(8,128)(2,1)} %join.1.own_ref, bf16[7,256,128]{2,1,0:T(8,128)(2,1)} %copy-done.4), custom_call_target="tpu_custom_call" | custom-call | bytes 1 | tf_op jit(solution)/shard_map/finish/pallas_call | solution.py:314
  88.8 1.3 collective-permute-start.24
  90.1 3.9 %pack.4.own = bf16[2,2,4,2,64,128]{5,4,3,2,1,0:T(8,128)(2,1)} custom-call(s32[6]{0:T(128)} %stack.43.scal, bf16[16,8,4,1536]{3,2,1,0:T(4,128)(2,1)} %k_ref.9, bf16[16,8,4,1536]{3,2,1,0:T(4,128)(2,1)} %v_ref.9), custom_call_target="tpu_custom_call" | custom-call | bytes 1 | tf_op jit(solution)/shard_map/pack/pallas_call | solution.py:71
  94.0 1.3 collective-permute-start.16
  95.3 15.9 %collective-permute-done.24 = bf16[256,768]{1,0:T(8,128)(2,1)S(1)} collective-permute-done((bf16[256,768]{1,0:T(8,128)(2,1)}, bf16[256,768]{1,0:T(8,128)(2,1)S(1)}, u32[]{:S(2)}, u32[]{:S(2)}) %collective-permute-start.24) | collective-permute-done | bytes 393248 | tf_op jit(solution)/shard_map/ppermute | solution.py:376
  111.2 0.7 copy-done.5
  112.0 2.3 %collective-permute-start.9 = (bf16[2,2,4,2,64,128]{5,4,3,2,1,0:T(8,128)(2,1)}, bf16[2,2,4,2,64,128]{5,4,3,2,1,0:T(8,128)(2,1)}, u32[]{:S(2)}, u32[]{:S(2)}) collective-permute-start(bf16[2,2,4,2,64,128]{5,4,3,2,1,0:T(8,128)(2,1)} %pack.4.own), channel_id=1, source_target_pairs={{0,4},{4,8},{8,12},{1,5},{5,9},{9,13},{2,6},{6,10},{10,14},{3,7},{... | collective-permute-start | bytes 1572872 | tf_op jit(solution)/shard_map/ppermute | solution.py:354
  114.3 1.0 broadcast_select_fusion
  115.3 0.1 collective-permute-start.25
  115.4 0.5 collective-permute-start.17
  115.9 10.0 %video.6.rest_0_ = bf16[16,8,4,1536]{3,2,1,0:T(4,128)(2,1)} custom-call(s32[6]{0:T(128)} %stack.43.scal, s32[1,256]{1,0:T(1,128)} %bitcast.10, bf16[16,8,4,1536]{3,2,1,0:T(4,128)(2,1)} %q_ref.8, bf16[2,4,4,2,64,128]{5,4,3,2,1,0:T(8,128)(2,1)} %pack.7.own, ...), custom_call_target="tpu_custom_call", output_to_operand_aliasing={{}: (11, {})} | custom-call | bytes 1 | tf_op jit(solution)/shard_map/video/pallas_call | solution.py:165
  125.9 0.1 collective-permute-start.19
  126.1 0.4 collective-permute-start.18
  126.5 1.1 broadcast_select_fusion.2
  127.6 0.9 pad_maximum_fusion
  128.5 0.5 collective-permute-done.18.edge_left
  129.0 0.3 copy-done.2
  129.3 6.3 %video.7 = bf16[16,8,4,1536]{3,2,1,0:T(4,128)(2,1)} custom-call(s32[6]{0:T(128)} %stack.43.scal, s32[1,256]{1,0:T(1,128)} %bitcast.11, bf16[16,8,4,1536]{3,2,1,0:T(4,128)(2,1)} %q_ref.8, bf16[2,2,4,2,64,128]{5,4,3,2,1,0:T(8,128)(2,1)} %pack.4.own, bf16[2,2,4,2,64,128]{5,4,3,2,1,0:T(8,128)(2,1)} %collective-permute-done.9.left, ...), custom_call_target="tpu_custom_call", output_to_operand_aliasing={{}: (11, {})} | custom-call | bytes 1 | tf_op jit(solution)/shard_map/video/pallas_call | solution.py:165
  (31 shorter events, 0.1 us)
Async XLA Ops:
  5.8 23.3 %collective-permute-start.20 = (bf16[16,8,4,768]{3,2,1,0:T(4,128)(2,1)}, bf16[16,8,4,768]{3,2,1,0:T(4,128)(2,1)S(1)}, u32[]{:S(2)}, u32[]{:S(2)}) collective-permute-start(bf16[16,8,4,768]{3,2,1,0:T(4,128)(2,1)} %get-tuple-element.25), channel_id=1, source_target_pairs={{0,2},{2,0},{1,3},{3,1},{4,6},{6,4},{5,7},{7,5},{8,10},{10,8},{9,1... | collective-permute-start | bytes 2359304 | tf_op jit(solution)/shard_map/ppermute | solution.py:343
  6.3 23.3 %collective-permute-start.21 = (bf16[16,8,4,768]{3,2,1,0:T(4,128)(2,1)}, bf16[16,8,4,768]{3,2,1,0:T(4,128)(2,1)}, u32[]{:S(2)}, u32[]{:S(2)}) collective-permute-start(bf16[16,8,4,768]{3,2,1,0:T(4,128)(2,1)} %get-tuple-element.26), channel_id=1, source_target_pairs={{0,2},{2,0},{1,3},{3,1},{4,6},{6,4},{5,7},{7,5},{8,10},{10,8},{9,1... | collective-permute-start | bytes 2359304 | tf_op jit(solution)/shard_map/ppermute | solution.py:343
  6.3 16.6 %collective-permute-start.1 = (bf16[2,2,4,2,64,128]{5,4,3,2,1,0:T(8,128)(2,1)}, bf16[2,2,4,2,64,128]{5,4,3,2,1,0:T(8,128)(2,1)}, u32[]{:S(2)}, u32[]{:S(2)}) collective-permute-start(bf16[2,2,4,2,64,128]{5,4,3,2,1,0:T(8,128)(2,1)} %get-tuple-element.16.own), channel_id=1, source_target_pairs={{0,4},{4,8},{8,12},{1,5},{5,9},{9,13},{2,6},{6,10},{10,14},{3,7},{... | collective-permute-start | bytes 1572872 | tf_op jit(solution)/shard_map/ppermute | solution.py:354
  12.1 17.0 %collective-permute-start.2 = (bf16[2,2,4,2,64,128]{5,4,3,2,1,0:T(8,128)(2,1)}, bf16[2,2,4,2,64,128]{5,4,3,2,1,0:T(8,128)(2,1)}, u32[]{:S(2)}, u32[]{:S(2)}) collective-permute-start(bf16[2,2,4,2,64,128]{5,4,3,2,1,0:T(8,128)(2,1)} %get-tuple-element.16.own), channel_id=1, source_target_pairs={{4,0},{8,4},{12,8},{5,1},{9,5},{13,9},{6,2},{10,6},{14,10},{7,3},{... | collective-permute-start | bytes 1572872 | tf_op jit(solution)/shard_map/ppermute | solution.py:354
  17.6 32.7 %collective-permute-start.7 = (bf16[2,4,4,2,64,128]{5,4,3,2,1,0:T(8,128)(2,1)}, bf16[2,4,4,2,64,128]{5,4,3,2,1,0:T(8,128)(2,1)}, u32[]{:S(2)}, u32[]{:S(2)}) collective-permute-start(bf16[2,4,4,2,64,128]{5,4,3,2,1,0:T(8,128)(2,1)} %pack.5.own), channel_id=1, source_target_pairs={{4,0},{8,4},{12,8},{5,1},{9,5},{13,9},{6,2},{10,6},{14,10},{7,3},{... | collective-permute-start | bytes 3145736 | tf_op jit(solution)/shard_map/ppermute | solution.py:354
  23.0 31.6 %collective-permute-start = (bf16[2,4,4,2,64,128]{5,4,3,2,1,0:T(8,128)(2,1)}, bf16[2,4,4,2,64,128]{5,4,3,2,1,0:T(8,128)(2,1)}, u32[]{:S(2)}, u32[]{:S(2)}) collective-permute-start(bf16[2,4,4,2,64,128]{5,4,3,2,1,0:T(8,128)(2,1)} %pack.5.own), channel_id=1, source_target_pairs={{0,4},{4,8},{8,12},{1,5},{5,9},{9,13},{2,6},{6,10},{10,14},{3,7},{... | collective-permute-start | bytes 3145736 | tf_op jit(solution)/shard_map/ppermute | solution.py:354
  29.1 10.4 %collective-permute-start.3 = (bf16[2,2,4,2,64,128]{5,4,3,2,1,0:T(8,128)(2,1)}, bf16[2,2,4,2,64,128]{5,4,3,2,1,0:T(8,128)(2,1)}, u32[]{:S(2)}, u32[]{:S(2)}) collective-permute-start(bf16[2,2,4,2,64,128]{5,4,3,2,1,0:T(8,128)(2,1)} %get-tuple-element.16.own), channel_id=1, source_target_pairs={{0,2},{2,0},{1,3},{3,1},{4,6},{6,4},{5,7},{7,5},{8,10},{10,8},{9,1... | collective-permute-start | bytes 1572872 | tf_op jit(solution)/shard_map/ppermute | solution.py:343
  29.1 0.9 copy-start.1
  29.1 13.1 %collective-permute-start.4 = (bf16[2,2,4,2,64,128]{5,4,3,2,1,0:T(8,128)(2,1)}, bf16[2,2,4,2,64,128]{5,4,3,2,1,0:T(8,128)(2,1)}, u32[]{:S(2)}, u32[]{:S(2)}) collective-permute-start(bf16[2,2,4,2,64,128]{5,4,3,2,1,0:T(8,128)(2,1)} %collective-permute-done.1.left), channel_id=1, source_target_pairs={{0,2},{2,0},{1,3},{3,1},{4,6},{6,4},{5,7},{7,5},{8,10},{10,8},{9,1... | collective-permute-start | bytes 1572872 | tf_op jit(solution)/shard_map/ppermute | solution.py:343
  29.6 12.9 %collective-permute-start.5 = (bf16[2,2,4,2,64,128]{5,4,3,2,1,0:T(8,128)(2,1)}, bf16[2,2,4,2,64,128]{5,4,3,2,1,0:T(8,128)(2,1)}, u32[]{:S(2)}, u32[]{:S(2)}) collective-permute-start(bf16[2,2,4,2,64,128]{5,4,3,2,1,0:T(8,128)(2,1)} %collective-permute-done.2.right), channel_id=1, source_target_pairs={{0,2},{2,0},{1,3},{3,1},{4,6},{6,4},{5,7},{7,5},{8,10},{10,8},{9,1... | collective-permute-start | bytes 1572872 | tf_op jit(solution)/shard_map/ppermute | solution.py:343
  39.5 19.8 %collective-permute-start.22 = (bf16[7,256,128]{2,1,0:T(8,128)(2,1)}, bf16[7,256,128]{2,1,0:T(8,128)(2,1)S(1)}, u32[]{:S(2)}, u32[]{:S(2)}) collective-permute-start(bf16[7,256,128]{2,1,0:T(8,128)(2,1)} %get-tuple-element.29), channel_id=1, source_target_pairs={{0,4},{12,8},{1,5},{13,9},{2,6},{14,10},{3,7},{15,11},{16,20},{28,... | collective-permute-start | bytes 1376264 | tf_op jit(solution)/shard_map/ppermute | solution.py:371
  42.2 25.2 %collective-permute-start.11 = (bf16[2,4,4,2,64,128]{5,4,3,2,1,0:T(8,128)(2,1)}, bf16[2,4,4,2,64,128]{5,4,3,2,1,0:T(8,128)(2,1)}, u32[]{:S(2)}, u32[]{:S(2)}) collective-permute-start(bf16[2,4,4,2,64,128]{5,4,3,2,1,0:T(8,128)(2,1)} %pack.5.own), channel_id=1, source_target_pairs={{0,2},{2,0},{1,3},{3,1},{4,6},{6,4},{5,7},{7,5},{8,10},{10,8},{9,1... | collective-permute-start | bytes 3145736 | tf_op jit(solution)/shard_map/ppermute | solution.py:343
  50.4 17.7 %collective-permute-start.8 = (bf16[2,4,4,2,64,128]{5,4,3,2,1,0:T(8,128)(2,1)}, bf16[2,4,4,2,64,128]{5,4,3,2,1,0:T(8,128)(2,1)}, u32[]{:S(2)}, u32[]{:S(2)}) collective-permute-start(bf16[2,4,4,2,64,128]{5,4,3,2,1,0:T(8,128)(2,1)} %collective-permute-done.7.right), channel_id=1, source_target_pairs={{0,2},{2,0},{1,3},{3,1},{4,6},{6,4},{5,7},{7,5},{8,10},{10,8},{9,1... | collective-permute-start | bytes 3145736 | tf_op jit(solution)/shard_map/ppermute | solution.py:343
  54.6 13.5 %collective-permute-start.6 = (bf16[2,4,4,2,64,128]{5,4,3,2,1,0:T(8,128)(2,1)}, bf16[2,4,4,2,64,128]{5,4,3,2,1,0:T(8,128)(2,1)}, u32[]{:S(2)}, u32[]{:S(2)}) collective-permute-start(bf16[2,4,4,2,64,128]{5,4,3,2,1,0:T(8,128)(2,1)} %collective-permute-done.left), channel_id=1, source_target_pairs={{0,2},{2,0},{1,3},{3,1},{4,6},{6,4},{5,7},{7,5},{8,10},{10,8},{9,1... | collective-permute-start | bytes 3145736 | tf_op jit(solution)/shard_map/ppermute | solution.py:343
  55.1 27.3 %collective-permute-start.12 = (bf16[2,4,4,2,64,128]{5,4,3,2,1,0:T(8,128)(2,1)}, bf16[2,4,4,2,64,128]{5,4,3,2,1,0:T(8,128)(2,1)}, u32[]{:S(2)}, u32[]{:S(2)}) collective-permute-start(bf16[2,4,4,2,64,128]{5,4,3,2,1,0:T(8,128)(2,1)} %pack.7.own), channel_id=1, source_target_pairs={{4,0},{8,4},{12,8},{5,1},{9,5},{13,9},{6,2},{10,6},{14,10},{7,3},{... | collective-permute-start | bytes 3145736 | tf_op jit(solution)/shard_map/ppermute | solution.py:354
  59.3 5.3 %copy-start.3 = (bf16[7,256,128]{2,1,0:T(8,128)(2,1)}, bf16[7,256,128]{2,1,0:T(8,128)(2,1)S(1)}, u32[]{:S(2)}) copy-start(bf16[7,256,128]{2,1,0:T(8,128)(2,1)S(1)} %collective-permute-done.22.got_ref) | copy-start | bytes 1376260
  59.3 25.5 %collective-permute-start.10 = (bf16[2,4,4,2,64,128]{5,4,3,2,1,0:T(8,128)(2,1)}, bf16[2,4,4,2,64,128]{5,4,3,2,1,0:T(8,128)(2,1)}, u32[]{:S(2)}, u32[]{:S(2)}) collective-permute-start(bf16[2,4,4,2,64,128]{5,4,3,2,1,0:T(8,128)(2,1)} %pack.7.own), channel_id=1, source_target_pairs={{0,4},{4,8},{8,12},{1,5},{5,9},{9,13},{2,6},{6,10},{10,14},{3,7},{... | collective-permute-start | bytes 3145736 | tf_op jit(solution)/shard_map/ppermute | solution.py:354
  67.4 17.4 %collective-permute-start.23 = (bf16[7,256,128]{2,1,0:T(8,128)(2,1)}, bf16[7,256,128]{2,1,0:T(8,128)(2,1)S(1)}, u32[]{:S(2)}, u32[]{:S(2)}) collective-permute-start(bf16[7,256,128]{2,1,0:T(8,128)(2,1)} %join.1.own_ref), channel_id=1, source_target_pairs={{4,8},{8,4},{5,9},{9,5},{6,10},{10,6},{7,11},{11,7},{20,24},{24,20... | collective-permute-start | bytes 1376264 | tf_op jit(solution)/shard_map/ppermute | solution.py:373
  68.1 47.3 %collective-permute-start.13 = (bf16[2,4,4,2,64,128]{5,4,3,2,1,0:T(8,128)(2,1)}, bf16[2,4,4,2,64,128]{5,4,3,2,1,0:T(8,128)(2,1)}, u32[]{:S(2)}, u32[]{:S(2)}) collective-permute-start(bf16[2,4,4,2,64,128]{5,4,3,2,1,0:T(8,128)(2,1)} %pack.7.own), channel_id=1, source_target_pairs={{0,2},{2,0},{1,3},{3,1},{4,6},{6,4},{5,7},{7,5},{8,10},{10,8},{9,1... | collective-permute-start | bytes 3145736 | tf_op jit(solution)/shard_map/ppermute | solution.py:343
  82.4 33.0 %collective-permute-start.15 = (bf16[2,4,4,2,64,128]{5,4,3,2,1,0:T(8,128)(2,1)}, bf16[2,4,4,2,64,128]{5,4,3,2,1,0:T(8,128)(2,1)}, u32[]{:S(2)}, u32[]{:S(2)}) collective-permute-start(bf16[2,4,4,2,64,128]{5,4,3,2,1,0:T(8,128)(2,1)} %collective-permute-done.12.right), channel_id=1, source_target_pairs={{0,2},{2,0},{1,3},{3,1},{4,6},{6,4},{5,7},{7,5},{8,10},{10,8},{9,1... | collective-permute-start | bytes 3145736 | tf_op jit(solution)/shard_map/ppermute | solution.py:343
  84.8 31.2 %collective-permute-start.14 = (bf16[2,4,4,2,64,128]{5,4,3,2,1,0:T(8,128)(2,1)}, bf16[2,4,4,2,64,128]{5,4,3,2,1,0:T(8,128)(2,1)}, u32[]{:S(2)}, u32[]{:S(2)}) collective-permute-start(bf16[2,4,4,2,64,128]{5,4,3,2,1,0:T(8,128)(2,1)} %collective-permute-done.10.left), channel_id=1, source_target_pairs={{0,2},{2,0},{1,3},{3,1},{4,6},{6,4},{5,7},{7,5},{8,10},{10,8},{9,1... | collective-permute-start | bytes 3145736 | tf_op jit(solution)/shard_map/ppermute | solution.py:343
  84.8 0.8 copy-start.4
  88.8 22.4 %collective-permute-start.24 = (bf16[256,768]{1,0:T(8,128)(2,1)}, bf16[256,768]{1,0:T(8,128)(2,1)S(1)}, u32[]{:S(2)}, u32[]{:S(2)}) collective-permute-start(bf16[256,768]{1,0:T(8,128)(2,1)} %finish.1), channel_id=1, source_target_pairs={{4,0},{8,12},{5,1},{9,13},{6,2},{10,14},{7,3},{11,15},{20,16},{24,... | collective-permute-start | bytes 1179656 | tf_op jit(solution)/shard_map/ppermute | solution.py:376
  90.1 24.2 %copy-start = (bf16[256,768]{1,0:T(8,128)(2,1)S(1)}, bf16[256,768]{1,0:T(8,128)(2,1)}, u32[]{:S(2)}) copy-start(bf16[256,768]{1,0:T(8,128)(2,1)} %finish.1) | copy-start | bytes 1179652
  94.0 31.9 %collective-permute-start.16 = (bf16[2,2,4,2,64,128]{5,4,3,2,1,0:T(8,128)(2,1)}, bf16[2,2,4,2,64,128]{5,4,3,2,1,0:T(8,128)(2,1)}, u32[]{:S(2)}, u32[]{:S(2)}) collective-permute-start(bf16[2,2,4,2,64,128]{5,4,3,2,1,0:T(8,128)(2,1)} %pack.4.own), channel_id=1, source_target_pairs={{4,0},{8,4},{12,8},{5,1},{9,5},{13,9},{6,2},{10,6},{14,10},{7,3},{... | collective-permute-start | bytes 1572872 | tf_op jit(solution)/shard_map/ppermute | solution.py:354
  111.2 0.7 copy-start.5
  112.0 14.1 %collective-permute-start.9 = (bf16[2,2,4,2,64,128]{5,4,3,2,1,0:T(8,128)(2,1)}, bf16[2,2,4,2,64,128]{5,4,3,2,1,0:T(8,128)(2,1)}, u32[]{:S(2)}, u32[]{:S(2)}) collective-permute-start(bf16[2,2,4,2,64,128]{5,4,3,2,1,0:T(8,128)(2,1)} %pack.4.own), channel_id=1, source_target_pairs={{0,4},{4,8},{8,12},{1,5},{5,9},{9,13},{2,6},{6,10},{10,14},{3,7},{... | collective-permute-start | bytes 1572872 | tf_op jit(solution)/shard_map/ppermute | solution.py:354
  115.3 11.2 %collective-permute-start.25 = (bf16[256,768]{1,0:T(8,128)(2,1)S(1)}, bf16[256,768]{1,0:T(8,128)(2,1)}, u32[]{:S(2)}, u32[]{:S(2)}) collective-permute-start(bf16[256,768]{1,0:T(8,128)(2,1)S(1)} %broadcast_select_fusion), channel_id=1, source_target_pairs={{0,2},{2,0},{1,3},{3,1},{4,6},{6,4},{5,7},{7,5},{8,10},{10,8},{9,1... | collective-permute-start | bytes 1179656 | tf_op jit(solution)/shard_map/ppermute | solution.py:343
  115.4 13.1 %collective-permute-start.17 = (bf16[2,2,4,2,64,128]{5,4,3,2,1,0:T(8,128)(2,1)}, bf16[2,2,4,2,64,128]{5,4,3,2,1,0:T(8,128)(2,1)S(1)}, u32[]{:S(2)}, u32[]{:S(2)}) collective-permute-start(bf16[2,2,4,2,64,128]{5,4,3,2,1,0:T(8,128)(2,1)} %pack.4.own), channel_id=1, source_target_pairs={{0,2},{2,0},{1,3},{3,1},{4,6},{6,4},{5,7},{7,5},{8,10},{10,8},{9,1... | collective-permute-start | bytes 1572872 | tf_op jit(solution)/shard_map/ppermute | solution.py:343
  125.9 2.6 %collective-permute-start.19 = (bf16[2,2,4,2,64,128]{5,4,3,2,1,0:T(8,128)(2,1)}, bf16[2,2,4,2,64,128]{5,4,3,2,1,0:T(8,128)(2,1)}, u32[]{:S(2)}, u32[]{:S(2)}) collective-permute-start(bf16[2,2,4,2,64,128]{5,4,3,2,1,0:T(8,128)(2,1)} %collective-permute-done.16.right), channel_id=1, source_target_pairs={{0,2},{2,0},{1,3},{3,1},{4,6},{6,4},{5,7},{7,5},{8,10},{10,8},{9,1... | collective-permute-start | bytes 1572872 | tf_op jit(solution)/shard_map/ppermute | solution.py:343
  126.1 2.9 %collective-permute-start.18 = (bf16[2,2,4,2,64,128]{5,4,3,2,1,0:T(8,128)(2,1)}, bf16[2,2,4,2,64,128]{5,4,3,2,1,0:T(8,128)(2,1)}, u32[]{:S(2)}, u32[]{:S(2)}) collective-permute-start(bf16[2,2,4,2,64,128]{5,4,3,2,1,0:T(8,128)(2,1)} %collective-permute-done.9.left), channel_id=1, source_target_pairs={{0,2},{2,0},{1,3},{3,1},{4,6},{6,4},{5,7},{7,5},{8,10},{10,8},{9,1... | collective-permute-start | bytes 1572872 | tf_op jit(solution)/shard_map/ppermute | solution.py:343
  128.5 0.8 copy-start.2

commit v2 on v1

v2 whole, which is shorter than its diff:
```python
import functools
import math

import jax
import jax.numpy as jnp
from jax import lax
from jax.experimental import pallas as pl
from jax.experimental.pallas import tpu as pltpu
from jax.sharding import PartitionSpec as P

HD = 128
TILE = 4
VOL = TILE**3
BF16 = jnp.bfloat16
F32 = jnp.float32
SCALE = 1.0 / math.sqrt(HD)
SCALE_2 = SCALE * math.log2(math.e)
VMEM = 63 << 20
THIRD = 32
SIZES = (3, 3)


def cost(microseconds):
    return pl.CostEstimate(flops=int(microseconds * 1.15e9), bytes_accessed=1, transcendentals=0)


def head_groups(heads):
    sizes = SIZES if heads == sum(SIZES) else [heads - 1, 1]
    starts = [sum(sizes[:i]) for i in range(len(sizes))]
    return list(zip(starts, sizes))


def dot_nt(a, b):
    return lax.dot_general(a, b, (((1,), (1,)), ((), ())), preferred_element_type=F32)


def dot_nn(a, b):
    return lax.dot_general(a, b, (((1,), (0,)), ((), ())), preferred_element_type=F32)


def weigh(p, v):
    return dot_nn(p.astype(BF16), jnp.concatenate([v, jnp.ones_like(v)], axis=1))


def pack_body(sizes, scal, *rest):
    k_ref, v_ref = rest[:2]
    tiles = rest[-len(sizes) - 1 : -1] if len(rest) == len(sizes) + 4 else rest[-len(sizes) :]
    head = 0
    for size, kv_ref in zip(sizes, tiles):
        for at in range(size):
            lanes = slice(head * HD, (head + 1) * HD)
            head += 1
            for which, ref in enumerate((k_ref, v_ref)):
                for r in range(ref.shape[1] // TILE):
                    kv_ref[which, at, 0, r] = ref[:, r * TILE : (r + 1) * TILE, :, lanes].reshape(VOL, HD)
    if len(rest) == len(sizes) + 4:
        rest[-1][...] = rest[2][...]


def pack_half(scal, key_video, value_video, sizes, query_video=None):
    frames, rows, cols, features = key_video.shape
    time_tiles = frames // TILE
    row_tiles = rows // TILE
    theirs = query_video is not None
    block = pl.BlockSpec(
        (TILE, rows, cols, features // 2), lambda t, s: (t, 0, 0, 1 - s[4] if theirs else s[4])
    )
    operands = [key_video, value_video]
    out_specs = [
        pl.BlockSpec((2, size, 1, row_tiles, VOL, HD), lambda t, s: (0, 0, t, 0, 0, 0)) for size in sizes
    ]
    out_shape = [jax.ShapeDtypeStruct((2, size, time_tiles, row_tiles, VOL, HD), BF16) for size in sizes]
    if theirs:
        operands.append(query_video)
        out_specs.append(pl.BlockSpec((TILE, rows, cols, features // 2), lambda t, s: (t, 0, 0, 0)))
        out_shape.append(jax.ShapeDtypeStruct((frames, rows, cols, features // 2), BF16))
    return pl.pallas_call(
        functools.partial(pack_body, sizes),
        grid_spec=pltpu.PrefetchScalarGridSpec(
            num_scalar_prefetch=1, grid=(time_tiles,), in_specs=[block] * len(operands), out_specs=out_specs
        ),
        out_shape=out_shape,
        compiler_params=pltpu.CompilerParams(vmem_limit_bytes=VMEM),
        cost_estimate=cost(0),
        name="pack",
    )(scal, *operands)


def video_body(scal, valid_ref, own_q, pair_q, *rest):
    own_tiles, pair_tiles, (tk_ref, tv_ref) = rest[:3], rest[3:6], rest[6:8]
    own_out, pair_out = rest[-2:]
    has_left = scal[1] > 0
    has_right = scal[2] > 0
    time_tiles = own_q.shape[0] // TILE
    open_keys = valid_ref[...] > 0

    def load(ref, which, first, last, row):
        picked = ref[which, 0, first:last] if row is None else ref[which, 0, first:last, pl.ds(row, 1)]
        return picked.reshape(picked.shape[0] * picked.shape[1] * VOL, HD)

    def scores(step):
        part, t = step
        q_ref = (own_q, pair_q)[part]
        near = scal[0] if part == 0 else 1 - scal[0]
        far_rows = pl.ds((1 - near) * TILE, TILE)
        near_rows = pl.ds(near * TILE, TILE)
        own, left, right = (own_tiles, pair_tiles)[part]
        edge, edge_left, edge_right = (pair_tiles, own_tiles)[part]
        row = 1 - near
        first = max(t - 1, 0)
        last = min(t + 1, time_tiles - 1) + 1
        frames = slice(t * TILE, (t + 1) * TILE)
        q_far = q_ref[frames, far_rows, :, :].reshape(VOL, HD)
        q_near = q_ref[frames, near_rows, :, :].reshape(VOL, HD)
        q_all = jnp.concatenate([q_far, q_near], axis=0)
        s_text = jnp.where(open_keys, dot_nt(q_all, tk_ref[...]), -jnp.inf)
        wide = [(s_text, None, None)]
        for ref, ok in ((own, None), (left, has_left), (right, has_right)):
            wide.append((dot_nt(q_all, load(ref, 0, first, last, None)), ref, ok))
        thin = []
        for ref, ok in ((edge, None), (edge_left, has_left), (edge_right, has_right)):
            thin.append((dot_nt(q_near, load(ref, 0, first, last, row)), ref, ok))
        return first, last, wide, thin, row, far_rows, near_rows

    def peak(entries):
        tops = []
        for s, _, ok in entries:
            top = jnp.max(s, axis=1, keepdims=True)
            tops.append(top if ok is None else jnp.where(ok, top, -jnp.inf))
        return functools.reduce(jnp.maximum, tops)

    def gather(entries, m, first, last, row):
        summed = None
        for s, ref, ok in entries:
            base = m if ok is None else jnp.where(ok, m, jnp.inf)
            v = tv_ref[...] if ref is None else load(ref, 1, first, last, row)
            part = weigh(jnp.exp2((s - base) * SCALE_2), v)
            summed = part if summed is None else summed + part
        return summed

    def finish(step, state):
        part, t = step
        out_ref = (own_out, pair_out)[part]
        first, last, wide, thin, row, far_rows, near_rows = state
        frames = slice(t * TILE, (t + 1) * TILE)
        m_all = peak(wide)
        m_near = jnp.maximum(m_all[VOL:], peak(thin))
        m_all = jnp.concatenate([m_all[:VOL], m_near], axis=0)
        summed = gather(wide, m_all, first, last, None)
        far = summed[:VOL]
        close = summed[VOL:] + gather(thin, m_near, first, last, row)
        for rows, value in ((far_rows, far), (near_rows, close)):
            out = value[:, :HD] / value[:, HD:]
            out_ref[frames, rows, :, :] = out.astype(BF16).reshape(TILE, TILE, TILE, HD)

    steps = [(part, t) for part in range(2) for t in range(time_tiles)]
    state = scores(steps[0])
    for at, step in enumerate(steps):
        following = scores(steps[at + 1]) if at + 1 < len(steps) else None
        finish(step, state)
        state = following


def video_group(scal, valid, query_video, pair_query, mine, pair, key_text, value_text, prior, start, count):
    frames, rows, cols, _ = query_video.shape
    half_heads = pair_query.shape[3] // HD
    time_tiles = frames // TILE
    text = key_text.shape[0]
    block = (frames, rows, cols, HD)
    own_head = pl.BlockSpec(block, lambda i, s: (0, 0, 0, s[4] * half_heads + start + i))
    pair_head = pl.BlockSpec(block, lambda i, s: (0, 0, 0, start + i))
    given = pl.BlockSpec(block, lambda i, s: (0, 0, 0, i))
    of_half = pl.BlockSpec((2, 1, time_tiles, 2, VOL, HD), lambda i, s: (0, start + i, 0, 0, 0, 0))
    of_group = pl.BlockSpec((2, 1, time_tiles, 2, VOL, HD), lambda i, s: (0, i, 0, 0, 0, 0))
    word = pl.BlockSpec((text, HD), lambda i, s: (0, s[4] * half_heads + start + i))
    specs = [pl.BlockSpec((1, text), lambda i, s: (0, 0)), own_head, pair_head]
    specs += [of_half] * 3 + [of_group] * 3 + [word, word]
    operands = [scal, valid, query_video, pair_query, *mine, *pair, key_text, value_text]
    aliases = {}
    if prior is not None:
        specs.append(pl.BlockSpec(memory_space=pl.ANY))
        aliases = {len(operands): 0}
        operands.append(prior)
    return pl.pallas_call(
        video_body,
        grid_spec=pltpu.PrefetchScalarGridSpec(
            num_scalar_prefetch=1,
            grid=(count,),
            in_specs=specs,
            out_specs=[own_head, given],
        ),
        out_shape=[
            jax.ShapeDtypeStruct(query_video.shape, BF16),
            jax.ShapeDtypeStruct((frames, rows, cols, count * HD), BF16),
        ],
        input_output_aliases=aliases,
        compiler_params=pltpu.CompilerParams(vmem_limit_bytes=VMEM),
        cost_estimate=cost(0),
        name="video",
    )(*operands)


def lane_of(shape):
    return lax.broadcasted_iota(jnp.int32, shape, len(shape) - 1)


def send_logs(logs):
    high = logs.astype(BF16).astype(F32)
    mid = (logs - high).astype(BF16).astype(F32)
    low = logs - high - mid
    lane = lane_of(logs.shape)
    whole = jnp.where(lane < THIRD, high, 0.0)
    whole = jnp.where((lane >= THIRD) & (lane < 2 * THIRD), pltpu.roll(mid, THIRD, 1), whole)
    whole = jnp.where((lane >= 2 * THIRD) & (lane < 3 * THIRD), pltpu.roll(low, 2 * THIRD, 1), whole)
    return jnp.where(lane == HD - 1, 1.0, whole).astype(BF16)


def read_logs(sent):
    whole = sent.astype(F32)
    logs = whole + pltpu.roll(whole, HD - THIRD, 1) + pltpu.roll(whole, HD - 2 * THIRD, 1)
    return jnp.where(whole[:, HD - 1 :] > 0, logs, -jnp.inf)


def text_body(groups, scal, valid_ref, q_ref, mine_ref, tk_ref, tv_ref, *rest):
    pairs = rest[: len(groups)]
    sum_ref, log_ref, send_ref = rest[len(groups) :]
    at = pl.program_id(0)
    heads = pl.num_programs(0) - 1

    def work(pair_ref):
        q = q_ref[...]

        def tokens(ref, which):
            whole = ref[which, 0]
            return whole.reshape(whole.shape[0] * whole.shape[1] * VOL, HD)

        def scores(rows):
            near = jnp.where((valid_ref[...] > 0) & (scal[3] > 0), dot_nt(q[rows], tk_ref[...]), -jnp.inf)
            return [dot_nt(q[rows], tokens(mine_ref, 0)), dot_nt(q[rows], tokens(pair_ref, 0)), near]

        def reduce(rows, parts):
            m = functools.reduce(jnp.maximum, [jnp.max(s, axis=1, keepdims=True) for s in parts])
            values = (tokens(mine_ref, 1), tokens(pair_ref, 1), tv_ref[...])
            both = functools.reduce(
                jnp.add, [weigh(jnp.exp2((s - m) * SCALE_2), v) for s, v in zip(parts, values)]
            )
            total = both[:, HD:]
            out = both[:, :HD] / total
            sum_ref[0, rows] = out
            send_ref[0, rows] = out.astype(BF16)
            logs = m * SCALE + jnp.log(total)
            prior = jnp.where(at == 0, 0.0, log_ref[rows])
            log_ref[rows] = jnp.where(lane_of(logs.shape) == at, logs, prior)

        size = q.shape[0] // 2
        low, high = slice(0, size), slice(size, 2 * size)
        first = scores(low)
        second = scores(high)
        reduce(low, first)
        reduce(high, second)

    for (start, count), pair_ref in zip(groups, pairs):
        pl.when((at >= start) & (at < start + count))(functools.partial(work, pair_ref))

    @pl.when(at == heads)
    def _():
        send_ref[0] = send_logs(log_ref[...])


def text_partial(scal, valid, query_text, mine, pairs, groups, key_text, value_text):
    _, heads, time_tiles, _, _, _ = mine.shape
    text = query_text.shape[0]
    block = (2, 1, time_tiles, 2, VOL, HD)

    def of_group(start, count):
        return pl.BlockSpec(block, lambda i, s: (0, jnp.clip(i - start, 0, count - 1), 0, 0, 0, 0))

    word = pl.BlockSpec((text, HD), lambda i, s: (0, s[4] * heads + jnp.minimum(i, heads - 1)))
    return pl.pallas_call(
        functools.partial(text_body, groups),
        grid_spec=pltpu.PrefetchScalarGridSpec(
            num_scalar_prefetch=1,
            grid=(heads + 1,),
            in_specs=[pl.BlockSpec((1, text), lambda i, s: (0, 0)), word, of_group(0, heads), word, word]
            + [of_group(start, count) for start, count in groups],
            out_specs=[
                pl.BlockSpec((1, text, HD), lambda i, s: (jnp.minimum(i, heads - 1), 0, 0)),
                pl.BlockSpec((text, HD), lambda i, s: (0, 0)),
                pl.BlockSpec((1, text, HD), lambda i, s: (i, 0, 0)),
            ],
        ),
        out_shape=[
            jax.ShapeDtypeStruct((heads, text, HD), F32),
            jax.ShapeDtypeStruct((text, HD), F32),
            jax.ShapeDtypeStruct((heads + 1, text, HD), BF16),
        ],
        compiler_params=pltpu.CompilerParams(vmem_limit_bytes=VMEM),
        cost_estimate=cost(0),
        name="text",
    )(scal, valid, query_text, mine, key_text, value_text, *pairs)


def combine(parts, heads):
    logs = [part[1] for part in parts]
    top = functools.reduce(jnp.maximum, logs)
    weights = [jnp.exp(log - top) for log in logs]
    total = functools.reduce(jnp.add, weights)
    weights = [weight / total for weight in weights]
    outs = []
    for head in range(heads):
        terms = [weight[:, head : head + 1] * part[0](head) for weight, part in zip(weights, parts)]
        outs.append(functools.reduce(jnp.add, terms))
    return outs, top + jnp.log(total)


def join_body(sum_ref, log_ref, got_ref, out_ref):
    heads = sum_ref.shape[0]
    own = (lambda head: sum_ref[head], log_ref[...])
    got = (lambda head: got_ref[head].astype(F32), read_logs(got_ref[heads]))
    outs, logs = combine([own, got], heads)
    for head in range(heads):
        out_ref[head] = outs[head].astype(BF16)
    out_ref[heads] = send_logs(logs)


def join(sums, logs, got):
    return pl.pallas_call(
        join_body,
        out_shape=jax.ShapeDtypeStruct(got.shape, BF16),
        compiler_params=pltpu.CompilerParams(vmem_limit_bytes=VMEM),
        cost_estimate=cost(0),
        name="join",
    )(sums, logs, got)


def finish_body(scal, own_ref, got_ref, out_ref):
    heads = own_ref.shape[0] - 1
    low = scal[5] > 0
    parts = []
    for flag in (low, jnp.logical_not(low)):

        def pick(index, flag=flag):
            return jnp.where(flag, own_ref[index].astype(F32), got_ref[index].astype(F32))

        parts.append((pick, read_logs(pick(heads))))
    outs, _ = combine(parts, heads)
    for head in range(heads):
        out_ref[:, head * HD : (head + 1) * HD] = outs[head].astype(BF16)


def finish(scal, own, got):
    heads, text, _ = own.shape
    return pl.pallas_call(
        finish_body,
        grid_spec=pltpu.PrefetchScalarGridSpec(
            num_scalar_prefetch=1,
            grid=(1,),
            in_specs=[pl.BlockSpec(own.shape, lambda i, s: (0, 0, 0))] * 2,
            out_specs=pl.BlockSpec((text, (heads - 1) * HD), lambda i, s: (0, 0)),
        ),
        out_shape=jax.ShapeDtypeStruct((text, (heads - 1) * HD), BF16),
        compiler_params=pltpu.CompilerParams(vmem_limit_bytes=VMEM),
        cost_estimate=cost(0),
        name="finish",
    )(scal, own, got)


def after(value, *others):
    return lax.optimization_barrier((value, *others))[0]


def shards(query_video, key_video, value_video, query_text, key_text, value_text, text_valid):
    features = query_video.shape[3]
    heads = features // HD
    strips = lax.axis_size("tm")
    strip = lax.axis_index("tm")
    half = lax.axis_index("height")
    half_heads = heads // 2

    def swap(array):
        return lax.ppermute(array, "height", [(0, 1), (1, 0)])

    up = [(i, i + 1) for i in range(strips - 1)]
    down = [(i + 1, i) for i in range(strips - 1)]
    scal = jnp.stack(
        [1 - half, strip > 0, strip < strips - 1, strip == 0, half, strip < strips // 2]
    ).astype(jnp.int32)
    valid = text_valid.reshape(1, -1)
    groups = head_groups(half_heads)

    def to_neighbours(array):
        return lax.ppermute(array, "tm", up), lax.ppermute(array, "tm", down)

    (mine,) = pack_half(scal, key_video, value_video, (half_heads,))
    mine_sides = to_neighbours(mine)
    theirs = pack_half(after(scal, mine), key_video, value_video, [count for _, count in groups], query_video)
    pairs = [swap(array) for array in theirs[:-1]]
    pair_query = swap(theirs[-1])
    sums, logs, sent = text_partial(after(scal, pair_query), valid, query_text, mine, pairs, groups, key_text, value_text)

    middle = strips // 2
    for step in range(1, middle):
        got = lax.ppermute(sent, "tm", [(step - 1, step), (strips - step, strips - step - 1)])
        sent = join(sums, after(logs, *mine_sides), got)
    got = lax.ppermute(sent, "tm", [(middle - 1, middle), (middle, middle - 1)])

    def place(whole, part, start):
        column = ((1 - half) * half_heads + start) * HD
        return lax.dynamic_update_slice_in_dim(whole, part, column, 3)

    out_video = None
    waiting = []
    for index, (start, count) in enumerate(groups):
        pair = (pairs[index], *to_neighbours(pairs[index]))
        out_video, given = video_group(
            scal, valid, query_video, pair_query, (mine, *mine_sides), pair, key_text, value_text, out_video, start, count
        )
        if index == 0:
            opened = after(scal, out_video)
        for part in waiting:
            out_video = place(out_video, *part)
        waiting = [(swap(given), start)]
    for part in waiting:
        out_video = place(out_video, *part)

    done = finish(opened, sent, got)
    for step in range(middle - 1, 0, -1):
        got = lax.ppermute(done, "tm", [(step, step - 1), (strips - step - 1, strips - step)])
        done = jnp.where((strip == step - 1) | (strip == strips - step), got, done)
    other = swap(done)
    first = half == 0
    out_text = jnp.concatenate([jnp.where(first, done, other), jnp.where(first, other, done)], axis=1)
    return (out_video, out_text)


def solution(mesh):
    if mesh.shape["height"] != 2 or mesh.shape["tm"] % 2:
        raise ValueError("unsupported mesh")
    placed = (
        P("grp", "height", "tm", "head"),
        P("grp", "height", "tm", "head"),
        P("grp", "height", "tm", "head"),
        P("grp", "head"),
        P("grp", "head"),
        P("grp", "head"),
        P("grp"),
    )
    return jax.shard_map(
        shards,
        mesh=mesh,
        in_specs=placed,
        out_specs=(P("grp", "height", "tm", "head"), P("grp", "head")),
        check_vma=False,
    )
```

time: 137 us -> 112 us (0.82)
  the two profiles are of different devices: /device:TPU:0 before, /device:TPU:21 now
where the time goes in v2:
time: 112 us; the launch traced here: 111 us
  Pallas kernels  49.7 us (44%)
  waiting for transfers between devices  28.8 us (26%)
  starting transfers between devices  28.7 us (26%)
  local copies, waits for them, and re-layouts  2.44 us (2%)
    pallas_call x2, Pallas kernels, video_group(): pl.pallas_call(video_body, grid_spec=pltpu.PrefetchScalarGridSpec(num_sca...  25.7 us
    ppermute x6, starting transfers between devices, to_neighbours(): return (lax.ppermute(array, 'tm', up), lax.ppermute(array, 'tm', down))  17.6 us
    ppermute x6, waiting for transfers between devices, to_neighbours(): return (lax.ppermute(array, 'tm', up), lax.ppermute(array, 'tm', down))  14.5 us
    ppermute x1, waiting for transfers between devices, shards(): lax.ppermute(sent, 'tm', [(step - 1, step), (strips - step, strips - step...  9.83 us
    pallas_call x2, Pallas kernels, pack_half(): pl.pallas_call(functools.partial(pack_body, sizes), grid_spec=pltpu.Prefe...  9.46 us
    pallas_call x1, Pallas kernels, text_partial(): pl.pallas_call(functools.partial(text_body, groups), grid_spec=pltpu.Pref...  8.46 us
    ppermute x6, starting transfers between devices, swap(): return lax.ppermute(array, 'height', [(0, 1), (1, 0)])  5.87 us
    ppermute x6, waiting for transfers between devices, swap(): return lax.ppermute(array, 'height', [(0, 1), (1, 0)])  4.41 us
  transfers between devices with their start and end apart: 15, of which 8 were waited for; matrix products, arithmetic and copies ran while one was open for 2% of the time, Pallas kernels for 40%

profile of v2, /device:TPU:21, one launch (start us, length us, event | category | flops | bytes accessed | tf_op | source)
XLA Modules:
  0.0 111.4 jit_solution(17638670658400454736)
XLA Ops:
  0.6 0.7 stack.43.scal
  1.3 4.6 %pack.2.rest_0_.mine_ref = bf16[2,6,4,2,64,128]{5,4,3,2,1,0:T(8,128)(2,1)} custom-call(s32[6]{0:T(128)} %stack.43.scal, bf16[16,8,4,1536]{3,2,1,0:T(4,128)(2,1)} %rest_0_.3, bf16[16,8,4,1536]{3,2,1,0:T(4,128)(2,1)} %rest_1_.3), custom_call_target="tpu_custom_call" | custom-call | bytes 1 | tf_op jit(solution)/shard_map/pack/pallas_call | solution.py:77
  5.9 3.2 %collective-permute-start.1 = (bf16[2,6,4,2,64,128]{5,4,3,2,1,0:T(8,128)(2,1)}, bf16[2,6,4,2,64,128]{5,4,3,2,1,0:T(8,128)(2,1)}, u32[]{:S(2)}, u32[]{:S(2)}) collective-permute-start(bf16[2,6,4,2,64,128]{5,4,3,2,1,0:T(8,128)(2,1)} %pack.2.rest_0_.mine_ref), channel_id=1, source_target_pairs={{0,4},{4,8},{8,12},{1,5},{5,9},{9,13},{2,6},{6,10},{10,14},{3,7},{... | collective-permute-start | bytes 4718600 | tf_op jit(solution)/shard_map/ppermute | solution.py:392
  9.2 2.1 %collective-permute-start.2 = (bf16[2,6,4,2,64,128]{5,4,3,2,1,0:T(8,128)(2,1)}, bf16[2,6,4,2,64,128]{5,4,3,2,1,0:T(8,128)(2,1)}, u32[]{:S(2)}, u32[]{:S(2)}) collective-permute-start(bf16[2,6,4,2,64,128]{5,4,3,2,1,0:T(8,128)(2,1)} %pack.2.rest_0_.mine_ref), channel_id=1, source_target_pairs={{4,0},{8,4},{12,8},{5,1},{9,5},{13,9},{6,2},{10,6},{14,10},{7,3},{... | collective-permute-start | bytes 4718600 | tf_op jit(solution)/shard_map/ppermute | solution.py:392
  11.2 4.8 %pack.3 = (bf16[2,3,4,2,64,128]{5,4,3,2,1,0:T(8,128)(2,1)}, bf16[2,3,4,2,64,128]{5,4,3,2,1,0:T(8,128)(2,1)}, bf16[16,8,4,768]{3,2,1,0:T(4,128)(2,1)}) custom-call(s32[6]{0:T(128)} %stack.43.scal, bf16[16,8,4,1536]{3,2,1,0:T(4,128)(2,1)} %rest_0_.3, bf16[16,8,4,1536]{3,2,1,0:T(4,128)(2,1)} %rest_1_.3, bf16[16,8,4,1536]{3,2,1,0:T(4,128)(2,1)} %own_q.3), custom_call_target="tpu_custom_call" | custom-call | bytes 1 | tf_op jit(solution)/shard_map/pack/pallas_call | solution.py:77
  16.1 1.2 %collective-permute-start = (bf16[16,8,4,768]{3,2,1,0:T(4,128)(2,1)}, bf16[16,8,4,768]{3,2,1,0:T(4,128)(2,1)S(1)}, u32[]{:S(2)}, u32[]{:S(2)}) collective-permute-start(bf16[16,8,4,768]{3,2,1,0:T(4,128)(2,1)} %get-tuple-element.17), channel_id=1, source_target_pairs={{0,2},{2,0},{1,3},{3,1},{4,6},{6,4},{5,7},{7,5},{8,10},{10,8},{9,1... | collective-permute-start | bytes 2359304 | tf_op jit(solution)/shard_map/ppermute | solution.py:381
  17.3 0.0 collective-permute-start.3
  17.3 0.5 collective-permute-start.6
  17.8 2.4 %collective-permute-done.pair_q = bf16[16,8,4,768]{3,2,1,0:T(4,128)(2,1)S(1)} collective-permute-done((bf16[16,8,4,768]{3,2,1,0:T(4,128)(2,1)}, bf16[16,8,4,768]{3,2,1,0:T(4,128)(2,1)S(1)}, u32[]{:S(2)}, u32[]{:S(2)}) %collective-permute-start) | collective-permute-done | bytes 786464 | tf_op jit(solution)/shard_map/ppermute | solution.py:381
  20.2 0.0 copy-start
  20.2 0.5 collective-permute-done.3.rest_3_.rest_1_
  20.7 1.1 %collective-permute-done.6.rest_3_.rest_0_ = bf16[2,3,4,2,64,128]{5,4,3,2,1,0:T(8,128)(2,1)} collective-permute-done((bf16[2,3,4,2,64,128]{5,4,3,2,1,0:T(8,128)(2,1)}, bf16[2,3,4,2,64,128]{5,4,3,2,1,0:T(8,128)(2,1)}, u32[]{:S(2)}, u32[]{:S(2)}) %collective-permute-start.6) | collective-permute-done | bytes 786464 | tf_op jit(solution)/shard_map/ppermute | solution.py:381
  21.8 8.5 %text.1 = (f32[6,256,128]{2,1,0:T(8,128)}, f32[256,128]{1,0:T(8,128)}, bf16[7,256,128]{2,1,0:T(8,128)(2,1)}) custom-call(s32[6]{0:T(128)} %stack.43.scal, s32[1,256]{1,0:T(1,128)} %bitcast.7, bf16[256,1536]{1,0:T(8,128)(2,1)} %q_ref.1, bf16[2,6,4,2,64,128]{5,4,3,2,1,0:T(8,128)(2,1)} %pack.2.rest_0_.mine_ref, bf16[256,1536]{1,0:T(8,128)(2,1)} %tk_ref.1, ...), custom_call_target="tpu_custom_call" | custom-call | bytes 1 | tf_op jit(solution)/shard_map/text/pallas_call | solution.py:279
  30.3 0.0 copy-done
  30.3 1.3 %collective-permute-start.11 = (bf16[7,256,128]{2,1,0:T(8,128)(2,1)}, bf16[7,256,128]{2,1,0:T(8,128)(2,1)}, u32[]{:S(2)}, u32[]{:S(2)}) collective-permute-start(bf16[7,256,128]{2,1,0:T(8,128)(2,1)} %get-tuple-element.29), channel_id=1, source_target_pairs={{0,4},{12,8},{1,5},{13,9},{2,6},{14,10},{3,7},{15,11},{16,20},{28,... | collective-permute-start | bytes 1376264 | tf_op jit(solution)/shard_map/ppermute | solution.py:403
  31.6 5.1 %collective-permute-start.7 = (bf16[2,3,4,2,64,128]{5,4,3,2,1,0:T(8,128)(2,1)}, bf16[2,3,4,2,64,128]{5,4,3,2,1,0:T(8,128)(2,1)S(1)}, u32[]{:S(2)}, u32[]{:S(2)}) collective-permute-start(bf16[2,3,4,2,64,128]{5,4,3,2,1,0:T(8,128)(2,1)} %collective-permute-done.6.rest_3_.rest_0_), channel_id=1, source_target_pairs={{0,4},{4,8},{8,12},{1,5},{5,9},{9,13},{2,6},{6,10},{10,14},{3,7},{... | collective-permute-start | bytes 2359304 | tf_op jit(solution)/shard_map/ppermute | solution.py:392
  36.7 1.9 %collective-permute-start.8 = (bf16[2,3,4,2,64,128]{5,4,3,2,1,0:T(8,128)(2,1)}, bf16[2,3,4,2,64,128]{5,4,3,2,1,0:T(8,128)(2,1)}, u32[]{:S(2)}, u32[]{:S(2)}) collective-permute-start(bf16[2,3,4,2,64,128]{5,4,3,2,1,0:T(8,128)(2,1)} %collective-permute-done.6.rest_3_.rest_0_), channel_id=1, source_target_pairs={{4,0},{8,4},{12,8},{5,1},{9,5},{13,9},{6,2},{10,6},{14,10},{7,3},{... | collective-permute-start | bytes 2359304 | tf_op jit(solution)/shard_map/ppermute | solution.py:392
  38.6 4.8 %collective-permute-done.1.rest_1_ = bf16[2,6,4,2,64,128]{5,4,3,2,1,0:T(8,128)(2,1)} collective-permute-done((bf16[2,6,4,2,64,128]{5,4,3,2,1,0:T(8,128)(2,1)}, bf16[2,6,4,2,64,128]{5,4,3,2,1,0:T(8,128)(2,1)}, u32[]{:S(2)}, u32[]{:S(2)}) %collective-permute-start.1) | collective-permute-done | bytes 1572896 | tf_op jit(solution)/shard_map/ppermute | solution.py:392
  43.4 2.9 %collective-permute-done.2.rest_2_ = bf16[2,6,4,2,64,128]{5,4,3,2,1,0:T(8,128)(2,1)} collective-permute-done((bf16[2,6,4,2,64,128]{5,4,3,2,1,0:T(8,128)(2,1)}, bf16[2,6,4,2,64,128]{5,4,3,2,1,0:T(8,128)(2,1)}, u32[]{:S(2)}, u32[]{:S(2)}) %collective-permute-start.2) | collective-permute-done | bytes 1572896 | tf_op jit(solution)/shard_map/ppermute | solution.py:392
  46.3 9.8 %collective-permute-done.11.got_ref = bf16[7,256,128]{2,1,0:T(8,128)(2,1)} collective-permute-done((bf16[7,256,128]{2,1,0:T(8,128)(2,1)}, bf16[7,256,128]{2,1,0:T(8,128)(2,1)}, u32[]{:S(2)}, u32[]{:S(2)}) %collective-permute-start.11) | collective-permute-done | bytes 458784 | tf_op jit(solution)/shard_map/ppermute | solution.py:403
  56.1 2.8 %join.1.own_ref = bf16[7,256,128]{2,1,0:T(8,128)(2,1)} custom-call(f32[6,256,128]{2,1,0:T(8,128)} %get-tuple-element.26.sum_ref, f32[256,128]{1,0:T(8,128)} %get-tuple-element.28.log_ref, bf16[7,256,128]{2,1,0:T(8,128)(2,1)} %collective-permute-done.11.got_ref), custom_call_target="tpu_custom_call" | custom-call | bytes 1 | tf_op jit(solution)/shard_map/join/pallas_call | solution.py:327
  58.9 1.9 %collective-permute-start.12 = (bf16[7,256,128]{2,1,0:T(8,128)(2,1)}, bf16[7,256,128]{2,1,0:T(8,128)(2,1)}, u32[]{:S(2)}, u32[]{:S(2)}) collective-permute-start(bf16[7,256,128]{2,1,0:T(8,128)(2,1)} %join.1.own_ref), channel_id=1, source_target_pairs={{4,8},{8,4},{5,9},{9,5},{6,10},{10,6},{7,11},{11,7},{20,24},{24,20... | collective-permute-start | bytes 1376264 | tf_op jit(solution)/shard_map/ppermute | solution.py:405
  60.8 1.9 %collective-permute-start.4 = (bf16[2,3,4,2,64,128]{5,4,3,2,1,0:T(8,128)(2,1)}, bf16[2,3,4,2,64,128]{5,4,3,2,1,0:T(8,128)(2,1)}, u32[]{:S(2)}, u32[]{:S(2)}) collective-permute-start(bf16[2,3,4,2,64,128]{5,4,3,2,1,0:T(8,128)(2,1)} %collective-permute-done.3.rest_3_.rest_1_), channel_id=1, source_target_pairs={{0,4},{4,8},{8,12},{1,5},{5,9},{9,13},{2,6},{6,10},{10,14},{3,7},{... | collective-permute-start | bytes 2359304 | tf_op jit(solution)/shard_map/ppermute | solution.py:392
  62.8 3.4 %collective-permute-start.5 = (bf16[2,3,4,2,64,128]{5,4,3,2,1,0:T(8,128)(2,1)}, bf16[2,3,4,2,64,128]{5,4,3,2,1,0:T(8,128)(2,1)}, u32[]{:S(2)}, u32[]{:S(2)}) collective-permute-start(bf16[2,3,4,2,64,128]{5,4,3,2,1,0:T(8,128)(2,1)} %collective-permute-done.3.rest_3_.rest_1_), channel_id=1, source_target_pairs={{4,0},{8,4},{12,8},{5,1},{9,5},{13,9},{6,2},{10,6},{14,10},{7,3},{... | collective-permute-start | bytes 2359304 | tf_op jit(solution)/shard_map/ppermute | solution.py:392
  66.1 0.0 collective-permute-done.7.rest_4_
  66.2 0.0 copy-start.2
  66.2 6.8 %collective-permute-done.8.rest_5_ = bf16[2,3,4,2,64,128]{5,4,3,2,1,0:T(8,128)(2,1)} collective-permute-done((bf16[2,3,4,2,64,128]{5,4,3,2,1,0:T(8,128)(2,1)}, bf16[2,3,4,2,64,128]{5,4,3,2,1,0:T(8,128)(2,1)}, u32[]{:S(2)}, u32[]{:S(2)}) %collective-permute-start.8) | collective-permute-done | bytes 786464 | tf_op jit(solution)/shard_map/ppermute | solution.py:392
  73.0 0.0 copy-done.2
  73.0 12.8 %video.2 = (bf16[16,8,4,1536]{3,2,1,0:T(4,128)(2,1)}, bf16[16,8,4,384]{3,2,1,0:T(4,128)(2,1)}) custom-call(s32[6]{0:T(128)} %stack.43.scal, s32[1,256]{1,0:T(1,128)} %bitcast.8, bf16[16,8,4,1536]{3,2,1,0:T(4,128)(2,1)} %own_q.3, bf16[16,8,4,768]{3,2,1,0:T(4,128)(2,1)} %copy-done, bf16[2,6,4,2,64,128]{5,4,3,2,1,0:T(8,128)(2,1)} %pack.2.rest_0_.mine_ref, ...), custom_call_target="tpu_custom_call" | custom-call | bytes 1 | tf_op jit(solution)/shard_map/video/pallas_call | solution.py:184
  85.8 0.0 collective-permute-done.12.got_ref
  85.8 3.3 %finish.1 = bf16[256,768]{1,0:T(8,128)(2,1)} custom-call(s32[6]{0:T(128)} %stack.43.scal, bf16[7,256,128]{2,1,0:T(8,128)(2,1)} %join.1.own_ref, bf16[7,256,128]{2,1,0:T(8,128)(2,1)} %collective-permute-done.12.got_ref), custom_call_target="tpu_custom_call" | custom-call | bytes 1 | tf_op jit(solution)/shard_map/finish/pallas_call | solution.py:353
  89.1 2.1 %collective-permute-start.13 = (bf16[256,768]{1,0:T(8,128)(2,1)}, bf16[256,768]{1,0:T(8,128)(2,1)}, u32[]{:S(2)}, u32[]{:S(2)}) collective-permute-start(bf16[256,768]{1,0:T(8,128)(2,1)} %finish.1), channel_id=1, source_target_pairs={{4,0},{8,12},{5,1},{9,13},{6,2},{10,14},{7,3},{11,15},{20,16},{24,... | collective-permute-start | bytes 1179656 | tf_op jit(solution)/shard_map/ppermute | solution.py:428
  91.2 0.0 copy-start.1
  91.2 3.5 %collective-permute-start.9 = (bf16[16,8,4,384]{3,2,1,0:T(4,128)(2,1)}, bf16[16,8,4,384]{3,2,1,0:T(4,128)(2,1)S(1)}, u32[]{:S(2)}, u32[]{:S(2)}) collective-permute-start(bf16[16,8,4,384]{3,2,1,0:T(4,128)(2,1)} %get-tuple-element.22), channel_id=1, source_target_pairs={{0,2},{2,0},{1,3},{3,1},{4,6},{6,4},{5,7},{7,5},{8,10},{10,8},{9,1... | collective-permute-start | bytes 1179656 | tf_op jit(solution)/shard_map/ppermute | solution.py:381
  94.7 0.0 collective-permute-done.4.rest_4_
  94.7 0.0 collective-permute-done.5.rest_5_
  94.7 12.9 %video.3 = (bf16[16,8,4,1536]{3,2,1,0:T(4,128)(2,1)}, bf16[16,8,4,384]{3,2,1,0:T(4,128)(2,1)}) custom-call(s32[6]{0:T(128)} %stack.43.scal, s32[1,256]{1,0:T(1,128)} %bitcast.9, bf16[16,8,4,1536]{3,2,1,0:T(4,128)(2,1)} %own_q.3, bf16[16,8,4,768]{3,2,1,0:T(4,128)(2,1)} %copy-done, ...), custom_call_target="tpu_custom_call", output_to_operand_aliasing={{0}: (12, {})} | custom-call | bytes 1 | tf_op jit(solution)/shard_map/video/pallas_call | solution.py:184
  107.6 0.2 collective-permute-start.10
  107.8 0.0 collective-permute-done.13
  107.8 0.0 copy-done.1
  107.8 0.5 collective-permute-start.14
  108.3 0.0 collective-permute-done.9
  108.3 0.9 constant_dynamic-update-slice_fusion.1
  109.1 0.4 collective-permute-done.10
  109.6 0.9 constant_dynamic-update-slice_fusion
  110.4 0.0 collective-permute-done.14
  110.4 0.1 broadcast_select_fusion.2
  110.5 0.9 pad_maximum_fusion
  (1 shorter events, 0.0 us)
Async XLA Ops:
  5.9 37.5 %collective-permute-start.1 = (bf16[2,6,4,2,64,128]{5,4,3,2,1,0:T(8,128)(2,1)}, bf16[2,6,4,2,64,128]{5,4,3,2,1,0:T(8,128)(2,1)}, u32[]{:S(2)}, u32[]{:S(2)}) collective-permute-start(bf16[2,6,4,2,64,128]{5,4,3,2,1,0:T(8,128)(2,1)} %pack.2.rest_0_.mine_ref), channel_id=1, source_target_pairs={{0,4},{4,8},{8,12},{1,5},{5,9},{9,13},{2,6},{6,10},{10,14},{3,7},{... | collective-permute-start | bytes 4718600 | tf_op jit(solution)/shard_map/ppermute | solution.py:392
  9.2 37.2 %collective-permute-start.2 = (bf16[2,6,4,2,64,128]{5,4,3,2,1,0:T(8,128)(2,1)}, bf16[2,6,4,2,64,128]{5,4,3,2,1,0:T(8,128)(2,1)}, u32[]{:S(2)}, u32[]{:S(2)}) collective-permute-start(bf16[2,6,4,2,64,128]{5,4,3,2,1,0:T(8,128)(2,1)} %pack.2.rest_0_.mine_ref), channel_id=1, source_target_pairs={{4,0},{8,4},{12,8},{5,1},{9,5},{13,9},{6,2},{10,6},{14,10},{7,3},{... | collective-permute-start | bytes 4718600 | tf_op jit(solution)/shard_map/ppermute | solution.py:392
  16.1 4.1 %collective-permute-start = (bf16[16,8,4,768]{3,2,1,0:T(4,128)(2,1)}, bf16[16,8,4,768]{3,2,1,0:T(4,128)(2,1)S(1)}, u32[]{:S(2)}, u32[]{:S(2)}) collective-permute-start(bf16[16,8,4,768]{3,2,1,0:T(4,128)(2,1)} %get-tuple-element.17), channel_id=1, source_target_pairs={{0,2},{2,0},{1,3},{3,1},{4,6},{6,4},{5,7},{7,5},{8,10},{10,8},{9,1... | collective-permute-start | bytes 2359304 | tf_op jit(solution)/shard_map/ppermute | solution.py:381
  17.3 3.4 %collective-permute-start.3 = (bf16[2,3,4,2,64,128]{5,4,3,2,1,0:T(8,128)(2,1)}, bf16[2,3,4,2,64,128]{5,4,3,2,1,0:T(8,128)(2,1)}, u32[]{:S(2)}, u32[]{:S(2)}) collective-permute-start(bf16[2,3,4,2,64,128]{5,4,3,2,1,0:T(8,128)(2,1)} %get-tuple-element.18), channel_id=1, source_target_pairs={{0,2},{2,0},{1,3},{3,1},{4,6},{6,4},{5,7},{7,5},{8,10},{10,8},{9,1... | collective-permute-start | bytes 2359304 | tf_op jit(solution)/shard_map/ppermute | solution.py:381
  17.3 4.5 %collective-permute-start.6 = (bf16[2,3,4,2,64,128]{5,4,3,2,1,0:T(8,128)(2,1)}, bf16[2,3,4,2,64,128]{5,4,3,2,1,0:T(8,128)(2,1)}, u32[]{:S(2)}, u32[]{:S(2)}) collective-permute-start(bf16[2,3,4,2,64,128]{5,4,3,2,1,0:T(8,128)(2,1)} %get-tuple-element.19), channel_id=1, source_target_pairs={{0,2},{2,0},{1,3},{3,1},{4,6},{6,4},{5,7},{7,5},{8,10},{10,8},{9,1... | collective-permute-start | bytes 2359304 | tf_op jit(solution)/shard_map/ppermute | solution.py:381
  20.2 10.1 %copy-start = (bf16[16,8,4,768]{3,2,1,0:T(4,128)(2,1)}, bf16[16,8,4,768]{3,2,1,0:T(4,128)(2,1)S(1)}, u32[]{:S(2)}) copy-start(bf16[16,8,4,768]{3,2,1,0:T(4,128)(2,1)S(1)} %collective-permute-done.pair_q) | copy-start | bytes 2359300
  30.3 25.9 %collective-permute-start.11 = (bf16[7,256,128]{2,1,0:T(8,128)(2,1)}, bf16[7,256,128]{2,1,0:T(8,128)(2,1)}, u32[]{:S(2)}, u32[]{:S(2)}) collective-permute-start(bf16[7,256,128]{2,1,0:T(8,128)(2,1)} %get-tuple-element.29), channel_id=1, source_target_pairs={{0,4},{12,8},{1,5},{13,9},{2,6},{14,10},{3,7},{15,11},{16,20},{28,... | collective-permute-start | bytes 1376264 | tf_op jit(solution)/shard_map/ppermute | solution.py:403
  31.6 34.6 %collective-permute-start.7 = (bf16[2,3,4,2,64,128]{5,4,3,2,1,0:T(8,128)(2,1)}, bf16[2,3,4,2,64,128]{5,4,3,2,1,0:T(8,128)(2,1)S(1)}, u32[]{:S(2)}, u32[]{:S(2)}) collective-permute-start(bf16[2,3,4,2,64,128]{5,4,3,2,1,0:T(8,128)(2,1)} %collective-permute-done.6.rest_3_.rest_0_), channel_id=1, source_target_pairs={{0,4},{4,8},{8,12},{1,5},{5,9},{9,13},{2,6},{6,10},{10,14},{3,7},{... | collective-permute-start | bytes 2359304 | tf_op jit(solution)/shard_map/ppermute | solution.py:392
  36.7 36.3 %collective-permute-start.8 = (bf16[2,3,4,2,64,128]{5,4,3,2,1,0:T(8,128)(2,1)}, bf16[2,3,4,2,64,128]{5,4,3,2,1,0:T(8,128)(2,1)}, u32[]{:S(2)}, u32[]{:S(2)}) collective-permute-start(bf16[2,3,4,2,64,128]{5,4,3,2,1,0:T(8,128)(2,1)} %collective-permute-done.6.rest_3_.rest_0_), channel_id=1, source_target_pairs={{4,0},{8,4},{12,8},{5,1},{9,5},{13,9},{6,2},{10,6},{14,10},{7,3},{... | collective-permute-start | bytes 2359304 | tf_op jit(solution)/shard_map/ppermute | solution.py:392
  58.9 26.9 %collective-permute-start.12 = (bf16[7,256,128]{2,1,0:T(8,128)(2,1)}, bf16[7,256,128]{2,1,0:T(8,128)(2,1)}, u32[]{:S(2)}, u32[]{:S(2)}) collective-permute-start(bf16[7,256,128]{2,1,0:T(8,128)(2,1)} %join.1.own_ref), channel_id=1, source_target_pairs={{4,8},{8,4},{5,9},{9,5},{6,10},{10,6},{7,11},{11,7},{20,24},{24,20... | collective-permute-start | bytes 1376264 | tf_op jit(solution)/shard_map/ppermute | solution.py:405
  60.8 33.8 %collective-permute-start.4 = (bf16[2,3,4,2,64,128]{5,4,3,2,1,0:T(8,128)(2,1)}, bf16[2,3,4,2,64,128]{5,4,3,2,1,0:T(8,128)(2,1)}, u32[]{:S(2)}, u32[]{:S(2)}) collective-permute-start(bf16[2,3,4,2,64,128]{5,4,3,2,1,0:T(8,128)(2,1)} %collective-permute-done.3.rest_3_.rest_1_), channel_id=1, source_target_pairs={{0,4},{4,8},{8,12},{1,5},{5,9},{9,13},{2,6},{6,10},{10,14},{3,7},{... | collective-permute-start | bytes 2359304 | tf_op jit(solution)/shard_map/ppermute | solution.py:392
  62.8 31.9 %collective-permute-start.5 = (bf16[2,3,4,2,64,128]{5,4,3,2,1,0:T(8,128)(2,1)}, bf16[2,3,4,2,64,128]{5,4,3,2,1,0:T(8,128)(2,1)}, u32[]{:S(2)}, u32[]{:S(2)}) collective-permute-start(bf16[2,3,4,2,64,128]{5,4,3,2,1,0:T(8,128)(2,1)} %collective-permute-done.3.rest_3_.rest_1_), channel_id=1, source_target_pairs={{4,0},{8,4},{12,8},{5,1},{9,5},{13,9},{6,2},{10,6},{14,10},{7,3},{... | collective-permute-start | bytes 2359304 | tf_op jit(solution)/shard_map/ppermute | solution.py:392
  66.2 6.8 %copy-start.2 = (bf16[2,3,4,2,64,128]{5,4,3,2,1,0:T(8,128)(2,1)}, bf16[2,3,4,2,64,128]{5,4,3,2,1,0:T(8,128)(2,1)S(1)}, u32[]{:S(2)}) copy-start(bf16[2,3,4,2,64,128]{5,4,3,2,1,0:T(8,128)(2,1)S(1)} %collective-permute-done.7.rest_4_) | copy-start | bytes 2359300
  89.1 18.6 %collective-permute-start.13 = (bf16[256,768]{1,0:T(8,128)(2,1)}, bf16[256,768]{1,0:T(8,128)(2,1)}, u32[]{:S(2)}, u32[]{:S(2)}) collective-permute-start(bf16[256,768]{1,0:T(8,128)(2,1)} %finish.1), channel_id=1, source_target_pairs={{4,0},{8,12},{5,1},{9,13},{6,2},{10,14},{7,3},{11,15},{20,16},{24,... | collective-permute-start | bytes 1179656 | tf_op jit(solution)/shard_map/ppermute | solution.py:428
  91.2 16.6 %copy-start.1 = (bf16[256,768]{1,0:T(8,128)(2,1)S(1)}, bf16[256,768]{1,0:T(8,128)(2,1)}, u32[]{:S(2)}) copy-start(bf16[256,768]{1,0:T(8,128)(2,1)} %finish.1) | copy-start | bytes 1179652
  91.2 17.1 %collective-permute-start.9 = (bf16[16,8,4,384]{3,2,1,0:T(4,128)(2,1)}, bf16[16,8,4,384]{3,2,1,0:T(4,128)(2,1)S(1)}, u32[]{:S(2)}, u32[]{:S(2)}) collective-permute-start(bf16[16,8,4,384]{3,2,1,0:T(4,128)(2,1)} %get-tuple-element.22), channel_id=1, source_target_pairs={{0,2},{2,0},{1,3},{3,1},{4,6},{6,4},{5,7},{7,5},{8,10},{10,8},{9,1... | collective-permute-start | bytes 1179656 | tf_op jit(solution)/shard_map/ppermute | solution.py:381
  107.6 2.0 %collective-permute-start.10 = (bf16[16,8,4,384]{3,2,1,0:T(4,128)(2,1)}, bf16[16,8,4,384]{3,2,1,0:T(4,128)(2,1)S(1)}, u32[]{:S(2)}, u32[]{:S(2)}) collective-permute-start(bf16[16,8,4,384]{3,2,1,0:T(4,128)(2,1)} %get-tuple-element.23), channel_id=1, source_target_pairs={{0,2},{2,0},{1,3},{3,1},{4,6},{6,4},{5,7},{7,5},{8,10},{10,8},{9,1... | collective-permute-start | bytes 1179656 | tf_op jit(solution)/shard_map/ppermute | solution.py:381
  107.8 2.6 %collective-permute-start.14 = (bf16[256,768]{1,0:T(8,128)(2,1)S(1)}, bf16[256,768]{1,0:T(8,128)(2,1)S(1)}, u32[]{:S(2)}, u32[]{:S(2)}) collective-permute-start(bf16[256,768]{1,0:T(8,128)(2,1)S(1)} %broadcast_select_fusion), channel_id=1, source_target_pairs={{0,2},{2,0},{1,3},{3,1},{4,6},{6,4},{5,7},{7,5},{8,10},{10,8},{9,1... | collective-permute-start | bytes 1179656 | tf_op jit(solution)/shard_map/ppermute | solution.py:381

commit v3 on v2

--- a/solution.py
+++ b/solution.py
@@ -15,7 +15,7 @@
 F32 = jnp.float32
 SCALE = 1.0 / math.sqrt(HD)
 SCALE_2 = SCALE * math.log2(math.e)
-VMEM = 63 << 20
+VMEM = 255 << 18
 THIRD = 32
 SIZES = (3, 3)
 
@@ -51,8 +51,11 @@
             lanes = slice(head * HD, (head + 1) * HD)
             head += 1
             for which, ref in enumerate((k_ref, v_ref)):
-                for r in range(ref.shape[1] // TILE):
-                    kv_ref[which, at, 0, r] = ref[:, r * TILE : (r + 1) * TILE, :, lanes].reshape(VOL, HD)
+                for t in range(ref.shape[0] // TILE):
+                    frames = slice(t * TILE, (t + 1) * TILE)
+                    for r in range(ref.shape[1] // TILE):
+                        tile = ref[frames, r * TILE : (r + 1) * TILE, :, lanes]
+                        kv_ref[which, at, t, r] = tile.reshape(VOL, HD)
     if len(rest) == len(sizes) + 4:
         rest[-1][...] = rest[2][...]
 
@@ -62,22 +65,23 @@
     time_tiles = frames // TILE
     row_tiles = rows // TILE
     theirs = query_video is not None
+    depth = 2 if time_tiles % 2 == 0 else 1
     block = pl.BlockSpec(
-        (TILE, rows, cols, features // 2), lambda t, s: (t, 0, 0, 1 - s[4] if theirs else s[4])
+        (depth * TILE, rows, cols, features // 2), lambda t, s: (t, 0, 0, 1 - s[4] if theirs else s[4])
     )
     operands = [key_video, value_video]
     out_specs = [
-        pl.BlockSpec((2, size, 1, row_tiles, VOL, HD), lambda t, s: (0, 0, t, 0, 0, 0)) for size in sizes
+        pl.BlockSpec((2, size, depth, row_tiles, VOL, HD), lambda t, s: (0, 0, t, 0, 0, 0)) for size in sizes
     ]
     out_shape = [jax.ShapeDtypeStruct((2, size, time_tiles, row_tiles, VOL, HD), BF16) for size in sizes]
     if theirs:
         operands.append(query_video)
-        out_specs.append(pl.BlockSpec((TILE, rows, cols, features // 2), lambda t, s: (t, 0, 0, 0)))
+        out_specs.append(pl.BlockSpec((depth * TILE, rows, cols, features // 2), lambda t, s: (t, 0, 0, 0)))
         out_shape.append(jax.ShapeDtypeStruct((frames, rows, cols, features // 2), BF16))
     return pl.pallas_call(
         functools.partial(pack_body, sizes),
         grid_spec=pltpu.PrefetchScalarGridSpec(
-            num_scalar_prefetch=1, grid=(time_tiles,), in_specs=[block] * len(operands), out_specs=out_specs
+            num_scalar_prefetch=1, grid=(time_tiles // depth,), in_specs=[block] * len(operands), out_specs=out_specs
         ),
         out_shape=out_shape,
         compiler_params=pltpu.CompilerParams(vmem_limit_bytes=VMEM),

time: 112 us -> 112 us (level)
  Pallas kernels: 49.7 us -> 47.3 us
    pallas_call x2, Pallas kernels: 9.46 us -> 6.98 us  [pack_half(): pl.pallas_call(functools.partial(pack_body, sizes), grid_spec=pltpu.Prefe...]
    ppermute x6, waiting for transfers between devices: 14.5 us -> 15.7 us  [to_neighbours(): return (lax.ppermute(array, 'tm', up), lax.ppermute(array, 'tm', down))]
  transfers between devices with their start and end apart: 15 -> 15, of which waited for: 8 -> 7; matrix products, arithmetic and copies ran while one was open for 2% -> 3% of each run, Pallas kernels for 40% -> 39%
where the time goes in v3:
time: 112 us
  Pallas kernels  47.3 us (42%)
  waiting for transfers between devices  29.5 us (26%)
  starting transfers between devices  28.7 us (26%)
  local copies, waits for them, and re-layouts  3.38 us (3%)
  other arithmetic  2.04 us (2%)
    pallas_call x2, Pallas kernels, video_group(): pl.pallas_call(video_body, grid_spec=pltpu.PrefetchScalarGridSpec(num_sca...  25.7 us
    ppermute x6, starting transfers between devices, to_neighbours(): return (lax.ppermute(array, 'tm', up), lax.ppermute(array, 'tm', down))  17.6 us
    ppermute x6, waiting for transfers between devices, to_neighbours(): return (lax.ppermute(array, 'tm', up), lax.ppermute(array, 'tm', down))  15.7 us
    ppermute x1, waiting for transfers between devices, shards(): lax.ppermute(sent, 'tm', [(step - 1, step), (strips - step, strips - step...  9.83 us
    pallas_call x1, Pallas kernels, text_partial(): pl.pallas_call(functools.partial(text_body, groups), grid_spec=pltpu.Pref...  8.46 us
    pallas_call x2, Pallas kernels, pack_half(): pl.pallas_call(functools.partial(pack_body, sizes), grid_spec=pltpu.Prefe...  6.98 us
    ppermute x6, starting transfers between devices, swap(): return lax.ppermute(array, 'height', [(0, 1), (1, 0)])  5.84 us
    ppermute x6, waiting for transfers between devices, swap(): return lax.ppermute(array, 'height', [(0, 1), (1, 0)])  4 us
  transfers between devices with their start and end apart: 15, of which 7 were waited for; matrix products, arithmetic and copies ran while one was open for 3% of the time, Pallas kernels for 39%

profile of v3, /device:TPU:21, one launch (start us, length us, event | category | flops | bytes accessed | tf_op | source)
XLA Modules:
  0.0 111.7 jit_solution(11223824174633641130)
XLA Ops:
  0.6 0.6 stack.43.scal
  1.3 3.3 %pack.2.rest_0_.mine_ref = bf16[2,6,4,2,64,128]{5,4,3,2,1,0:T(8,128)(2,1)} custom-call(s32[6]{0:T(128)} %stack.43.scal, bf16[16,8,4,1536]{3,2,1,0:T(4,128)(2,1)} %rest_0_.3, bf16[16,8,4,1536]{3,2,1,0:T(4,128)(2,1)} %rest_1_.3), custom_call_target="tpu_custom_call" | custom-call | bytes 1 | tf_op jit(solution)/shard_map/pack/pallas_call | solution.py:81
  4.6 3.2 %collective-permute-start.1 = (bf16[2,6,4,2,64,128]{5,4,3,2,1,0:T(8,128)(2,1)}, bf16[2,6,4,2,64,128]{5,4,3,2,1,0:T(8,128)(2,1)}, u32[]{:S(2)}, u32[]{:S(2)}) collective-permute-start(bf16[2,6,4,2,64,128]{5,4,3,2,1,0:T(8,128)(2,1)} %pack.2.rest_0_.mine_ref), channel_id=1, source_target_pairs={{0,4},{4,8},{8,12},{1,5},{5,9},{9,13},{2,6},{6,10},{10,14},{3,7},{... | collective-permute-start | bytes 4718600 | tf_op jit(solution)/shard_map/ppermute | solution.py:396
  7.8 2.1 %collective-permute-start.2 = (bf16[2,6,4,2,64,128]{5,4,3,2,1,0:T(8,128)(2,1)}, bf16[2,6,4,2,64,128]{5,4,3,2,1,0:T(8,128)(2,1)}, u32[]{:S(2)}, u32[]{:S(2)}) collective-permute-start(bf16[2,6,4,2,64,128]{5,4,3,2,1,0:T(8,128)(2,1)} %pack.2.rest_0_.mine_ref), channel_id=1, source_target_pairs={{4,0},{8,4},{12,8},{5,1},{9,5},{13,9},{6,2},{10,6},{14,10},{7,3},{... | collective-permute-start | bytes 4718600 | tf_op jit(solution)/shard_map/ppermute | solution.py:396
  9.9 3.7 %pack.3 = (bf16[2,3,4,2,64,128]{5,4,3,2,1,0:T(8,128)(2,1)}, bf16[2,3,4,2,64,128]{5,4,3,2,1,0:T(8,128)(2,1)}, bf16[16,8,4,768]{3,2,1,0:T(4,128)(2,1)}) custom-call(s32[6]{0:T(128)} %stack.43.scal, bf16[16,8,4,1536]{3,2,1,0:T(4,128)(2,1)} %rest_0_.3, bf16[16,8,4,1536]{3,2,1,0:T(4,128)(2,1)} %rest_1_.3, bf16[16,8,4,1536]{3,2,1,0:T(4,128)(2,1)} %own_q.3), custom_call_target="tpu_custom_call" | custom-call | bytes 1 | tf_op jit(solution)/shard_map/pack/pallas_call | solution.py:81
  13.5 1.2 %collective-permute-start = (bf16[16,8,4,768]{3,2,1,0:T(4,128)(2,1)}, bf16[16,8,4,768]{3,2,1,0:T(4,128)(2,1)}, u32[]{:S(2)}, u32[]{:S(2)}) collective-permute-start(bf16[16,8,4,768]{3,2,1,0:T(4,128)(2,1)} %get-tuple-element.17), channel_id=1, source_target_pairs={{0,2},{2,0},{1,3},{3,1},{4,6},{6,4},{5,7},{7,5},{8,10},{10,8},{9,1... | collective-permute-start | bytes 2359304 | tf_op jit(solution)/shard_map/ppermute | solution.py:385
  14.8 0.0 collective-permute-start.3
  14.8 0.5 collective-permute-start.6
  15.3 1.7 %collective-permute-done.pair_q = bf16[16,8,4,768]{3,2,1,0:T(4,128)(2,1)} collective-permute-done((bf16[16,8,4,768]{3,2,1,0:T(4,128)(2,1)}, bf16[16,8,4,768]{3,2,1,0:T(4,128)(2,1)}, u32[]{:S(2)}, u32[]{:S(2)}) %collective-permute-start) | collective-permute-done | bytes 786464 | tf_op jit(solution)/shard_map/ppermute | solution.py:385
  17.0 1.1 %collective-permute-done.3.rest_3_.rest_1_ = bf16[2,3,4,2,64,128]{5,4,3,2,1,0:T(8,128)(2,1)} collective-permute-done((bf16[2,3,4,2,64,128]{5,4,3,2,1,0:T(8,128)(2,1)}, bf16[2,3,4,2,64,128]{5,4,3,2,1,0:T(8,128)(2,1)}, u32[]{:S(2)}, u32[]{:S(2)}) %collective-permute-start.3) | collective-permute-done | bytes 786464 | tf_op jit(solution)/shard_map/ppermute | solution.py:385
  18.2 1.1 %collective-permute-done.6.rest_3_.rest_0_ = bf16[2,3,4,2,64,128]{5,4,3,2,1,0:T(8,128)(2,1)} collective-permute-done((bf16[2,3,4,2,64,128]{5,4,3,2,1,0:T(8,128)(2,1)}, bf16[2,3,4,2,64,128]{5,4,3,2,1,0:T(8,128)(2,1)}, u32[]{:S(2)}, u32[]{:S(2)}) %collective-permute-start.6) | collective-permute-done | bytes 786464 | tf_op jit(solution)/shard_map/ppermute | solution.py:385
  19.3 8.5 %text.1 = (f32[6,256,128]{2,1,0:T(8,128)}, f32[256,128]{1,0:T(8,128)}, bf16[7,256,128]{2,1,0:T(8,128)(2,1)}) custom-call(s32[6]{0:T(128)} %stack.43.scal, s32[1,256]{1,0:T(1,128)} %bitcast.7, bf16[256,1536]{1,0:T(8,128)(2,1)} %q_ref.1, bf16[2,6,4,2,64,128]{5,4,3,2,1,0:T(8,128)(2,1)} %pack.2.rest_0_.mine_ref, bf16[256,1536]{1,0:T(8,128)(2,1)} %tk_ref.1, ...), custom_call_target="tpu_custom_call" | custom-call | bytes 1 | tf_op jit(solution)/shard_map/text/pallas_call | solution.py:283
  27.7 1.3 %collective-permute-start.11 = (bf16[7,256,128]{2,1,0:T(8,128)(2,1)}, bf16[7,256,128]{2,1,0:T(8,128)(2,1)}, u32[]{:S(2)}, u32[]{:S(2)}) collective-permute-start(bf16[7,256,128]{2,1,0:T(8,128)(2,1)} %get-tuple-element.29), channel_id=1, source_target_pairs={{0,4},{12,8},{1,5},{13,9},{2,6},{14,10},{3,7},{15,11},{16,20},{28,... | collective-permute-start | bytes 1376264 | tf_op jit(solution)/shard_map/ppermute | solution.py:407
  29.0 5.1 %collective-permute-start.7 = (bf16[2,3,4,2,64,128]{5,4,3,2,1,0:T(8,128)(2,1)}, bf16[2,3,4,2,64,128]{5,4,3,2,1,0:T(8,128)(2,1)}, u32[]{:S(2)}, u32[]{:S(2)}) collective-permute-start(bf16[2,3,4,2,64,128]{5,4,3,2,1,0:T(8,128)(2,1)} %collective-permute-done.6.rest_3_.rest_0_), channel_id=1, source_target_pairs={{0,4},{4,8},{8,12},{1,5},{5,9},{9,13},{2,6},{6,10},{10,14},{3,7},{... | collective-permute-start | bytes 2359304 | tf_op jit(solution)/shard_map/ppermute | solution.py:396
  34.1 1.9 %collective-permute-start.8 = (bf16[2,3,4,2,64,128]{5,4,3,2,1,0:T(8,128)(2,1)}, bf16[2,3,4,2,64,128]{5,4,3,2,1,0:T(8,128)(2,1)}, u32[]{:S(2)}, u32[]{:S(2)}) collective-permute-start(bf16[2,3,4,2,64,128]{5,4,3,2,1,0:T(8,128)(2,1)} %collective-permute-done.6.rest_3_.rest_0_), channel_id=1, source_target_pairs={{4,0},{8,4},{12,8},{5,1},{9,5},{13,9},{6,2},{10,6},{14,10},{7,3},{... | collective-permute-start | bytes 2359304 | tf_op jit(solution)/shard_map/ppermute | solution.py:396
  36.1 6.0 %collective-permute-done.1.rest_1_ = bf16[2,6,4,2,64,128]{5,4,3,2,1,0:T(8,128)(2,1)} collective-permute-done((bf16[2,6,4,2,64,128]{5,4,3,2,1,0:T(8,128)(2,1)}, bf16[2,6,4,2,64,128]{5,4,3,2,1,0:T(8,128)(2,1)}, u32[]{:S(2)}, u32[]{:S(2)}) %collective-permute-start.1) | collective-permute-done | bytes 1572896 | tf_op jit(solution)/shard_map/ppermute | solution.py:396
  42.1 2.9 %collective-permute-done.2.rest_2_ = bf16[2,6,4,2,64,128]{5,4,3,2,1,0:T(8,128)(2,1)} collective-permute-done((bf16[2,6,4,2,64,128]{5,4,3,2,1,0:T(8,128)(2,1)}, bf16[2,6,4,2,64,128]{5,4,3,2,1,0:T(8,128)(2,1)}, u32[]{:S(2)}, u32[]{:S(2)}) %collective-permute-start.2) | collective-permute-done | bytes 1572896 | tf_op jit(solution)/shard_map/ppermute | solution.py:396
  45.0 9.8 %collective-permute-done.11.got_ref = bf16[7,256,128]{2,1,0:T(8,128)(2,1)} collective-permute-done((bf16[7,256,128]{2,1,0:T(8,128)(2,1)}, bf16[7,256,128]{2,1,0:T(8,128)(2,1)}, u32[]{:S(2)}, u32[]{:S(2)}) %collective-permute-start.11) | collective-permute-done | bytes 458784 | tf_op jit(solution)/shard_map/ppermute | solution.py:407
  54.8 2.8 %join.1.own_ref = bf16[7,256,128]{2,1,0:T(8,128)(2,1)} custom-call(f32[6,256,128]{2,1,0:T(8,128)} %get-tuple-element.26.sum_ref, f32[256,128]{1,0:T(8,128)} %get-tuple-element.28.log_ref, bf16[7,256,128]{2,1,0:T(8,128)(2,1)} %collective-permute-done.11.got_ref), custom_call_target="tpu_custom_call" | custom-call | bytes 1 | tf_op jit(solution)/shard_map/join/pallas_call | solution.py:331
  57.6 1.9 %collective-permute-start.12 = (bf16[7,256,128]{2,1,0:T(8,128)(2,1)}, bf16[7,256,128]{2,1,0:T(8,128)(2,1)}, u32[]{:S(2)}, u32[]{:S(2)}) collective-permute-start(bf16[7,256,128]{2,1,0:T(8,128)(2,1)} %join.1.own_ref), channel_id=1, source_target_pairs={{4,8},{8,4},{5,9},{9,5},{6,10},{10,6},{7,11},{11,7},{20,24},{24,20... | collective-permute-start | bytes 1376264 | tf_op jit(solution)/shard_map/ppermute | solution.py:409
  59.5 1.9 %collective-permute-start.4 = (bf16[2,3,4,2,64,128]{5,4,3,2,1,0:T(8,128)(2,1)}, bf16[2,3,4,2,64,128]{5,4,3,2,1,0:T(8,128)(2,1)}, u32[]{:S(2)}, u32[]{:S(2)}) collective-permute-start(bf16[2,3,4,2,64,128]{5,4,3,2,1,0:T(8,128)(2,1)} %collective-permute-done.3.rest_3_.rest_1_), channel_id=1, source_target_pairs={{0,4},{4,8},{8,12},{1,5},{5,9},{9,13},{2,6},{6,10},{10,14},{3,7},{... | collective-permute-start | bytes 2359304 | tf_op jit(solution)/shard_map/ppermute | solution.py:396
  61.4 3.4 %collective-permute-start.5 = (bf16[2,3,4,2,64,128]{5,4,3,2,1,0:T(8,128)(2,1)}, bf16[2,3,4,2,64,128]{5,4,3,2,1,0:T(8,128)(2,1)}, u32[]{:S(2)}, u32[]{:S(2)}) collective-permute-start(bf16[2,3,4,2,64,128]{5,4,3,2,1,0:T(8,128)(2,1)} %collective-permute-done.3.rest_3_.rest_1_), channel_id=1, source_target_pairs={{4,0},{8,4},{12,8},{5,1},{9,5},{13,9},{6,2},{10,6},{14,10},{7,3},{... | collective-permute-start | bytes 2359304 | tf_op jit(solution)/shard_map/ppermute | solution.py:396
  64.8 0.0 collective-permute-done.7.rest_4_
  64.8 6.8 %collective-permute-done.8.rest_5_ = bf16[2,3,4,2,64,128]{5,4,3,2,1,0:T(8,128)(2,1)} collective-permute-done((bf16[2,3,4,2,64,128]{5,4,3,2,1,0:T(8,128)(2,1)}, bf16[2,3,4,2,64,128]{5,4,3,2,1,0:T(8,128)(2,1)}, u32[]{:S(2)}, u32[]{:S(2)}) %collective-permute-start.8) | collective-permute-done | bytes 786464 | tf_op jit(solution)/shard_map/ppermute | solution.py:396
  71.6 12.8 %video.2 = (bf16[16,8,4,1536]{3,2,1,0:T(4,128)(2,1)}, bf16[16,8,4,384]{3,2,1,0:T(4,128)(2,1)}) custom-call(s32[6]{0:T(128)} %stack.43.scal, s32[1,256]{1,0:T(1,128)} %bitcast.8, bf16[16,8,4,1536]{3,2,1,0:T(4,128)(2,1)} %own_q.3, bf16[16,8,4,768]{3,2,1,0:T(4,128)(2,1)} %collective-permute-done.pair_q, bf16[2,6,4,2,64,128]{5,4,3,2,1,0:T(8,128)(2,1)} %pack.2.rest_0_.mine_ref, ...), custom_call_target="tpu_custom_call" | custom-call | bytes 1 | tf_op jit(solution)/shard_map/video/pallas_call | solution.py:188
  84.5 0.0 collective-permute-done.12.got_ref
  84.5 3.3 %finish.1 = bf16[256,768]{1,0:T(8,128)(2,1)} custom-call(s32[6]{0:T(128)} %stack.43.scal, bf16[7,256,128]{2,1,0:T(8,128)(2,1)} %join.1.own_ref, bf16[7,256,128]{2,1,0:T(8,128)(2,1)} %collective-permute-done.12.got_ref), custom_call_target="tpu_custom_call" | custom-call | bytes 1 | tf_op jit(solution)/shard_map/finish/pallas_call | solution.py:357
  87.8 2.0 %collective-permute-start.13 = (bf16[256,768]{1,0:T(8,128)(2,1)}, bf16[256,768]{1,0:T(8,128)(2,1)}, u32[]{:S(2)}, u32[]{:S(2)}) collective-permute-start(bf16[256,768]{1,0:T(8,128)(2,1)} %finish.1), channel_id=1, source_target_pairs={{4,0},{8,12},{5,1},{9,13},{6,2},{10,14},{7,3},{11,15},{20,16},{24,... | collective-permute-start | bytes 1179656 | tf_op jit(solution)/shard_map/ppermute | solution.py:432
  89.8 3.5 %collective-permute-start.9 = (bf16[16,8,4,384]{3,2,1,0:T(4,128)(2,1)}, bf16[16,8,4,384]{3,2,1,0:T(4,128)(2,1)}, u32[]{:S(2)}, u32[]{:S(2)}) collective-permute-start(bf16[16,8,4,384]{3,2,1,0:T(4,128)(2,1)} %get-tuple-element.22), channel_id=1, source_target_pairs={{0,2},{2,0},{1,3},{3,1},{4,6},{6,4},{5,7},{7,5},{8,10},{10,8},{9,1... | collective-permute-start | bytes 1179656 | tf_op jit(solution)/shard_map/ppermute | solution.py:385
  93.3 0.0 collective-permute-done.4.rest_4_
  93.3 0.0 collective-permute-done.5.rest_5_
  93.3 12.9 %video.3 = (bf16[16,8,4,1536]{3,2,1,0:T(4,128)(2,1)}, bf16[16,8,4,384]{3,2,1,0:T(4,128)(2,1)}) custom-call(s32[6]{0:T(128)} %stack.43.scal, s32[1,256]{1,0:T(1,128)} %bitcast.9, bf16[16,8,4,1536]{3,2,1,0:T(4,128)(2,1)} %own_q.3, bf16[16,8,4,768]{3,2,1,0:T(4,128)(2,1)} %collective-permute-done.pair_q, ...), custom_call_target="tpu_custom_call", output_to_operand_aliasing={{0}: (12, {})} | custom-call | bytes 1 | tf_op jit(solution)/shard_map/video/pallas_call | solution.py:188
  106.2 0.1 collective-permute-start.10
  106.3 0.0 collective-permute-done.13
  106.3 1.1 broadcast_select_fusion
  107.3 0.5 collective-permute-start.14
  107.9 0.0 collective-permute-done.9
  107.9 1.9 %constant_dynamic-update-slice_fusion.1 = bf16[16,8,4,1536]{3,2,1,0:T(4,128)(2,1)} fusion(bf16[16,8,4,1536]{3,2,1,0:T(4,128)(2,1)} %get-tuple-element.21, bf16[16,8,4,384]{3,2,1,0:T(4,128)(2,1)} %collective-permute-done.9, s32[]{:T(128)S(6)} %select_n.24), kind=kLoop, calls=%fused_computation.5 | loop fusion | bytes 786436 | tf_op jit(solution)/shard_map/dynamic_update_slice | solution.py:413
  109.8 0.0 collective-permute-done.10
  109.8 0.9 constant_dynamic-update-slice_fusion
  110.7 0.0 collective-permute-done.14
  110.7 0.1 broadcast_select_fusion.2
  110.7 0.9 pad_maximum_fusion
Async XLA Ops:
  4.6 37.5 %collective-permute-start.1 = (bf16[2,6,4,2,64,128]{5,4,3,2,1,0:T(8,128)(2,1)}, bf16[2,6,4,2,64,128]{5,4,3,2,1,0:T(8,128)(2,1)}, u32[]{:S(2)}, u32[]{:S(2)}) collective-permute-start(bf16[2,6,4,2,64,128]{5,4,3,2,1,0:T(8,128)(2,1)} %pack.2.rest_0_.mine_ref), channel_id=1, source_target_pairs={{0,4},{4,8},{8,12},{1,5},{5,9},{9,13},{2,6},{6,10},{10,14},{3,7},{... | collective-permute-start | bytes 4718600 | tf_op jit(solution)/shard_map/ppermute | solution.py:396
  7.8 37.2 %collective-permute-start.2 = (bf16[2,6,4,2,64,128]{5,4,3,2,1,0:T(8,128)(2,1)}, bf16[2,6,4,2,64,128]{5,4,3,2,1,0:T(8,128)(2,1)}, u32[]{:S(2)}, u32[]{:S(2)}) collective-permute-start(bf16[2,6,4,2,64,128]{5,4,3,2,1,0:T(8,128)(2,1)} %pack.2.rest_0_.mine_ref), channel_id=1, source_target_pairs={{4,0},{8,4},{12,8},{5,1},{9,5},{13,9},{6,2},{10,6},{14,10},{7,3},{... | collective-permute-start | bytes 4718600 | tf_op jit(solution)/shard_map/ppermute | solution.py:396
  13.5 3.5 %collective-permute-start = (bf16[16,8,4,768]{3,2,1,0:T(4,128)(2,1)}, bf16[16,8,4,768]{3,2,1,0:T(4,128)(2,1)}, u32[]{:S(2)}, u32[]{:S(2)}) collective-permute-start(bf16[16,8,4,768]{3,2,1,0:T(4,128)(2,1)} %get-tuple-element.17), channel_id=1, source_target_pairs={{0,2},{2,0},{1,3},{3,1},{4,6},{6,4},{5,7},{7,5},{8,10},{10,8},{9,1... | collective-permute-start | bytes 2359304 | tf_op jit(solution)/shard_map/ppermute | solution.py:385
  14.8 3.4 %collective-permute-start.3 = (bf16[2,3,4,2,64,128]{5,4,3,2,1,0:T(8,128)(2,1)}, bf16[2,3,4,2,64,128]{5,4,3,2,1,0:T(8,128)(2,1)}, u32[]{:S(2)}, u32[]{:S(2)}) collective-permute-start(bf16[2,3,4,2,64,128]{5,4,3,2,1,0:T(8,128)(2,1)} %get-tuple-element.18), channel_id=1, source_target_pairs={{0,2},{2,0},{1,3},{3,1},{4,6},{6,4},{5,7},{7,5},{8,10},{10,8},{9,1... | collective-permute-start | bytes 2359304 | tf_op jit(solution)/shard_map/ppermute | solution.py:385
  14.8 4.5 %collective-permute-start.6 = (bf16[2,3,4,2,64,128]{5,4,3,2,1,0:T(8,128)(2,1)}, bf16[2,3,4,2,64,128]{5,4,3,2,1,0:T(8,128)(2,1)}, u32[]{:S(2)}, u32[]{:S(2)}) collective-permute-start(bf16[2,3,4,2,64,128]{5,4,3,2,1,0:T(8,128)(2,1)} %get-tuple-element.19), channel_id=1, source_target_pairs={{0,2},{2,0},{1,3},{3,1},{4,6},{6,4},{5,7},{7,5},{8,10},{10,8},{9,1... | collective-permute-start | bytes 2359304 | tf_op jit(solution)/shard_map/ppermute | solution.py:385
  27.7 27.0 %collective-permute-start.11 = (bf16[7,256,128]{2,1,0:T(8,128)(2,1)}, bf16[7,256,128]{2,1,0:T(8,128)(2,1)}, u32[]{:S(2)}, u32[]{:S(2)}) collective-permute-start(bf16[7,256,128]{2,1,0:T(8,128)(2,1)} %get-tuple-element.29), channel_id=1, source_target_pairs={{0,4},{12,8},{1,5},{13,9},{2,6},{14,10},{3,7},{15,11},{16,20},{28,... | collective-permute-start | bytes 1376264 | tf_op jit(solution)/shard_map/ppermute | solution.py:407
  29.0 35.8 %collective-permute-start.7 = (bf16[2,3,4,2,64,128]{5,4,3,2,1,0:T(8,128)(2,1)}, bf16[2,3,4,2,64,128]{5,4,3,2,1,0:T(8,128)(2,1)}, u32[]{:S(2)}, u32[]{:S(2)}) collective-permute-start(bf16[2,3,4,2,64,128]{5,4,3,2,1,0:T(8,128)(2,1)} %collective-permute-done.6.rest_3_.rest_0_), channel_id=1, source_target_pairs={{0,4},{4,8},{8,12},{1,5},{5,9},{9,13},{2,6},{6,10},{10,14},{3,7},{... | collective-permute-start | bytes 2359304 | tf_op jit(solution)/shard_map/ppermute | solution.py:396
  34.1 37.5 %collective-permute-start.8 = (bf16[2,3,4,2,64,128]{5,4,3,2,1,0:T(8,128)(2,1)}, bf16[2,3,4,2,64,128]{5,4,3,2,1,0:T(8,128)(2,1)}, u32[]{:S(2)}, u32[]{:S(2)}) collective-permute-start(bf16[2,3,4,2,64,128]{5,4,3,2,1,0:T(8,128)(2,1)} %collective-permute-done.6.rest_3_.rest_0_), channel_id=1, source_target_pairs={{4,0},{8,4},{12,8},{5,1},{9,5},{13,9},{6,2},{10,6},{14,10},{7,3},{... | collective-permute-start | bytes 2359304 | tf_op jit(solution)/shard_map/ppermute | solution.py:396
  57.6 26.9 %collective-permute-start.12 = (bf16[7,256,128]{2,1,0:T(8,128)(2,1)}, bf16[7,256,128]{2,1,0:T(8,128)(2,1)}, u32[]{:S(2)}, u32[]{:S(2)}) collective-permute-start(bf16[7,256,128]{2,1,0:T(8,128)(2,1)} %join.1.own_ref), channel_id=1, source_target_pairs={{4,8},{8,4},{5,9},{9,5},{6,10},{10,6},{7,11},{11,7},{20,24},{24,20... | collective-permute-start | bytes 1376264 | tf_op jit(solution)/shard_map/ppermute | solution.py:409
  59.5 33.8 %collective-permute-start.4 = (bf16[2,3,4,2,64,128]{5,4,3,2,1,0:T(8,128)(2,1)}, bf16[2,3,4,2,64,128]{5,4,3,2,1,0:T(8,128)(2,1)}, u32[]{:S(2)}, u32[]{:S(2)}) collective-permute-start(bf16[2,3,4,2,64,128]{5,4,3,2,1,0:T(8,128)(2,1)} %collective-permute-done.3.rest_3_.rest_1_), channel_id=1, source_target_pairs={{0,4},{4,8},{8,12},{1,5},{5,9},{9,13},{2,6},{6,10},{10,14},{3,7},{... | collective-permute-start | bytes 2359304 | tf_op jit(solution)/shard_map/ppermute | solution.py:396
  61.4 31.9 %collective-permute-start.5 = (bf16[2,3,4,2,64,128]{5,4,3,2,1,0:T(8,128)(2,1)}, bf16[2,3,4,2,64,128]{5,4,3,2,1,0:T(8,128)(2,1)}, u32[]{:S(2)}, u32[]{:S(2)}) collective-permute-start(bf16[2,3,4,2,64,128]{5,4,3,2,1,0:T(8,128)(2,1)} %collective-permute-done.3.rest_3_.rest_1_), channel_id=1, source_target_pairs={{4,0},{8,4},{12,8},{5,1},{9,5},{13,9},{6,2},{10,6},{14,10},{7,3},{... | collective-permute-start | bytes 2359304 | tf_op jit(solution)/shard_map/ppermute | solution.py:396
  87.8 18.5 %collective-permute-start.13 = (bf16[256,768]{1,0:T(8,128)(2,1)}, bf16[256,768]{1,0:T(8,128)(2,1)}, u32[]{:S(2)}, u32[]{:S(2)}) collective-permute-start(bf16[256,768]{1,0:T(8,128)(2,1)} %finish.1), channel_id=1, source_target_pairs={{4,0},{8,12},{5,1},{9,13},{6,2},{10,14},{7,3},{11,15},{20,16},{24,... | collective-permute-start | bytes 1179656 | tf_op jit(solution)/shard_map/ppermute | solution.py:432
  89.8 18.1 %collective-permute-start.9 = (bf16[16,8,4,384]{3,2,1,0:T(4,128)(2,1)}, bf16[16,8,4,384]{3,2,1,0:T(4,128)(2,1)}, u32[]{:S(2)}, u32[]{:S(2)}) collective-permute-start(bf16[16,8,4,384]{3,2,1,0:T(4,128)(2,1)} %get-tuple-element.22), channel_id=1, source_target_pairs={{0,2},{2,0},{1,3},{3,1},{4,6},{6,4},{5,7},{7,5},{8,10},{10,8},{9,1... | collective-permute-start | bytes 1179656 | tf_op jit(solution)/shard_map/ppermute | solution.py:385
  106.2 3.6 %collective-permute-start.10 = (bf16[16,8,4,384]{3,2,1,0:T(4,128)(2,1)}, bf16[16,8,4,384]{3,2,1,0:T(4,128)(2,1)S(1)}, u32[]{:S(2)}, u32[]{:S(2)}) collective-permute-start(bf16[16,8,4,384]{3,2,1,0:T(4,128)(2,1)} %get-tuple-element.23), channel_id=1, source_target_pairs={{0,2},{2,0},{1,3},{3,1},{4,6},{6,4},{5,7},{7,5},{8,10},{10,8},{9,1... | collective-permute-start | bytes 1179656 | tf_op jit(solution)/shard_map/ppermute | solution.py:385
  107.3 3.3 %collective-permute-start.14 = (bf16[256,768]{1,0:T(8,128)(2,1)S(1)}, bf16[256,768]{1,0:T(8,128)(2,1)S(1)}, u32[]{:S(2)}, u32[]{:S(2)}) collective-permute-start(bf16[256,768]{1,0:T(8,128)(2,1)S(1)} %broadcast_select_fusion), channel_id=1, source_target_pairs={{0,2},{2,0},{1,3},{3,1},{4,6},{6,4},{5,7},{7,5},{8,10},{10,8},{9,1... | collective-permute-start | bytes 1179656 | tf_op jit(solution)/shard_map/ppermute | solution.py:385

commit v4 on v3

--- a/solution.py
+++ b/solution.py
@@ -173,7 +173,6 @@
     block = (frames, rows, cols, HD)
     own_head = pl.BlockSpec(block, lambda i, s: (0, 0, 0, s[4] * half_heads + start + i))
     pair_head = pl.BlockSpec(block, lambda i, s: (0, 0, 0, start + i))
-    given = pl.BlockSpec(block, lambda i, s: (0, 0, 0, i))
     of_half = pl.BlockSpec((2, 1, time_tiles, 2, VOL, HD), lambda i, s: (0, start + i, 0, 0, 0, 0))
     of_group = pl.BlockSpec((2, 1, time_tiles, 2, VOL, HD), lambda i, s: (0, i, 0, 0, 0, 0))
     word = pl.BlockSpec((text, HD), lambda i, s: (0, s[4] * half_heads + start + i))
@@ -181,21 +180,21 @@
     specs += [of_half] * 3 + [of_group] * 3 + [word, word]
     operands = [scal, valid, query_video, pair_query, *mine, *pair, key_text, value_text]
     aliases = {}
-    if prior is not None:
+    for at, array in enumerate(prior):
         specs.append(pl.BlockSpec(memory_space=pl.ANY))
-        aliases = {len(operands): 0}
-        operands.append(prior)
+        aliases[len(operands)] = at
+        operands.append(array)
     return pl.pallas_call(
         video_body,
         grid_spec=pltpu.PrefetchScalarGridSpec(
             num_scalar_prefetch=1,
             grid=(count,),
             in_specs=specs,
-            out_specs=[own_head, given],
+            out_specs=[own_head, pair_head],
         ),
         out_shape=[
             jax.ShapeDtypeStruct(query_video.shape, BF16),
-            jax.ShapeDtypeStruct((frames, rows, cols, count * HD), BF16),
+            jax.ShapeDtypeStruct(pair_query.shape, BF16),
         ],
         input_output_aliases=aliases,
         compiler_params=pltpu.CompilerParams(vmem_limit_bytes=VMEM),
@@ -408,29 +407,21 @@
         sent = join(sums, after(logs, *mine_sides), got)
     got = lax.ppermute(sent, "tm", [(middle - 1, middle), (middle, middle - 1)])
 
-    def place(whole, part, start):
-        column = ((1 - half) * half_heads + start) * HD
-        return lax.dynamic_update_slice_in_dim(whole, part, column, 3)
-
-    out_video = None
-    waiting = []
+    outs = ()
     for index, (start, count) in enumerate(groups):
-        pair = (pairs[index], *to_neighbours(pairs[index]))
-        out_video, given = video_group(
-            scal, valid, query_video, pair_query, (mine, *mine_sides), pair, key_text, value_text, out_video, start, count
+        pair = (pairs[index], *to_neighbours(after(pairs[index], sent) if index else pairs[index]))
+        outs = video_group(
+            scal, valid, query_video, pair_query, (mine, *mine_sides), pair, key_text, value_text, outs, start, count
         )
         if index == 0:
-            opened = after(scal, out_video)
-        for part in waiting:
-            out_video = place(out_video, *part)
-        waiting = [(swap(given), start)]
-    for part in waiting:
-        out_video = place(out_video, *part)
+            opened = after(scal, outs[0])
+    column = (1 - half) * half_heads * HD
+    out_video = lax.dynamic_update_slice_in_dim(outs[0], swap(outs[1]), column, 3)
 
     done = finish(opened, sent, got)
     for step in range(middle - 1, 0, -1):
         got = lax.ppermute(done, "tm", [(step, step - 1), (strips - step - 1, strips - step)])
-        done = jnp.where((strip == step - 1) | (strip == strips - step), got, done)
+        done = jnp.where((strip == step - 1) | (strip == strips - step), after(got, outs[1]), done)
     other = swap(done)
     first = half == 0
     out_text = jnp.concatenate([jnp.where(first, done, other), jnp.where(first, other, done)], axis=1)

time: 112 us -> 112 us (level)
  waiting for transfers between devices: 29.5 us -> 31.2 us
  local copies, waits for them, and re-layouts: 3.38 us -> 2.18 us
    dynamic_update_slice x2 -> x1, local copies, waits for them, and re-layouts: 2.76 us -> 0.41 us  [shards(): lax.dynamic_update_slice_in_dim(outs[0], swap(outs[1]), column, 3)]
    ppermute x6 -> x5, waiting for transfers between devices: 4 us -> 5.6 us  [swap(): return lax.ppermute(array, 'height', [(0, 1), (1, 0)])]
    unnamed x0 -> x4, local copies, waits for them, and re-layouts: none -> 1.14 us
    ppermute x6 -> x5, starting transfers between devices: 5.84 us -> 5.34 us  [swap(): return lax.ppermute(array, 'height', [(0, 1), (1, 0)])]
  transfers between devices with their start and end apart: 15 -> 14, of which waited for: 7 -> 9; matrix products, arithmetic and copies ran while one was open for 3% -> 1% of each run, Pallas kernels for 39% -> 39%
where the time goes in v4:
time: 112 us
  Pallas kernels  47.2 us (42%)
  waiting for transfers between devices  31.2 us (28%)
  starting transfers between devices  28.2 us (25%)
  local copies, waits for them, and re-layouts  2.18 us (2%)
  other arithmetic  2.04 us (2%)
    pallas_call x2, Pallas kernels, video_group(): pl.pallas_call(video_body, grid_spec=pltpu.PrefetchScalarGridSpec(num_sca...  25.7 us
    ppermute x6, starting transfers between devices, to_neighbours(): return (lax.ppermute(array, 'tm', up), lax.ppermute(array, 'tm', down))  17.6 us
    ppermute x6, waiting for transfers between devices, to_neighbours(): return (lax.ppermute(array, 'tm', up), lax.ppermute(array, 'tm', down))  15.8 us
    ppermute x1, waiting for transfers between devices, shards(): lax.ppermute(sent, 'tm', [(step - 1, step), (strips - step, strips - step...  9.83 us
    pallas_call x1, Pallas kernels, text_partial(): pl.pallas_call(functools.partial(text_body, groups), grid_spec=pltpu.Pref...  8.45 us
    pallas_call x2, Pallas kernels, pack_half(): pl.pallas_call(functools.partial(pack_body, sizes), grid_spec=pltpu.Prefe...  6.96 us
    ppermute x5, waiting for transfers between devices, swap(): return lax.ppermute(array, 'height', [(0, 1), (1, 0)])  5.6 us
    ppermute x5, starting transfers between devices, swap(): return lax.ppermute(array, 'height', [(0, 1), (1, 0)])  5.34 us
  transfers between devices with their start and end apart: 14, of which 9 were waited for; matrix products, arithmetic and copies ran while one was open for 1% of the time, Pallas kernels for 39%

profile of v4, /device:TPU:21, one launch (start us, length us, event | category | flops | bytes accessed | tf_op | source)
XLA Modules:
  0.0 111.6 jit_solution(5105728259491945353)
XLA Ops:
  0.6 0.6 stack.43.scal
  1.3 3.3 %pack.2.mine_ref.rest_0_ = bf16[2,6,4,2,64,128]{5,4,3,2,1,0:T(8,128)(2,1)} custom-call(s32[6]{0:T(128)} %stack.43.scal, bf16[16,8,4,1536]{3,2,1,0:T(4,128)(2,1)} %rest_0_.3, bf16[16,8,4,1536]{3,2,1,0:T(4,128)(2,1)} %rest_1_.3), custom_call_target="tpu_custom_call" | custom-call | bytes 1 | tf_op jit(solution)/shard_map/pack/pallas_call | solution.py:81
  4.6 3.2 %collective-permute-start.1 = (bf16[2,6,4,2,64,128]{5,4,3,2,1,0:T(8,128)(2,1)}, bf16[2,6,4,2,64,128]{5,4,3,2,1,0:T(8,128)(2,1)}, u32[]{:S(2)}, u32[]{:S(2)}) collective-permute-start(bf16[2,6,4,2,64,128]{5,4,3,2,1,0:T(8,128)(2,1)} %pack.2.mine_ref.rest_0_), channel_id=1, source_target_pairs={{0,4},{4,8},{8,12},{1,5},{5,9},{9,13},{2,6},{6,10},{10,14},{3,7},{... | collective-permute-start | bytes 4718600 | tf_op jit(solution)/shard_map/ppermute | solution.py:395
  7.8 2.1 %collective-permute-start.2 = (bf16[2,6,4,2,64,128]{5,4,3,2,1,0:T(8,128)(2,1)}, bf16[2,6,4,2,64,128]{5,4,3,2,1,0:T(8,128)(2,1)}, u32[]{:S(2)}, u32[]{:S(2)}) collective-permute-start(bf16[2,6,4,2,64,128]{5,4,3,2,1,0:T(8,128)(2,1)} %pack.2.mine_ref.rest_0_), channel_id=1, source_target_pairs={{4,0},{8,4},{12,8},{5,1},{9,5},{13,9},{6,2},{10,6},{14,10},{7,3},{... | collective-permute-start | bytes 4718600 | tf_op jit(solution)/shard_map/ppermute | solution.py:395
  9.9 3.6 %pack.3 = (bf16[2,3,4,2,64,128]{5,4,3,2,1,0:T(8,128)(2,1)}, bf16[2,3,4,2,64,128]{5,4,3,2,1,0:T(8,128)(2,1)}, bf16[16,8,4,768]{3,2,1,0:T(4,128)(2,1)}) custom-call(s32[6]{0:T(128)} %stack.43.scal, bf16[16,8,4,1536]{3,2,1,0:T(4,128)(2,1)} %rest_0_.3, bf16[16,8,4,1536]{3,2,1,0:T(4,128)(2,1)} %rest_1_.3, bf16[16,8,4,1536]{3,2,1,0:T(4,128)(2,1)} %own_q.3), custom_call_target="tpu_custom_call" | custom-call | bytes 1 | tf_op jit(solution)/shard_map/pack/pallas_call | solution.py:81
  13.5 1.2 %collective-permute-start = (bf16[16,8,4,768]{3,2,1,0:T(4,128)(2,1)}, bf16[16,8,4,768]{3,2,1,0:T(4,128)(2,1)}, u32[]{:S(2)}, u32[]{:S(2)}) collective-permute-start(bf16[16,8,4,768]{3,2,1,0:T(4,128)(2,1)} %get-tuple-element.19), channel_id=1, source_target_pairs={{0,2},{2,0},{1,3},{3,1},{4,6},{6,4},{5,7},{7,5},{8,10},{10,8},{9,1... | collective-permute-start | bytes 2359304 | tf_op jit(solution)/shard_map/ppermute | solution.py:384
  14.8 0.0 collective-permute-start.4
  14.8 0.5 collective-permute-start.3
  15.3 1.7 %collective-permute-done.pair_q = bf16[16,8,4,768]{3,2,1,0:T(4,128)(2,1)} collective-permute-done((bf16[16,8,4,768]{3,2,1,0:T(4,128)(2,1)}, bf16[16,8,4,768]{3,2,1,0:T(4,128)(2,1)}, u32[]{:S(2)}, u32[]{:S(2)}) %collective-permute-start) | collective-permute-done | bytes 786464 | tf_op jit(solution)/shard_map/ppermute | solution.py:384
  17.0 1.1 %collective-permute-done.4.rest_0_.rest_3_ = bf16[2,3,4,2,64,128]{5,4,3,2,1,0:T(8,128)(2,1)} collective-permute-done((bf16[2,3,4,2,64,128]{5,4,3,2,1,0:T(8,128)(2,1)}, bf16[2,3,4,2,64,128]{5,4,3,2,1,0:T(8,128)(2,1)}, u32[]{:S(2)}, u32[]{:S(2)}) %collective-permute-start.4) | collective-permute-done | bytes 786464 | tf_op jit(solution)/shard_map/ppermute | solution.py:384
  18.1 1.1 %collective-permute-done.3.rest_1_.rest_3_ = bf16[2,3,4,2,64,128]{5,4,3,2,1,0:T(8,128)(2,1)} collective-permute-done((bf16[2,3,4,2,64,128]{5,4,3,2,1,0:T(8,128)(2,1)}, bf16[2,3,4,2,64,128]{5,4,3,2,1,0:T(8,128)(2,1)}, u32[]{:S(2)}, u32[]{:S(2)}) %collective-permute-start.3) | collective-permute-done | bytes 786464 | tf_op jit(solution)/shard_map/ppermute | solution.py:384
  19.3 8.5 %text.1 = (f32[6,256,128]{2,1,0:T(8,128)}, f32[256,128]{1,0:T(8,128)}, bf16[7,256,128]{2,1,0:T(8,128)(2,1)}) custom-call(s32[6]{0:T(128)} %stack.43.scal, s32[1,256]{1,0:T(1,128)} %bitcast.7, bf16[256,1536]{1,0:T(8,128)(2,1)} %q_ref.1, bf16[2,6,4,2,64,128]{5,4,3,2,1,0:T(8,128)(2,1)} %pack.2.mine_ref.rest_0_, bf16[256,1536]{1,0:T(8,128)(2,1)} %rest_6_.3, ...), custom_call_target="tpu_custom_call" | custom-call | bytes 1 | tf_op jit(solution)/shard_map/text/pallas_call | solution.py:282
  27.7 1.3 %collective-permute-start.5 = (bf16[7,256,128]{2,1,0:T(8,128)(2,1)}, bf16[7,256,128]{2,1,0:T(8,128)(2,1)}, u32[]{:S(2)}, u32[]{:S(2)}) collective-permute-start(bf16[7,256,128]{2,1,0:T(8,128)(2,1)} %get-tuple-element.26), channel_id=1, source_target_pairs={{0,4},{12,8},{1,5},{13,9},{2,6},{14,10},{3,7},{15,11},{16,20},{28,... | collective-permute-start | bytes 1376264 | tf_op jit(solution)/shard_map/ppermute | solution.py:406
  29.0 5.1 %collective-permute-start.8 = (bf16[2,3,4,2,64,128]{5,4,3,2,1,0:T(8,128)(2,1)}, bf16[2,3,4,2,64,128]{5,4,3,2,1,0:T(8,128)(2,1)}, u32[]{:S(2)}, u32[]{:S(2)}) collective-permute-start(bf16[2,3,4,2,64,128]{5,4,3,2,1,0:T(8,128)(2,1)} %collective-permute-done.4.rest_0_.rest_3_), channel_id=1, source_target_pairs={{0,4},{4,8},{8,12},{1,5},{5,9},{9,13},{2,6},{6,10},{10,14},{3,7},{... | collective-permute-start | bytes 2359304 | tf_op jit(solution)/shard_map/ppermute | solution.py:395
  34.1 1.9 %collective-permute-start.9 = (bf16[2,3,4,2,64,128]{5,4,3,2,1,0:T(8,128)(2,1)}, bf16[2,3,4,2,64,128]{5,4,3,2,1,0:T(8,128)(2,1)}, u32[]{:S(2)}, u32[]{:S(2)}) collective-permute-start(bf16[2,3,4,2,64,128]{5,4,3,2,1,0:T(8,128)(2,1)} %collective-permute-done.4.rest_0_.rest_3_), channel_id=1, source_target_pairs={{4,0},{8,4},{12,8},{5,1},{9,5},{13,9},{6,2},{10,6},{14,10},{7,3},{... | collective-permute-start | bytes 2359304 | tf_op jit(solution)/shard_map/ppermute | solution.py:395
  36.1 6.0 %collective-permute-done.1.rest_1_ = bf16[2,6,4,2,64,128]{5,4,3,2,1,0:T(8,128)(2,1)} collective-permute-done((bf16[2,6,4,2,64,128]{5,4,3,2,1,0:T(8,128)(2,1)}, bf16[2,6,4,2,64,128]{5,4,3,2,1,0:T(8,128)(2,1)}, u32[]{:S(2)}, u32[]{:S(2)}) %collective-permute-start.1) | collective-permute-done | bytes 1572896 | tf_op jit(solution)/shard_map/ppermute | solution.py:395
  42.1 2.9 %collective-permute-done.2.rest_2_ = bf16[2,6,4,2,64,128]{5,4,3,2,1,0:T(8,128)(2,1)} collective-permute-done((bf16[2,6,4,2,64,128]{5,4,3,2,1,0:T(8,128)(2,1)}, bf16[2,6,4,2,64,128]{5,4,3,2,1,0:T(8,128)(2,1)}, u32[]{:S(2)}, u32[]{:S(2)}) %collective-permute-start.2) | collective-permute-done | bytes 1572896 | tf_op jit(solution)/shard_map/ppermute | solution.py:395
  45.0 9.8 %collective-permute-done.5.got_ref = bf16[7,256,128]{2,1,0:T(8,128)(2,1)} collective-permute-done((bf16[7,256,128]{2,1,0:T(8,128)(2,1)}, bf16[7,256,128]{2,1,0:T(8,128)(2,1)}, u32[]{:S(2)}, u32[]{:S(2)}) %collective-permute-start.5) | collective-permute-done | bytes 458784 | tf_op jit(solution)/shard_map/ppermute | solution.py:406
  54.8 2.8 %join.1.own_ref = bf16[7,256,128]{2,1,0:T(8,128)(2,1)} custom-call(f32[6,256,128]{2,1,0:T(8,128)} %get-tuple-element.23.sum_ref, f32[256,128]{1,0:T(8,128)} %get-tuple-element.25.log_ref, bf16[7,256,128]{2,1,0:T(8,128)(2,1)} %collective-permute-done.5.got_ref), custom_call_target="tpu_custom_call" | custom-call | bytes 1 | tf_op jit(solution)/shard_map/join/pallas_call | solution.py:330
  57.6 1.9 %collective-permute-start.11 = (bf16[7,256,128]{2,1,0:T(8,128)(2,1)}, bf16[7,256,128]{2,1,0:T(8,128)(2,1)}, u32[]{:S(2)}, u32[]{:S(2)}) collective-permute-start(bf16[7,256,128]{2,1,0:T(8,128)(2,1)} %join.1.own_ref), channel_id=1, source_target_pairs={{4,8},{8,4},{5,9},{9,5},{6,10},{10,6},{7,11},{11,7},{20,24},{24,20... | collective-permute-start | bytes 1376264 | tf_op jit(solution)/shard_map/ppermute | solution.py:408
  59.5 1.9 %collective-permute-start.6 = (bf16[2,3,4,2,64,128]{5,4,3,2,1,0:T(8,128)(2,1)}, bf16[2,3,4,2,64,128]{5,4,3,2,1,0:T(8,128)(2,1)}, u32[]{:S(2)}, u32[]{:S(2)}) collective-permute-start(bf16[2,3,4,2,64,128]{5,4,3,2,1,0:T(8,128)(2,1)} %collective-permute-done.3.rest_1_.rest_3_), channel_id=1, source_target_pairs={{0,4},{4,8},{8,12},{1,5},{5,9},{9,13},{2,6},{6,10},{10,14},{3,7},{... | collective-permute-start | bytes 2359304 | tf_op jit(solution)/shard_map/ppermute | solution.py:395
  61.4 3.4 %collective-permute-start.7 = (bf16[2,3,4,2,64,128]{5,4,3,2,1,0:T(8,128)(2,1)}, bf16[2,3,4,2,64,128]{5,4,3,2,1,0:T(8,128)(2,1)}, u32[]{:S(2)}, u32[]{:S(2)}) collective-permute-start(bf16[2,3,4,2,64,128]{5,4,3,2,1,0:T(8,128)(2,1)} %collective-permute-done.3.rest_1_.rest_3_), channel_id=1, source_target_pairs={{4,0},{8,4},{12,8},{5,1},{9,5},{13,9},{6,2},{10,6},{14,10},{7,3},{... | collective-permute-start | bytes 2359304 | tf_op jit(solution)/shard_map/ppermute | solution.py:395
  64.8 0.0 collective-permute-done.8.rest_4_
  64.8 6.9 %collective-permute-done.9.rest_5_ = bf16[2,3,4,2,64,128]{5,4,3,2,1,0:T(8,128)(2,1)} collective-permute-done((bf16[2,3,4,2,64,128]{5,4,3,2,1,0:T(8,128)(2,1)}, bf16[2,3,4,2,64,128]{5,4,3,2,1,0:T(8,128)(2,1)}, u32[]{:S(2)}, u32[]{:S(2)}) %collective-permute-start.9) | collective-permute-done | bytes 786464 | tf_op jit(solution)/shard_map/ppermute | solution.py:395
  71.6 12.8 %video.2 = (bf16[16,8,4,1536]{3,2,1,0:T(4,128)(2,1)}, bf16[16,8,4,768]{3,2,1,0:T(4,128)(2,1)}) custom-call(s32[6]{0:T(128)} %stack.43.scal, s32[1,256]{1,0:T(1,128)} %bitcast.8, bf16[16,8,4,1536]{3,2,1,0:T(4,128)(2,1)} %own_q.3, bf16[16,8,4,768]{3,2,1,0:T(4,128)(2,1)} %collective-permute-done.pair_q, bf16[2,6,4,2,64,128]{5,4,3,2,1,0:T(8,128)(2,1)} %pack.2.mine_ref.rest_0_, ...), custom_call_target="tpu_custom_call" | custom-call | bytes 1 | tf_op jit(solution)/shard_map/video/pallas_call | solution.py:187
  84.5 0.0 collective-permute-done.11.got_ref
  84.5 3.3 %finish.1 = bf16[256,768]{1,0:T(8,128)(2,1)} custom-call(s32[6]{0:T(128)} %stack.43.scal, bf16[7,256,128]{2,1,0:T(8,128)(2,1)} %join.1.own_ref, bf16[7,256,128]{2,1,0:T(8,128)(2,1)} %collective-permute-done.11.got_ref), custom_call_target="tpu_custom_call" | custom-call | bytes 1 | tf_op jit(solution)/shard_map/finish/pallas_call | solution.py:356
  87.8 2.0 %collective-permute-start.12 = (bf16[256,768]{1,0:T(8,128)(2,1)}, bf16[256,768]{1,0:T(8,128)(2,1)}, u32[]{:S(2)}, u32[]{:S(2)}) collective-permute-start(bf16[256,768]{1,0:T(8,128)(2,1)} %finish.1), channel_id=1, source_target_pairs={{4,0},{8,12},{5,1},{9,13},{6,2},{10,14},{7,3},{11,15},{20,16},{24,... | collective-permute-start | bytes 1179656 | tf_op jit(solution)/shard_map/ppermute | solution.py:423
  89.8 0.0 collective-permute-done.6.rest_4_
  89.8 0.0 collective-permute-done.7.rest_5_
  89.8 12.9 %video.3 = (bf16[16,8,4,1536]{3,2,1,0:T(4,128)(2,1)}, bf16[16,8,4,768]{3,2,1,0:T(4,128)(2,1)}) custom-call(s32[6]{0:T(128)} %stack.43.scal, s32[1,256]{1,0:T(1,128)} %bitcast.9, bf16[16,8,4,1536]{3,2,1,0:T(4,128)(2,1)} %own_q.3, bf16[16,8,4,768]{3,2,1,0:T(4,128)(2,1)} %collective-permute-done.pair_q, ...), custom_call_target="tpu_custom_call", output_to_operand_aliasing={{0}: (12, {}), {1}: (13, {})} | custom-call | bytes 1 | tf_op jit(solution)/shard_map/video/pallas_call | solution.py:187
  102.7 0.0 collective-permute-done.12
  102.7 1.1 broadcast_select_fusion
  103.8 3.5 %collective-permute-start.13 = (bf16[256,768]{1,0:T(8,128)(2,1)S(1)}, bf16[256,768]{1,0:T(8,128)(2,1)S(1)}, u32[]{:S(2)}, u32[]{:S(2)}) collective-permute-start(bf16[256,768]{1,0:T(8,128)(2,1)S(1)} %broadcast_select_fusion), channel_id=1, source_target_pairs={{0,2},{2,0},{1,3},{3,1},{4,6},{6,4},{5,7},{7,5},{8,10},{10,8},{9,1... | collective-permute-start | bytes 1179656 | tf_op jit(solution)/shard_map/ppermute | solution.py:384
  107.3 0.1 collective-permute-start.10
  107.4 0.0 copy-start
  107.4 1.3 %collective-permute-done.13 = bf16[256,768]{1,0:T(8,128)(2,1)S(1)} collective-permute-done((bf16[256,768]{1,0:T(8,128)(2,1)S(1)}, bf16[256,768]{1,0:T(8,128)(2,1)S(1)}, u32[]{:S(2)}, u32[]{:S(2)}) %collective-permute-start.13) | collective-permute-done | bytes 393248 | tf_op jit(solution)/shard_map/ppermute | solution.py:384
  108.7 0.1 broadcast_select_fusion.2
  108.7 0.9 pad_maximum_fusion
  109.6 0.3 collective-permute-done.10
  110.0 0.0 copy-done
  110.0 0.4 constant_dynamic-update-slice_fusion
  110.4 0.0 copy-start.1
  110.4 1.1 %copy-done.1 = bf16[16,8,4,1536]{3,2,1,0:T(4,128)(2,1)} copy-done((bf16[16,8,4,1536]{3,2,1,0:T(4,128)(2,1)}, bf16[16,8,4,1536]{3,2,1,0:T(4,128)(2,1)S(1)}, u32[]{:S(2)}) %copy-start.1) | copy-done | bytes 1572888
Async XLA Ops:
  4.6 37.5 %collective-permute-start.1 = (bf16[2,6,4,2,64,128]{5,4,3,2,1,0:T(8,128)(2,1)}, bf16[2,6,4,2,64,128]{5,4,3,2,1,0:T(8,128)(2,1)}, u32[]{:S(2)}, u32[]{:S(2)}) collective-permute-start(bf16[2,6,4,2,64,128]{5,4,3,2,1,0:T(8,128)(2,1)} %pack.2.mine_ref.rest_0_), channel_id=1, source_target_pairs={{0,4},{4,8},{8,12},{1,5},{5,9},{9,13},{2,6},{6,10},{10,14},{3,7},{... | collective-permute-start | bytes 4718600 | tf_op jit(solution)/shard_map/ppermute | solution.py:395
  7.8 37.2 %collective-permute-start.2 = (bf16[2,6,4,2,64,128]{5,4,3,2,1,0:T(8,128)(2,1)}, bf16[2,6,4,2,64,128]{5,4,3,2,1,0:T(8,128)(2,1)}, u32[]{:S(2)}, u32[]{:S(2)}) collective-permute-start(bf16[2,6,4,2,64,128]{5,4,3,2,1,0:T(8,128)(2,1)} %pack.2.mine_ref.rest_0_), channel_id=1, source_target_pairs={{4,0},{8,4},{12,8},{5,1},{9,5},{13,9},{6,2},{10,6},{14,10},{7,3},{... | collective-permute-start | bytes 4718600 | tf_op jit(solution)/shard_map/ppermute | solution.py:395
  13.5 3.5 %collective-permute-start = (bf16[16,8,4,768]{3,2,1,0:T(4,128)(2,1)}, bf16[16,8,4,768]{3,2,1,0:T(4,128)(2,1)}, u32[]{:S(2)}, u32[]{:S(2)}) collective-permute-start(bf16[16,8,4,768]{3,2,1,0:T(4,128)(2,1)} %get-tuple-element.19), channel_id=1, source_target_pairs={{0,2},{2,0},{1,3},{3,1},{4,6},{6,4},{5,7},{7,5},{8,10},{10,8},{9,1... | collective-permute-start | bytes 2359304 | tf_op jit(solution)/shard_map/ppermute | solution.py:384
  14.8 3.4 %collective-permute-start.4 = (bf16[2,3,4,2,64,128]{5,4,3,2,1,0:T(8,128)(2,1)}, bf16[2,3,4,2,64,128]{5,4,3,2,1,0:T(8,128)(2,1)}, u32[]{:S(2)}, u32[]{:S(2)}) collective-permute-start(bf16[2,3,4,2,64,128]{5,4,3,2,1,0:T(8,128)(2,1)} %get-tuple-element.22), channel_id=1, source_target_pairs={{0,2},{2,0},{1,3},{3,1},{4,6},{6,4},{5,7},{7,5},{8,10},{10,8},{9,1... | collective-permute-start | bytes 2359304 | tf_op jit(solution)/shard_map/ppermute | solution.py:384
  14.8 4.5 %collective-permute-start.3 = (bf16[2,3,4,2,64,128]{5,4,3,2,1,0:T(8,128)(2,1)}, bf16[2,3,4,2,64,128]{5,4,3,2,1,0:T(8,128)(2,1)}, u32[]{:S(2)}, u32[]{:S(2)}) collective-permute-start(bf16[2,3,4,2,64,128]{5,4,3,2,1,0:T(8,128)(2,1)} %get-tuple-element.20), channel_id=1, source_target_pairs={{0,2},{2,0},{1,3},{3,1},{4,6},{6,4},{5,7},{7,5},{8,10},{10,8},{9,1... | collective-permute-start | bytes 2359304 | tf_op jit(solution)/shard_map/ppermute | solution.py:384
  27.7 27.1 %collective-permute-start.5 = (bf16[7,256,128]{2,1,0:T(8,128)(2,1)}, bf16[7,256,128]{2,1,0:T(8,128)(2,1)}, u32[]{:S(2)}, u32[]{:S(2)}) collective-permute-start(bf16[7,256,128]{2,1,0:T(8,128)(2,1)} %get-tuple-element.26), channel_id=1, source_target_pairs={{0,4},{12,8},{1,5},{13,9},{2,6},{14,10},{3,7},{15,11},{16,20},{28,... | collective-permute-start | bytes 1376264 | tf_op jit(solution)/shard_map/ppermute | solution.py:406
  29.0 35.8 %collective-permute-start.8 = (bf16[2,3,4,2,64,128]{5,4,3,2,1,0:T(8,128)(2,1)}, bf16[2,3,4,2,64,128]{5,4,3,2,1,0:T(8,128)(2,1)}, u32[]{:S(2)}, u32[]{:S(2)}) collective-permute-start(bf16[2,3,4,2,64,128]{5,4,3,2,1,0:T(8,128)(2,1)} %collective-permute-done.4.rest_0_.rest_3_), channel_id=1, source_target_pairs={{0,4},{4,8},{8,12},{1,5},{5,9},{9,13},{2,6},{6,10},{10,14},{3,7},{... | collective-permute-start | bytes 2359304 | tf_op jit(solution)/shard_map/ppermute | solution.py:395
  34.1 37.5 %collective-permute-start.9 = (bf16[2,3,4,2,64,128]{5,4,3,2,1,0:T(8,128)(2,1)}, bf16[2,3,4,2,64,128]{5,4,3,2,1,0:T(8,128)(2,1)}, u32[]{:S(2)}, u32[]{:S(2)}) collective-permute-start(bf16[2,3,4,2,64,128]{5,4,3,2,1,0:T(8,128)(2,1)} %collective-permute-done.4.rest_0_.rest_3_), channel_id=1, source_target_pairs={{4,0},{8,4},{12,8},{5,1},{9,5},{13,9},{6,2},{10,6},{14,10},{7,3},{... | collective-permute-start | bytes 2359304 | tf_op jit(solution)/shard_map/ppermute | solution.py:395
  57.6 26.9 %collective-permute-start.11 = (bf16[7,256,128]{2,1,0:T(8,128)(2,1)}, bf16[7,256,128]{2,1,0:T(8,128)(2,1)}, u32[]{:S(2)}, u32[]{:S(2)}) collective-permute-start(bf16[7,256,128]{2,1,0:T(8,128)(2,1)} %join.1.own_ref), channel_id=1, source_target_pairs={{4,8},{8,4},{5,9},{9,5},{6,10},{10,6},{7,11},{11,7},{20,24},{24,20... | collective-permute-start | bytes 1376264 | tf_op jit(solution)/shard_map/ppermute | solution.py:408
  59.5 30.3 %collective-permute-start.6 = (bf16[2,3,4,2,64,128]{5,4,3,2,1,0:T(8,128)(2,1)}, bf16[2,3,4,2,64,128]{5,4,3,2,1,0:T(8,128)(2,1)}, u32[]{:S(2)}, u32[]{:S(2)}) collective-permute-start(bf16[2,3,4,2,64,128]{5,4,3,2,1,0:T(8,128)(2,1)} %collective-permute-done.3.rest_1_.rest_3_), channel_id=1, source_target_pairs={{0,4},{4,8},{8,12},{1,5},{5,9},{9,13},{2,6},{6,10},{10,14},{3,7},{... | collective-permute-start | bytes 2359304 | tf_op jit(solution)/shard_map/ppermute | solution.py:395
  61.4 28.4 %collective-permute-start.7 = (bf16[2,3,4,2,64,128]{5,4,3,2,1,0:T(8,128)(2,1)}, bf16[2,3,4,2,64,128]{5,4,3,2,1,0:T(8,128)(2,1)}, u32[]{:S(2)}, u32[]{:S(2)}) collective-permute-start(bf16[2,3,4,2,64,128]{5,4,3,2,1,0:T(8,128)(2,1)} %collective-permute-done.3.rest_1_.rest_3_), channel_id=1, source_target_pairs={{4,0},{8,4},{12,8},{5,1},{9,5},{13,9},{6,2},{10,6},{14,10},{7,3},{... | collective-permute-start | bytes 2359304 | tf_op jit(solution)/shard_map/ppermute | solution.py:395
  87.8 15.0 %collective-permute-start.12 = (bf16[256,768]{1,0:T(8,128)(2,1)}, bf16[256,768]{1,0:T(8,128)(2,1)}, u32[]{:S(2)}, u32[]{:S(2)}) collective-permute-start(bf16[256,768]{1,0:T(8,128)(2,1)} %finish.1), channel_id=1, source_target_pairs={{4,0},{8,12},{5,1},{9,13},{6,2},{10,14},{7,3},{11,15},{20,16},{24,... | collective-permute-start | bytes 1179656 | tf_op jit(solution)/shard_map/ppermute | solution.py:423
  103.8 4.9 %collective-permute-start.13 = (bf16[256,768]{1,0:T(8,128)(2,1)S(1)}, bf16[256,768]{1,0:T(8,128)(2,1)S(1)}, u32[]{:S(2)}, u32[]{:S(2)}) collective-permute-start(bf16[256,768]{1,0:T(8,128)(2,1)S(1)} %broadcast_select_fusion), channel_id=1, source_target_pairs={{0,2},{2,0},{1,3},{3,1},{4,6},{6,4},{5,7},{7,5},{8,10},{10,8},{9,1... | collective-permute-start | bytes 1179656 | tf_op jit(solution)/shard_map/ppermute | solution.py:384
  107.3 2.7 %collective-permute-start.10 = (bf16[16,8,4,768]{3,2,1,0:T(4,128)(2,1)}, bf16[16,8,4,768]{3,2,1,0:T(4,128)(2,1)S(1)}, u32[]{:S(2)}, u32[]{:S(2)}) collective-permute-start(bf16[16,8,4,768]{3,2,1,0:T(4,128)(2,1)} %get-tuple-element.31), channel_id=1, source_target_pairs={{0,2},{2,0},{1,3},{3,1},{4,6},{6,4},{5,7},{7,5},{8,10},{10,8},{9,1... | collective-permute-start | bytes 2359304 | tf_op jit(solution)/shard_map/ppermute | solution.py:384
  107.4 2.6 %copy-start = (bf16[16,8,4,1536]{3,2,1,0:T(4,128)(2,1)S(1)}, bf16[16,8,4,1536]{3,2,1,0:T(4,128)(2,1)}, u32[]{:S(2)}) copy-start(bf16[16,8,4,1536]{3,2,1,0:T(4,128)(2,1)} %get-tuple-element.30) | copy-start | bytes 4718596
  110.4 1.1 %copy-start.1 = (bf16[16,8,4,1536]{3,2,1,0:T(4,128)(2,1)}, bf16[16,8,4,1536]{3,2,1,0:T(4,128)(2,1)S(1)}, u32[]{:S(2)}) copy-start(bf16[16,8,4,1536]{3,2,1,0:T(4,128)(2,1)S(1)} %constant_dynamic-update-slice_fusion) | copy-start | bytes 4718596

commit v5 on v4

--- a/solution.py
+++ b/solution.py
@@ -127,11 +127,17 @@
         return first, last, wide, thin, row, far_rows, near_rows
 
     def peak(entries):
-        tops = []
+        tops = {}
         for s, _, ok in entries:
-            top = jnp.max(s, axis=1, keepdims=True)
-            tops.append(top if ok is None else jnp.where(ok, top, -jnp.inf))
-        return functools.reduce(jnp.maximum, tops)
+            local = {}
+            for at in range(0, s.shape[1], HD):
+                piece = s[:, at : at + HD]
+                width = piece.shape[1]
+                local[width] = jnp.maximum(local[width], piece) if width in local else piece
+            for width, top in local.items():
+                top = top if ok is None else jnp.where(ok, top, -jnp.inf)
+                tops[width] = jnp.maximum(tops[width], top) if width in tops else top
+        return functools.reduce(jnp.maximum, [jnp.max(top, axis=1, keepdims=True) for top in tops.values()])
 
     def gather(entries, m, first, last, row):
         summed = None

time: 112 us -> 112 us (level)
  no operation moved by 1% of the time
where the time goes in v5:
time: 112 us; the launch traced here: 111 us
  Pallas kernels  46.5 us (42%)
  waiting for transfers between devices  31.2 us (28%)
  starting transfers between devices  28.2 us (25%)
  local copies, waits for them, and re-layouts  2.18 us (2%)
  other arithmetic  2.04 us (2%)
    pallas_call x2, Pallas kernels, video_group(): pl.pallas_call(video_body, grid_spec=pltpu.PrefetchScalarGridSpec(num_sca...  25 us
    ppermute x6, starting transfers between devices, to_neighbours(): return (lax.ppermute(array, 'tm', up), lax.ppermute(array, 'tm', down))  17.6 us
    ppermute x6, waiting for transfers between devices, to_neighbours(): return (lax.ppermute(array, 'tm', up), lax.ppermute(array, 'tm', down))  15.8 us
    ppermute x1, waiting for transfers between devices, shards(): lax.ppermute(sent, 'tm', [(step - 1, step), (strips - step, strips - step...  9.83 us
    pallas_call x1, Pallas kernels, text_partial(): pl.pallas_call(functools.partial(text_body, groups), grid_spec=pltpu.Pref...  8.45 us
    pallas_call x2, Pallas kernels, pack_half(): pl.pallas_call(functools.partial(pack_body, sizes), grid_spec=pltpu.Prefe...  6.96 us
    ppermute x5, waiting for transfers between devices, swap(): return lax.ppermute(array, 'height', [(0, 1), (1, 0)])  5.6 us
    ppermute x5, starting transfers between devices, swap(): return lax.ppermute(array, 'height', [(0, 1), (1, 0)])  5.41 us
  transfers between devices with their start and end apart: 14, of which 9 were waited for; matrix products, arithmetic and copies ran while one was open for 1% of the time, Pallas kernels for 39%

profile of v5, /device:TPU:21, one launch (start us, length us, event | category | flops | bytes accessed | tf_op | source)
XLA Modules:
  0.0 110.9 jit_solution(18111422680662294932)
XLA Ops:
  0.6 0.6 stack.43.scal
  1.3 3.3 %pack.2.mine_ref.rest_0_ = bf16[2,6,4,2,64,128]{5,4,3,2,1,0:T(8,128)(2,1)} custom-call(s32[6]{0:T(128)} %stack.43.scal, bf16[16,8,4,1536]{3,2,1,0:T(4,128)(2,1)} %rest_0_.3, bf16[16,8,4,1536]{3,2,1,0:T(4,128)(2,1)} %rest_1_.3), custom_call_target="tpu_custom_call" | custom-call | bytes 1 | tf_op jit(solution)/shard_map/pack/pallas_call | solution.py:81
  4.6 3.2 %collective-permute-start.1 = (bf16[2,6,4,2,64,128]{5,4,3,2,1,0:T(8,128)(2,1)}, bf16[2,6,4,2,64,128]{5,4,3,2,1,0:T(8,128)(2,1)}, u32[]{:S(2)}, u32[]{:S(2)}) collective-permute-start(bf16[2,6,4,2,64,128]{5,4,3,2,1,0:T(8,128)(2,1)} %pack.2.mine_ref.rest_0_), channel_id=1, source_target_pairs={{0,4},{4,8},{8,12},{1,5},{5,9},{9,13},{2,6},{6,10},{10,14},{3,7},{... | collective-permute-start | bytes 4718600 | tf_op jit(solution)/shard_map/ppermute | solution.py:401
  7.8 2.1 %collective-permute-start.2 = (bf16[2,6,4,2,64,128]{5,4,3,2,1,0:T(8,128)(2,1)}, bf16[2,6,4,2,64,128]{5,4,3,2,1,0:T(8,128)(2,1)}, u32[]{:S(2)}, u32[]{:S(2)}) collective-permute-start(bf16[2,6,4,2,64,128]{5,4,3,2,1,0:T(8,128)(2,1)} %pack.2.mine_ref.rest_0_), channel_id=1, source_target_pairs={{4,0},{8,4},{12,8},{5,1},{9,5},{13,9},{6,2},{10,6},{14,10},{7,3},{... | collective-permute-start | bytes 4718600 | tf_op jit(solution)/shard_map/ppermute | solution.py:401
  9.9 3.6 %pack.3 = (bf16[2,3,4,2,64,128]{5,4,3,2,1,0:T(8,128)(2,1)}, bf16[2,3,4,2,64,128]{5,4,3,2,1,0:T(8,128)(2,1)}, bf16[16,8,4,768]{3,2,1,0:T(4,128)(2,1)}) custom-call(s32[6]{0:T(128)} %stack.43.scal, bf16[16,8,4,1536]{3,2,1,0:T(4,128)(2,1)} %rest_0_.3, bf16[16,8,4,1536]{3,2,1,0:T(4,128)(2,1)} %rest_1_.3, bf16[16,8,4,1536]{3,2,1,0:T(4,128)(2,1)} %own_q.3), custom_call_target="tpu_custom_call" | custom-call | bytes 1 | tf_op jit(solution)/shard_map/pack/pallas_call | solution.py:81
  13.5 1.2 %collective-permute-start = (bf16[16,8,4,768]{3,2,1,0:T(4,128)(2,1)}, bf16[16,8,4,768]{3,2,1,0:T(4,128)(2,1)}, u32[]{:S(2)}, u32[]{:S(2)}) collective-permute-start(bf16[16,8,4,768]{3,2,1,0:T(4,128)(2,1)} %get-tuple-element.19), channel_id=1, source_target_pairs={{0,2},{2,0},{1,3},{3,1},{4,6},{6,4},{5,7},{7,5},{8,10},{10,8},{9,1... | collective-permute-start | bytes 2359304 | tf_op jit(solution)/shard_map/ppermute | solution.py:390
  14.8 0.0 collective-permute-start.4
  14.8 0.5 collective-permute-start.3
  15.3 1.7 %collective-permute-done.pair_q = bf16[16,8,4,768]{3,2,1,0:T(4,128)(2,1)} collective-permute-done((bf16[16,8,4,768]{3,2,1,0:T(4,128)(2,1)}, bf16[16,8,4,768]{3,2,1,0:T(4,128)(2,1)}, u32[]{:S(2)}, u32[]{:S(2)}) %collective-permute-start) | collective-permute-done | bytes 786464 | tf_op jit(solution)/shard_map/ppermute | solution.py:390
  17.0 1.1 %collective-permute-done.4.rest_0_.rest_3_ = bf16[2,3,4,2,64,128]{5,4,3,2,1,0:T(8,128)(2,1)} collective-permute-done((bf16[2,3,4,2,64,128]{5,4,3,2,1,0:T(8,128)(2,1)}, bf16[2,3,4,2,64,128]{5,4,3,2,1,0:T(8,128)(2,1)}, u32[]{:S(2)}, u32[]{:S(2)}) %collective-permute-start.4) | collective-permute-done | bytes 786464 | tf_op jit(solution)/shard_map/ppermute | solution.py:390
  18.1 1.1 %collective-permute-done.3.rest_1_.rest_3_ = bf16[2,3,4,2,64,128]{5,4,3,2,1,0:T(8,128)(2,1)} collective-permute-done((bf16[2,3,4,2,64,128]{5,4,3,2,1,0:T(8,128)(2,1)}, bf16[2,3,4,2,64,128]{5,4,3,2,1,0:T(8,128)(2,1)}, u32[]{:S(2)}, u32[]{:S(2)}) %collective-permute-start.3) | collective-permute-done | bytes 786464 | tf_op jit(solution)/shard_map/ppermute | solution.py:390
  19.3 8.5 %text.1 = (f32[6,256,128]{2,1,0:T(8,128)}, f32[256,128]{1,0:T(8,128)}, bf16[7,256,128]{2,1,0:T(8,128)(2,1)}) custom-call(s32[6]{0:T(128)} %stack.43.scal, s32[1,256]{1,0:T(1,128)} %bitcast.7, bf16[256,1536]{1,0:T(8,128)(2,1)} %q_ref.1, bf16[2,6,4,2,64,128]{5,4,3,2,1,0:T(8,128)(2,1)} %pack.2.mine_ref.rest_0_, bf16[256,1536]{1,0:T(8,128)(2,1)} %rest_6_.3, ...), custom_call_target="tpu_custom_call" | custom-call | bytes 1 | tf_op jit(solution)/shard_map/text/pallas_call | solution.py:288
  27.7 1.3 %collective-permute-start.5 = (bf16[7,256,128]{2,1,0:T(8,128)(2,1)}, bf16[7,256,128]{2,1,0:T(8,128)(2,1)}, u32[]{:S(2)}, u32[]{:S(2)}) collective-permute-start(bf16[7,256,128]{2,1,0:T(8,128)(2,1)} %get-tuple-element.26), channel_id=1, source_target_pairs={{0,4},{12,8},{1,5},{13,9},{2,6},{14,10},{3,7},{15,11},{16,20},{28,... | collective-permute-start | bytes 1376264 | tf_op jit(solution)/shard_map/ppermute | solution.py:412
  29.0 5.1 %collective-permute-start.8 = (bf16[2,3,4,2,64,128]{5,4,3,2,1,0:T(8,128)(2,1)}, bf16[2,3,4,2,64,128]{5,4,3,2,1,0:T(8,128)(2,1)}, u32[]{:S(2)}, u32[]{:S(2)}) collective-permute-start(bf16[2,3,4,2,64,128]{5,4,3,2,1,0:T(8,128)(2,1)} %collective-permute-done.4.rest_0_.rest_3_), channel_id=1, source_target_pairs={{0,4},{4,8},{8,12},{1,5},{5,9},{9,13},{2,6},{6,10},{10,14},{3,7},{... | collective-permute-start | bytes 2359304 | tf_op jit(solution)/shard_map/ppermute | solution.py:401
  34.1 1.9 %collective-permute-start.9 = (bf16[2,3,4,2,64,128]{5,4,3,2,1,0:T(8,128)(2,1)}, bf16[2,3,4,2,64,128]{5,4,3,2,1,0:T(8,128)(2,1)}, u32[]{:S(2)}, u32[]{:S(2)}) collective-permute-start(bf16[2,3,4,2,64,128]{5,4,3,2,1,0:T(8,128)(2,1)} %collective-permute-done.4.rest_0_.rest_3_), channel_id=1, source_target_pairs={{4,0},{8,4},{12,8},{5,1},{9,5},{13,9},{6,2},{10,6},{14,10},{7,3},{... | collective-permute-start | bytes 2359304 | tf_op jit(solution)/shard_map/ppermute | solution.py:401
  36.1 6.0 %collective-permute-done.1.rest_1_ = bf16[2,6,4,2,64,128]{5,4,3,2,1,0:T(8,128)(2,1)} collective-permute-done((bf16[2,6,4,2,64,128]{5,4,3,2,1,0:T(8,128)(2,1)}, bf16[2,6,4,2,64,128]{5,4,3,2,1,0:T(8,128)(2,1)}, u32[]{:S(2)}, u32[]{:S(2)}) %collective-permute-start.1) | collective-permute-done | bytes 1572896 | tf_op jit(solution)/shard_map/ppermute | solution.py:401
  42.1 2.9 %collective-permute-done.2.rest_2_ = bf16[2,6,4,2,64,128]{5,4,3,2,1,0:T(8,128)(2,1)} collective-permute-done((bf16[2,6,4,2,64,128]{5,4,3,2,1,0:T(8,128)(2,1)}, bf16[2,6,4,2,64,128]{5,4,3,2,1,0:T(8,128)(2,1)}, u32[]{:S(2)}, u32[]{:S(2)}) %collective-permute-start.2) | collective-permute-done | bytes 1572896 | tf_op jit(solution)/shard_map/ppermute | solution.py:401
  45.0 9.8 %collective-permute-done.5.got_ref = bf16[7,256,128]{2,1,0:T(8,128)(2,1)} collective-permute-done((bf16[7,256,128]{2,1,0:T(8,128)(2,1)}, bf16[7,256,128]{2,1,0:T(8,128)(2,1)}, u32[]{:S(2)}, u32[]{:S(2)}) %collective-permute-start.5) | collective-permute-done | bytes 458784 | tf_op jit(solution)/shard_map/ppermute | solution.py:412
  54.8 2.8 %join.1.own_ref = bf16[7,256,128]{2,1,0:T(8,128)(2,1)} custom-call(f32[6,256,128]{2,1,0:T(8,128)} %get-tuple-element.23.sum_ref, f32[256,128]{1,0:T(8,128)} %get-tuple-element.25.log_ref, bf16[7,256,128]{2,1,0:T(8,128)(2,1)} %collective-permute-done.5.got_ref), custom_call_target="tpu_custom_call" | custom-call | bytes 1 | tf_op jit(solution)/shard_map/join/pallas_call | solution.py:336
  57.6 1.9 %collective-permute-start.11 = (bf16[7,256,128]{2,1,0:T(8,128)(2,1)}, bf16[7,256,128]{2,1,0:T(8,128)(2,1)}, u32[]{:S(2)}, u32[]{:S(2)}) collective-permute-start(bf16[7,256,128]{2,1,0:T(8,128)(2,1)} %join.1.own_ref), channel_id=1, source_target_pairs={{4,8},{8,4},{5,9},{9,5},{6,10},{10,6},{7,11},{11,7},{20,24},{24,20... | collective-permute-start | bytes 1376264 | tf_op jit(solution)/shard_map/ppermute | solution.py:414
  59.5 1.9 %collective-permute-start.6 = (bf16[2,3,4,2,64,128]{5,4,3,2,1,0:T(8,128)(2,1)}, bf16[2,3,4,2,64,128]{5,4,3,2,1,0:T(8,128)(2,1)}, u32[]{:S(2)}, u32[]{:S(2)}) collective-permute-start(bf16[2,3,4,2,64,128]{5,4,3,2,1,0:T(8,128)(2,1)} %collective-permute-done.3.rest_1_.rest_3_), channel_id=1, source_target_pairs={{0,4},{4,8},{8,12},{1,5},{5,9},{9,13},{2,6},{6,10},{10,14},{3,7},{... | collective-permute-start | bytes 2359304 | tf_op jit(solution)/shard_map/ppermute | solution.py:401
  61.4 3.4 %collective-permute-start.7 = (bf16[2,3,4,2,64,128]{5,4,3,2,1,0:T(8,128)(2,1)}, bf16[2,3,4,2,64,128]{5,4,3,2,1,0:T(8,128)(2,1)}, u32[]{:S(2)}, u32[]{:S(2)}) collective-permute-start(bf16[2,3,4,2,64,128]{5,4,3,2,1,0:T(8,128)(2,1)} %collective-permute-done.3.rest_1_.rest_3_), channel_id=1, source_target_pairs={{4,0},{8,4},{12,8},{5,1},{9,5},{13,9},{6,2},{10,6},{14,10},{7,3},{... | collective-permute-start | bytes 2359304 | tf_op jit(solution)/shard_map/ppermute | solution.py:401
  64.8 0.0 collective-permute-done.8.rest_4_
  64.8 6.9 %collective-permute-done.9.rest_5_ = bf16[2,3,4,2,64,128]{5,4,3,2,1,0:T(8,128)(2,1)} collective-permute-done((bf16[2,3,4,2,64,128]{5,4,3,2,1,0:T(8,128)(2,1)}, bf16[2,3,4,2,64,128]{5,4,3,2,1,0:T(8,128)(2,1)}, u32[]{:S(2)}, u32[]{:S(2)}) %collective-permute-start.9) | collective-permute-done | bytes 786464 | tf_op jit(solution)/shard_map/ppermute | solution.py:401
  71.6 12.5 %video.2 = (bf16[16,8,4,1536]{3,2,1,0:T(4,128)(2,1)}, bf16[16,8,4,768]{3,2,1,0:T(4,128)(2,1)}) custom-call(s32[6]{0:T(128)} %stack.43.scal, s32[1,256]{1,0:T(1,128)} %bitcast.8, bf16[16,8,4,1536]{3,2,1,0:T(4,128)(2,1)} %own_q.3, bf16[16,8,4,768]{3,2,1,0:T(4,128)(2,1)} %collective-permute-done.pair_q, bf16[2,6,4,2,64,128]{5,4,3,2,1,0:T(8,128)(2,1)} %pack.2.mine_ref.rest_0_, ...), custom_call_target="tpu_custom_call" | custom-call | bytes 1 | tf_op jit(solution)/shard_map/video/pallas_call | solution.py:193
  84.1 0.0 collective-permute-done.11.got_ref
  84.1 3.3 %finish.1 = bf16[256,768]{1,0:T(8,128)(2,1)} custom-call(s32[6]{0:T(128)} %stack.43.scal, bf16[7,256,128]{2,1,0:T(8,128)(2,1)} %join.1.own_ref, bf16[7,256,128]{2,1,0:T(8,128)(2,1)} %collective-permute-done.11.got_ref), custom_call_target="tpu_custom_call" | custom-call | bytes 1 | tf_op jit(solution)/shard_map/finish/pallas_call | solution.py:362
  87.4 2.0 %collective-permute-start.12 = (bf16[256,768]{1,0:T(8,128)(2,1)}, bf16[256,768]{1,0:T(8,128)(2,1)}, u32[]{:S(2)}, u32[]{:S(2)}) collective-permute-start(bf16[256,768]{1,0:T(8,128)(2,1)} %finish.1), channel_id=1, source_target_pairs={{4,0},{8,12},{5,1},{9,13},{6,2},{10,14},{7,3},{11,15},{20,16},{24,... | collective-permute-start | bytes 1179656 | tf_op jit(solution)/shard_map/ppermute | solution.py:429
  89.4 0.0 collective-permute-done.6.rest_4_
  89.4 0.0 collective-permute-done.7.rest_5_
  89.4 12.6 %video.3 = (bf16[16,8,4,1536]{3,2,1,0:T(4,128)(2,1)}, bf16[16,8,4,768]{3,2,1,0:T(4,128)(2,1)}) custom-call(s32[6]{0:T(128)} %stack.43.scal, s32[1,256]{1,0:T(1,128)} %bitcast.9, bf16[16,8,4,1536]{3,2,1,0:T(4,128)(2,1)} %own_q.3, bf16[16,8,4,768]{3,2,1,0:T(4,128)(2,1)} %collective-permute-done.pair_q, ...), custom_call_target="tpu_custom_call", output_to_operand_aliasing={{0}: (12, {}), {1}: (13, {})} | custom-call | bytes 1 | tf_op jit(solution)/shard_map/video/pallas_call | solution.py:193
  102.0 0.0 collective-permute-done.12
  102.0 1.1 broadcast_select_fusion
  103.1 3.6 %collective-permute-start.13 = (bf16[256,768]{1,0:T(8,128)(2,1)S(1)}, bf16[256,768]{1,0:T(8,128)(2,1)S(1)}, u32[]{:S(2)}, u32[]{:S(2)}) collective-permute-start(bf16[256,768]{1,0:T(8,128)(2,1)S(1)} %broadcast_select_fusion), channel_id=1, source_target_pairs={{0,2},{2,0},{1,3},{3,1},{4,6},{6,4},{5,7},{7,5},{8,10},{10,8},{9,1... | collective-permute-start | bytes 1179656 | tf_op jit(solution)/shard_map/ppermute | solution.py:390
  106.7 0.1 collective-permute-start.10
  106.7 0.0 copy-start
  106.7 1.3 %collective-permute-done.13 = bf16[256,768]{1,0:T(8,128)(2,1)S(1)} collective-permute-done((bf16[256,768]{1,0:T(8,128)(2,1)S(1)}, bf16[256,768]{1,0:T(8,128)(2,1)S(1)}, u32[]{:S(2)}, u32[]{:S(2)}) %collective-permute-start.13) | collective-permute-done | bytes 393248 | tf_op jit(solution)/shard_map/ppermute | solution.py:390
  108.0 0.1 broadcast_select_fusion.2
  108.1 0.9 pad_maximum_fusion
  109.0 0.3 collective-permute-done.10
  109.3 0.0 copy-done
  109.3 0.4 constant_dynamic-update-slice_fusion
  109.8 0.0 copy-start.1
  109.8 1.1 %copy-done.1 = bf16[16,8,4,1536]{3,2,1,0:T(4,128)(2,1)} copy-done((bf16[16,8,4,1536]{3,2,1,0:T(4,128)(2,1)}, bf16[16,8,4,1536]{3,2,1,0:T(4,128)(2,1)S(1)}, u32[]{:S(2)}) %copy-start.1) | copy-done | bytes 1572888
Async XLA Ops:
  4.6 37.5 %collective-permute-start.1 = (bf16[2,6,4,2,64,128]{5,4,3,2,1,0:T(8,128)(2,1)}, bf16[2,6,4,2,64,128]{5,4,3,2,1,0:T(8,128)(2,1)}, u32[]{:S(2)}, u32[]{:S(2)}) collective-permute-start(bf16[2,6,4,2,64,128]{5,4,3,2,1,0:T(8,128)(2,1)} %pack.2.mine_ref.rest_0_), channel_id=1, source_target_pairs={{0,4},{4,8},{8,12},{1,5},{5,9},{9,13},{2,6},{6,10},{10,14},{3,7},{... | collective-permute-start | bytes 4718600 | tf_op jit(solution)/shard_map/ppermute | solution.py:401
  7.8 37.2 %collective-permute-start.2 = (bf16[2,6,4,2,64,128]{5,4,3,2,1,0:T(8,128)(2,1)}, bf16[2,6,4,2,64,128]{5,4,3,2,1,0:T(8,128)(2,1)}, u32[]{:S(2)}, u32[]{:S(2)}) collective-permute-start(bf16[2,6,4,2,64,128]{5,4,3,2,1,0:T(8,128)(2,1)} %pack.2.mine_ref.rest_0_), channel_id=1, source_target_pairs={{4,0},{8,4},{12,8},{5,1},{9,5},{13,9},{6,2},{10,6},{14,10},{7,3},{... | collective-permute-start | bytes 4718600 | tf_op jit(solution)/shard_map/ppermute | solution.py:401
  13.5 3.5 %collective-permute-start = (bf16[16,8,4,768]{3,2,1,0:T(4,128)(2,1)}, bf16[16,8,4,768]{3,2,1,0:T(4,128)(2,1)}, u32[]{:S(2)}, u32[]{:S(2)}) collective-permute-start(bf16[16,8,4,768]{3,2,1,0:T(4,128)(2,1)} %get-tuple-element.19), channel_id=1, source_target_pairs={{0,2},{2,0},{1,3},{3,1},{4,6},{6,4},{5,7},{7,5},{8,10},{10,8},{9,1... | collective-permute-start | bytes 2359304 | tf_op jit(solution)/shard_map/ppermute | solution.py:390
  14.8 3.4 %collective-permute-start.4 = (bf16[2,3,4,2,64,128]{5,4,3,2,1,0:T(8,128)(2,1)}, bf16[2,3,4,2,64,128]{5,4,3,2,1,0:T(8,128)(2,1)}, u32[]{:S(2)}, u32[]{:S(2)}) collective-permute-start(bf16[2,3,4,2,64,128]{5,4,3,2,1,0:T(8,128)(2,1)} %get-tuple-element.22), channel_id=1, source_target_pairs={{0,2},{2,0},{1,3},{3,1},{4,6},{6,4},{5,7},{7,5},{8,10},{10,8},{9,1... | collective-permute-start | bytes 2359304 | tf_op jit(solution)/shard_map/ppermute | solution.py:390
  14.8 4.5 %collective-permute-start.3 = (bf16[2,3,4,2,64,128]{5,4,3,2,1,0:T(8,128)(2,1)}, bf16[2,3,4,2,64,128]{5,4,3,2,1,0:T(8,128)(2,1)}, u32[]{:S(2)}, u32[]{:S(2)}) collective-permute-start(bf16[2,3,4,2,64,128]{5,4,3,2,1,0:T(8,128)(2,1)} %get-tuple-element.20), channel_id=1, source_target_pairs={{0,2},{2,0},{1,3},{3,1},{4,6},{6,4},{5,7},{7,5},{8,10},{10,8},{9,1... | collective-permute-start | bytes 2359304 | tf_op jit(solution)/shard_map/ppermute | solution.py:390
  27.7 27.1 %collective-permute-start.5 = (bf16[7,256,128]{2,1,0:T(8,128)(2,1)}, bf16[7,256,128]{2,1,0:T(8,128)(2,1)}, u32[]{:S(2)}, u32[]{:S(2)}) collective-permute-start(bf16[7,256,128]{2,1,0:T(8,128)(2,1)} %get-tuple-element.26), channel_id=1, source_target_pairs={{0,4},{12,8},{1,5},{13,9},{2,6},{14,10},{3,7},{15,11},{16,20},{28,... | collective-permute-start | bytes 1376264 | tf_op jit(solution)/shard_map/ppermute | solution.py:412
  29.0 35.8 %collective-permute-start.8 = (bf16[2,3,4,2,64,128]{5,4,3,2,1,0:T(8,128)(2,1)}, bf16[2,3,4,2,64,128]{5,4,3,2,1,0:T(8,128)(2,1)}, u32[]{:S(2)}, u32[]{:S(2)}) collective-permute-start(bf16[2,3,4,2,64,128]{5,4,3,2,1,0:T(8,128)(2,1)} %collective-permute-done.4.rest_0_.rest_3_), channel_id=1, source_target_pairs={{0,4},{4,8},{8,12},{1,5},{5,9},{9,13},{2,6},{6,10},{10,14},{3,7},{... | collective-permute-start | bytes 2359304 | tf_op jit(solution)/shard_map/ppermute | solution.py:401
  34.1 37.5 %collective-permute-start.9 = (bf16[2,3,4,2,64,128]{5,4,3,2,1,0:T(8,128)(2,1)}, bf16[2,3,4,2,64,128]{5,4,3,2,1,0:T(8,128)(2,1)}, u32[]{:S(2)}, u32[]{:S(2)}) collective-permute-start(bf16[2,3,4,2,64,128]{5,4,3,2,1,0:T(8,128)(2,1)} %collective-permute-done.4.rest_0_.rest_3_), channel_id=1, source_target_pairs={{4,0},{8,4},{12,8},{5,1},{9,5},{13,9},{6,2},{10,6},{14,10},{7,3},{... | collective-permute-start | bytes 2359304 | tf_op jit(solution)/shard_map/ppermute | solution.py:401
  57.6 26.6 %collective-permute-start.11 = (bf16[7,256,128]{2,1,0:T(8,128)(2,1)}, bf16[7,256,128]{2,1,0:T(8,128)(2,1)}, u32[]{:S(2)}, u32[]{:S(2)}) collective-permute-start(bf16[7,256,128]{2,1,0:T(8,128)(2,1)} %join.1.own_ref), channel_id=1, source_target_pairs={{4,8},{8,4},{5,9},{9,5},{6,10},{10,6},{7,11},{11,7},{20,24},{24,20... | collective-permute-start | bytes 1376264 | tf_op jit(solution)/shard_map/ppermute | solution.py:414
  59.5 30.0 %collective-permute-start.6 = (bf16[2,3,4,2,64,128]{5,4,3,2,1,0:T(8,128)(2,1)}, bf16[2,3,4,2,64,128]{5,4,3,2,1,0:T(8,128)(2,1)}, u32[]{:S(2)}, u32[]{:S(2)}) collective-permute-start(bf16[2,3,4,2,64,128]{5,4,3,2,1,0:T(8,128)(2,1)} %collective-permute-done.3.rest_1_.rest_3_), channel_id=1, source_target_pairs={{0,4},{4,8},{8,12},{1,5},{5,9},{9,13},{2,6},{6,10},{10,14},{3,7},{... | collective-permute-start | bytes 2359304 | tf_op jit(solution)/shard_map/ppermute | solution.py:401
  61.4 28.0 %collective-permute-start.7 = (bf16[2,3,4,2,64,128]{5,4,3,2,1,0:T(8,128)(2,1)}, bf16[2,3,4,2,64,128]{5,4,3,2,1,0:T(8,128)(2,1)}, u32[]{:S(2)}, u32[]{:S(2)}) collective-permute-start(bf16[2,3,4,2,64,128]{5,4,3,2,1,0:T(8,128)(2,1)} %collective-permute-done.3.rest_1_.rest_3_), channel_id=1, source_target_pairs={{4,0},{8,4},{12,8},{5,1},{9,5},{13,9},{6,2},{10,6},{14,10},{7,3},{... | collective-permute-start | bytes 2359304 | tf_op jit(solution)/shard_map/ppermute | solution.py:401
  87.4 14.6 %collective-permute-start.12 = (bf16[256,768]{1,0:T(8,128)(2,1)}, bf16[256,768]{1,0:T(8,128)(2,1)}, u32[]{:S(2)}, u32[]{:S(2)}) collective-permute-start(bf16[256,768]{1,0:T(8,128)(2,1)} %finish.1), channel_id=1, source_target_pairs={{4,0},{8,12},{5,1},{9,13},{6,2},{10,14},{7,3},{11,15},{20,16},{24,... | collective-permute-start | bytes 1179656 | tf_op jit(solution)/shard_map/ppermute | solution.py:429
  103.1 4.9 %collective-permute-start.13 = (bf16[256,768]{1,0:T(8,128)(2,1)S(1)}, bf16[256,768]{1,0:T(8,128)(2,1)S(1)}, u32[]{:S(2)}, u32[]{:S(2)}) collective-permute-start(bf16[256,768]{1,0:T(8,128)(2,1)S(1)} %broadcast_select_fusion), channel_id=1, source_target_pairs={{0,2},{2,0},{1,3},{3,1},{4,6},{6,4},{5,7},{7,5},{8,10},{10,8},{9,1... | collective-permute-start | bytes 1179656 | tf_op jit(solution)/shard_map/ppermute | solution.py:390
  106.7 2.7 %collective-permute-start.10 = (bf16[16,8,4,768]{3,2,1,0:T(4,128)(2,1)}, bf16[16,8,4,768]{3,2,1,0:T(4,128)(2,1)S(1)}, u32[]{:S(2)}, u32[]{:S(2)}) collective-permute-start(bf16[16,8,4,768]{3,2,1,0:T(4,128)(2,1)} %get-tuple-element.31), channel_id=1, source_target_pairs={{0,2},{2,0},{1,3},{3,1},{4,6},{6,4},{5,7},{7,5},{8,10},{10,8},{9,1... | collective-permute-start | bytes 2359304 | tf_op jit(solution)/shard_map/ppermute | solution.py:390
  106.7 2.6 %copy-start = (bf16[16,8,4,1536]{3,2,1,0:T(4,128)(2,1)S(1)}, bf16[16,8,4,1536]{3,2,1,0:T(4,128)(2,1)}, u32[]{:S(2)}) copy-start(bf16[16,8,4,1536]{3,2,1,0:T(4,128)(2,1)} %get-tuple-element.30) | copy-start | bytes 4718596
  109.8 1.1 %copy-start.1 = (bf16[16,8,4,1536]{3,2,1,0:T(4,128)(2,1)}, bf16[16,8,4,1536]{3,2,1,0:T(4,128)(2,1)S(1)}, u32[]{:S(2)}) copy-start(bf16[16,8,4,1536]{3,2,1,0:T(4,128)(2,1)S(1)} %constant_dynamic-update-slice_fusion) | copy-start | bytes 4718596

commit v6 on v5

--- a/solution.py
+++ b/solution.py
@@ -349,7 +349,7 @@
     for flag in (low, jnp.logical_not(low)):
 
         def pick(index, flag=flag):
-            return jnp.where(flag, own_ref[index].astype(F32), got_ref[index].astype(F32))
+            return jnp.where(flag, own_ref[index], got_ref[index]).astype(F32)
 
         parts.append((pick, read_logs(pick(heads))))
     outs, _ = combine(parts, heads)

time: 112 us -> 112 us (level)
  no operation moved by 1% of the time
where the time goes in v6:
time: 112 us; the launch traced here: 111 us
  Pallas kernels  46.4 us (41%)
  waiting for transfers between devices  31.2 us (28%)
  starting transfers between devices  28.3 us (25%)
  local copies, waits for them, and re-layouts  2.18 us (2%)
  other arithmetic  2.04 us (2%)
    pallas_call x2, Pallas kernels, video_group(): pl.pallas_call(video_body, grid_spec=pltpu.PrefetchScalarGridSpec(num_sca...  25 us
    ppermute x6, starting transfers between devices, to_neighbours(): return (lax.ppermute(array, 'tm', up), lax.ppermute(array, 'tm', down))  17.6 us
    ppermute x6, waiting for transfers between devices, to_neighbours(): return (lax.ppermute(array, 'tm', up), lax.ppermute(array, 'tm', down))  15.8 us
    ppermute x1, waiting for transfers between devices, shards(): lax.ppermute(sent, 'tm', [(step - 1, step), (strips - step, strips - step...  9.83 us
    pallas_call x1, Pallas kernels, text_partial(): pl.pallas_call(functools.partial(text_body, groups), grid_spec=pltpu.Pref...  8.45 us
    pallas_call x2, Pallas kernels, pack_half(): pl.pallas_call(functools.partial(pack_body, sizes), grid_spec=pltpu.Prefe...  6.96 us
    ppermute x5, waiting for transfers between devices, swap(): return lax.ppermute(array, 'height', [(0, 1), (1, 0)])  5.6 us
    ppermute x5, starting transfers between devices, swap(): return lax.ppermute(array, 'height', [(0, 1), (1, 0)])  5.46 us
  transfers between devices with their start and end apart: 14, of which 9 were waited for; matrix products, arithmetic and copies ran while one was open for 1% of the time, Pallas kernels for 39%

profile of v6, /device:TPU:21, one launch (start us, length us, event | category | flops | bytes accessed | tf_op | source)
XLA Modules:
  0.0 110.9 jit_solution(16995097500805845124)
XLA Ops:
  0.6 0.6 stack.43.scal
  1.3 3.3 %pack.2.mine_ref.rest_0_ = bf16[2,6,4,2,64,128]{5,4,3,2,1,0:T(8,128)(2,1)} custom-call(s32[6]{0:T(128)} %stack.43.scal, bf16[16,8,4,1536]{3,2,1,0:T(4,128)(2,1)} %rest_0_.3, bf16[16,8,4,1536]{3,2,1,0:T(4,128)(2,1)} %rest_1_.3), custom_call_target="tpu_custom_call" | custom-call | bytes 1 | tf_op jit(solution)/shard_map/pack/pallas_call | solution.py:81
  4.6 3.2 %collective-permute-start.1 = (bf16[2,6,4,2,64,128]{5,4,3,2,1,0:T(8,128)(2,1)}, bf16[2,6,4,2,64,128]{5,4,3,2,1,0:T(8,128)(2,1)}, u32[]{:S(2)}, u32[]{:S(2)}) collective-permute-start(bf16[2,6,4,2,64,128]{5,4,3,2,1,0:T(8,128)(2,1)} %pack.2.mine_ref.rest_0_), channel_id=1, source_target_pairs={{0,4},{4,8},{8,12},{1,5},{5,9},{9,13},{2,6},{6,10},{10,14},{3,7},{... | collective-permute-start | bytes 4718600 | tf_op jit(solution)/shard_map/ppermute | solution.py:401
  7.8 2.1 %collective-permute-start.2 = (bf16[2,6,4,2,64,128]{5,4,3,2,1,0:T(8,128)(2,1)}, bf16[2,6,4,2,64,128]{5,4,3,2,1,0:T(8,128)(2,1)}, u32[]{:S(2)}, u32[]{:S(2)}) collective-permute-start(bf16[2,6,4,2,64,128]{5,4,3,2,1,0:T(8,128)(2,1)} %pack.2.mine_ref.rest_0_), channel_id=1, source_target_pairs={{4,0},{8,4},{12,8},{5,1},{9,5},{13,9},{6,2},{10,6},{14,10},{7,3},{... | collective-permute-start | bytes 4718600 | tf_op jit(solution)/shard_map/ppermute | solution.py:401
  9.9 3.6 %pack.3 = (bf16[2,3,4,2,64,128]{5,4,3,2,1,0:T(8,128)(2,1)}, bf16[2,3,4,2,64,128]{5,4,3,2,1,0:T(8,128)(2,1)}, bf16[16,8,4,768]{3,2,1,0:T(4,128)(2,1)}) custom-call(s32[6]{0:T(128)} %stack.43.scal, bf16[16,8,4,1536]{3,2,1,0:T(4,128)(2,1)} %rest_0_.3, bf16[16,8,4,1536]{3,2,1,0:T(4,128)(2,1)} %rest_1_.3, bf16[16,8,4,1536]{3,2,1,0:T(4,128)(2,1)} %own_q.3), custom_call_target="tpu_custom_call" | custom-call | bytes 1 | tf_op jit(solution)/shard_map/pack/pallas_call | solution.py:81
  13.5 1.2 %collective-permute-start = (bf16[16,8,4,768]{3,2,1,0:T(4,128)(2,1)}, bf16[16,8,4,768]{3,2,1,0:T(4,128)(2,1)}, u32[]{:S(2)}, u32[]{:S(2)}) collective-permute-start(bf16[16,8,4,768]{3,2,1,0:T(4,128)(2,1)} %get-tuple-element.19), channel_id=1, source_target_pairs={{0,2},{2,0},{1,3},{3,1},{4,6},{6,4},{5,7},{7,5},{8,10},{10,8},{9,1... | collective-permute-start | bytes 2359304 | tf_op jit(solution)/shard_map/ppermute | solution.py:390
  14.8 0.0 collective-permute-start.4
  14.8 0.5 collective-permute-start.3
  15.3 1.7 %collective-permute-done.pair_q = bf16[16,8,4,768]{3,2,1,0:T(4,128)(2,1)} collective-permute-done((bf16[16,8,4,768]{3,2,1,0:T(4,128)(2,1)}, bf16[16,8,4,768]{3,2,1,0:T(4,128)(2,1)}, u32[]{:S(2)}, u32[]{:S(2)}) %collective-permute-start) | collective-permute-done | bytes 786464 | tf_op jit(solution)/shard_map/ppermute | solution.py:390
  17.0 1.1 %collective-permute-done.4.rest_0_.rest_3_ = bf16[2,3,4,2,64,128]{5,4,3,2,1,0:T(8,128)(2,1)} collective-permute-done((bf16[2,3,4,2,64,128]{5,4,3,2,1,0:T(8,128)(2,1)}, bf16[2,3,4,2,64,128]{5,4,3,2,1,0:T(8,128)(2,1)}, u32[]{:S(2)}, u32[]{:S(2)}) %collective-permute-start.4) | collective-permute-done | bytes 786464 | tf_op jit(solution)/shard_map/ppermute | solution.py:390
  18.1 1.1 %collective-permute-done.3.rest_1_.rest_3_ = bf16[2,3,4,2,64,128]{5,4,3,2,1,0:T(8,128)(2,1)} collective-permute-done((bf16[2,3,4,2,64,128]{5,4,3,2,1,0:T(8,128)(2,1)}, bf16[2,3,4,2,64,128]{5,4,3,2,1,0:T(8,128)(2,1)}, u32[]{:S(2)}, u32[]{:S(2)}) %collective-permute-start.3) | collective-permute-done | bytes 786464 | tf_op jit(solution)/shard_map/ppermute | solution.py:390
  19.3 8.5 %text.1 = (f32[6,256,128]{2,1,0:T(8,128)}, f32[256,128]{1,0:T(8,128)}, bf16[7,256,128]{2,1,0:T(8,128)(2,1)}) custom-call(s32[6]{0:T(128)} %stack.43.scal, s32[1,256]{1,0:T(1,128)} %bitcast.7, bf16[256,1536]{1,0:T(8,128)(2,1)} %q_ref.1, bf16[2,6,4,2,64,128]{5,4,3,2,1,0:T(8,128)(2,1)} %pack.2.mine_ref.rest_0_, bf16[256,1536]{1,0:T(8,128)(2,1)} %rest_6_.3, ...), custom_call_target="tpu_custom_call" | custom-call | bytes 1 | tf_op jit(solution)/shard_map/text/pallas_call | solution.py:288
  27.7 1.3 %collective-permute-start.5 = (bf16[7,256,128]{2,1,0:T(8,128)(2,1)}, bf16[7,256,128]{2,1,0:T(8,128)(2,1)}, u32[]{:S(2)}, u32[]{:S(2)}) collective-permute-start(bf16[7,256,128]{2,1,0:T(8,128)(2,1)} %get-tuple-element.26), channel_id=1, source_target_pairs={{0,4},{12,8},{1,5},{13,9},{2,6},{14,10},{3,7},{15,11},{16,20},{28,... | collective-permute-start | bytes 1376264 | tf_op jit(solution)/shard_map/ppermute | solution.py:412
  29.0 5.1 %collective-permute-start.8 = (bf16[2,3,4,2,64,128]{5,4,3,2,1,0:T(8,128)(2,1)}, bf16[2,3,4,2,64,128]{5,4,3,2,1,0:T(8,128)(2,1)}, u32[]{:S(2)}, u32[]{:S(2)}) collective-permute-start(bf16[2,3,4,2,64,128]{5,4,3,2,1,0:T(8,128)(2,1)} %collective-permute-done.4.rest_0_.rest_3_), channel_id=1, source_target_pairs={{0,4},{4,8},{8,12},{1,5},{5,9},{9,13},{2,6},{6,10},{10,14},{3,7},{... | collective-permute-start | bytes 2359304 | tf_op jit(solution)/shard_map/ppermute | solution.py:401
  34.1 1.9 %collective-permute-start.9 = (bf16[2,3,4,2,64,128]{5,4,3,2,1,0:T(8,128)(2,1)}, bf16[2,3,4,2,64,128]{5,4,3,2,1,0:T(8,128)(2,1)}, u32[]{:S(2)}, u32[]{:S(2)}) collective-permute-start(bf16[2,3,4,2,64,128]{5,4,3,2,1,0:T(8,128)(2,1)} %collective-permute-done.4.rest_0_.rest_3_), channel_id=1, source_target_pairs={{4,0},{8,4},{12,8},{5,1},{9,5},{13,9},{6,2},{10,6},{14,10},{7,3},{... | collective-permute-start | bytes 2359304 | tf_op jit(solution)/shard_map/ppermute | solution.py:401
  36.1 6.0 %collective-permute-done.1.rest_1_ = bf16[2,6,4,2,64,128]{5,4,3,2,1,0:T(8,128)(2,1)} collective-permute-done((bf16[2,6,4,2,64,128]{5,4,3,2,1,0:T(8,128)(2,1)}, bf16[2,6,4,2,64,128]{5,4,3,2,1,0:T(8,128)(2,1)}, u32[]{:S(2)}, u32[]{:S(2)}) %collective-permute-start.1) | collective-permute-done | bytes 1572896 | tf_op jit(solution)/shard_map/ppermute | solution.py:401
  42.1 2.9 %collective-permute-done.2.rest_2_ = bf16[2,6,4,2,64,128]{5,4,3,2,1,0:T(8,128)(2,1)} collective-permute-done((bf16[2,6,4,2,64,128]{5,4,3,2,1,0:T(8,128)(2,1)}, bf16[2,6,4,2,64,128]{5,4,3,2,1,0:T(8,128)(2,1)}, u32[]{:S(2)}, u32[]{:S(2)}) %collective-permute-start.2) | collective-permute-done | bytes 1572896 | tf_op jit(solution)/shard_map/ppermute | solution.py:401
  45.0 9.8 %collective-permute-done.5.got_ref = bf16[7,256,128]{2,1,0:T(8,128)(2,1)} collective-permute-done((bf16[7,256,128]{2,1,0:T(8,128)(2,1)}, bf16[7,256,128]{2,1,0:T(8,128)(2,1)}, u32[]{:S(2)}, u32[]{:S(2)}) %collective-permute-start.5) | collective-permute-done | bytes 458784 | tf_op jit(solution)/shard_map/ppermute | solution.py:412
  54.8 2.8 %join.1.own_ref = bf16[7,256,128]{2,1,0:T(8,128)(2,1)} custom-call(f32[6,256,128]{2,1,0:T(8,128)} %get-tuple-element.23.sum_ref, f32[256,128]{1,0:T(8,128)} %get-tuple-element.25.log_ref, bf16[7,256,128]{2,1,0:T(8,128)(2,1)} %collective-permute-done.5.got_ref), custom_call_target="tpu_custom_call" | custom-call | bytes 1 | tf_op jit(solution)/shard_map/join/pallas_call | solution.py:336
  57.6 1.9 %collective-permute-start.11 = (bf16[7,256,128]{2,1,0:T(8,128)(2,1)}, bf16[7,256,128]{2,1,0:T(8,128)(2,1)}, u32[]{:S(2)}, u32[]{:S(2)}) collective-permute-start(bf16[7,256,128]{2,1,0:T(8,128)(2,1)} %join.1.own_ref), channel_id=1, source_target_pairs={{4,8},{8,4},{5,9},{9,5},{6,10},{10,6},{7,11},{11,7},{20,24},{24,20... | collective-permute-start | bytes 1376264 | tf_op jit(solution)/shard_map/ppermute | solution.py:414
  59.5 1.9 %collective-permute-start.6 = (bf16[2,3,4,2,64,128]{5,4,3,2,1,0:T(8,128)(2,1)}, bf16[2,3,4,2,64,128]{5,4,3,2,1,0:T(8,128)(2,1)}, u32[]{:S(2)}, u32[]{:S(2)}) collective-permute-start(bf16[2,3,4,2,64,128]{5,4,3,2,1,0:T(8,128)(2,1)} %collective-permute-done.3.rest_1_.rest_3_), channel_id=1, source_target_pairs={{0,4},{4,8},{8,12},{1,5},{5,9},{9,13},{2,6},{6,10},{10,14},{3,7},{... | collective-permute-start | bytes 2359304 | tf_op jit(solution)/shard_map/ppermute | solution.py:401
  61.4 3.4 %collective-permute-start.7 = (bf16[2,3,4,2,64,128]{5,4,3,2,1,0:T(8,128)(2,1)}, bf16[2,3,4,2,64,128]{5,4,3,2,1,0:T(8,128)(2,1)}, u32[]{:S(2)}, u32[]{:S(2)}) collective-permute-start(bf16[2,3,4,2,64,128]{5,4,3,2,1,0:T(8,128)(2,1)} %collective-permute-done.3.rest_1_.rest_3_), channel_id=1, source_target_pairs={{4,0},{8,4},{12,8},{5,1},{9,5},{13,9},{6,2},{10,6},{14,10},{7,3},{... | collective-permute-start | bytes 2359304 | tf_op jit(solution)/shard_map/ppermute | solution.py:401
  64.8 0.0 collective-permute-done.8.rest_4_
  64.8 6.9 %collective-permute-done.9.rest_5_ = bf16[2,3,4,2,64,128]{5,4,3,2,1,0:T(8,128)(2,1)} collective-permute-done((bf16[2,3,4,2,64,128]{5,4,3,2,1,0:T(8,128)(2,1)}, bf16[2,3,4,2,64,128]{5,4,3,2,1,0:T(8,128)(2,1)}, u32[]{:S(2)}, u32[]{:S(2)}) %collective-permute-start.9) | collective-permute-done | bytes 786464 | tf_op jit(solution)/shard_map/ppermute | solution.py:401
  71.6 12.5 %video.2 = (bf16[16,8,4,1536]{3,2,1,0:T(4,128)(2,1)}, bf16[16,8,4,768]{3,2,1,0:T(4,128)(2,1)}) custom-call(s32[6]{0:T(128)} %stack.43.scal, s32[1,256]{1,0:T(1,128)} %bitcast.8, bf16[16,8,4,1536]{3,2,1,0:T(4,128)(2,1)} %own_q.3, bf16[16,8,4,768]{3,2,1,0:T(4,128)(2,1)} %collective-permute-done.pair_q, bf16[2,6,4,2,64,128]{5,4,3,2,1,0:T(8,128)(2,1)} %pack.2.mine_ref.rest_0_, ...), custom_call_target="tpu_custom_call" | custom-call | bytes 1 | tf_op jit(solution)/shard_map/video/pallas_call | solution.py:193
  84.1 0.0 collective-permute-done.11.got_ref
  84.1 3.3 %finish.1 = bf16[256,768]{1,0:T(8,128)(2,1)} custom-call(s32[6]{0:T(128)} %stack.43.scal, bf16[7,256,128]{2,1,0:T(8,128)(2,1)} %join.1.own_ref, bf16[7,256,128]{2,1,0:T(8,128)(2,1)} %collective-permute-done.11.got_ref), custom_call_target="tpu_custom_call" | custom-call | bytes 1 | tf_op jit(solution)/shard_map/finish/pallas_call | solution.py:362
  87.4 2.0 %collective-permute-start.12 = (bf16[256,768]{1,0:T(8,128)(2,1)}, bf16[256,768]{1,0:T(8,128)(2,1)}, u32[]{:S(2)}, u32[]{:S(2)}) collective-permute-start(bf16[256,768]{1,0:T(8,128)(2,1)} %finish.1), channel_id=1, source_target_pairs={{4,0},{8,12},{5,1},{9,13},{6,2},{10,14},{7,3},{11,15},{20,16},{24,... | collective-permute-start | bytes 1179656 | tf_op jit(solution)/shard_map/ppermute | solution.py:429
  89.4 0.0 collective-permute-done.6.rest_4_
  89.4 0.0 collective-permute-done.7.rest_5_
  89.4 12.5 %video.3 = (bf16[16,8,4,1536]{3,2,1,0:T(4,128)(2,1)}, bf16[16,8,4,768]{3,2,1,0:T(4,128)(2,1)}) custom-call(s32[6]{0:T(128)} %stack.43.scal, s32[1,256]{1,0:T(1,128)} %bitcast.9, bf16[16,8,4,1536]{3,2,1,0:T(4,128)(2,1)} %own_q.3, bf16[16,8,4,768]{3,2,1,0:T(4,128)(2,1)} %collective-permute-done.pair_q, ...), custom_call_target="tpu_custom_call", output_to_operand_aliasing={{0}: (12, {}), {1}: (13, {})} | custom-call | bytes 1 | tf_op jit(solution)/shard_map/video/pallas_call | solution.py:193
  102.0 0.0 collective-permute-done.12
  102.0 1.1 broadcast_select_fusion
  103.0 3.6 %collective-permute-start.13 = (bf16[256,768]{1,0:T(8,128)(2,1)S(1)}, bf16[256,768]{1,0:T(8,128)(2,1)S(1)}, u32[]{:S(2)}, u32[]{:S(2)}) collective-permute-start(bf16[256,768]{1,0:T(8,128)(2,1)S(1)} %broadcast_select_fusion), channel_id=1, source_target_pairs={{0,2},{2,0},{1,3},{3,1},{4,6},{6,4},{5,7},{7,5},{8,10},{10,8},{9,1... | collective-permute-start | bytes 1179656 | tf_op jit(solution)/shard_map/ppermute | solution.py:390
  106.7 0.1 collective-permute-start.10
  106.7 0.0 copy-start
  106.7 1.3 %collective-permute-done.13 = bf16[256,768]{1,0:T(8,128)(2,1)S(1)} collective-permute-done((bf16[256,768]{1,0:T(8,128)(2,1)S(1)}, bf16[256,768]{1,0:T(8,128)(2,1)S(1)}, u32[]{:S(2)}, u32[]{:S(2)}) %collective-permute-start.13) | collective-permute-done | bytes 393248 | tf_op jit(solution)/shard_map/ppermute | solution.py:390
  108.0 0.1 broadcast_select_fusion.2
  108.1 0.9 pad_maximum_fusion
  109.0 0.3 collective-permute-done.10
  109.3 0.0 copy-done
  109.3 0.4 constant_dynamic-update-slice_fusion
  109.8 0.0 copy-start.1
  109.8 1.1 %copy-done.1 = bf16[16,8,4,1536]{3,2,1,0:T(4,128)(2,1)} copy-done((bf16[16,8,4,1536]{3,2,1,0:T(4,128)(2,1)}, bf16[16,8,4,1536]{3,2,1,0:T(4,128)(2,1)S(1)}, u32[]{:S(2)}) %copy-start.1) | copy-done | bytes 1572888
Async XLA Ops:
  4.6 37.5 %collective-permute-start.1 = (bf16[2,6,4,2,64,128]{5,4,3,2,1,0:T(8,128)(2,1)}, bf16[2,6,4,2,64,128]{5,4,3,2,1,0:T(8,128)(2,1)}, u32[]{:S(2)}, u32[]{:S(2)}) collective-permute-start(bf16[2,6,4,2,64,128]{5,4,3,2,1,0:T(8,128)(2,1)} %pack.2.mine_ref.rest_0_), channel_id=1, source_target_pairs={{0,4},{4,8},{8,12},{1,5},{5,9},{9,13},{2,6},{6,10},{10,14},{3,7},{... | collective-permute-start | bytes 4718600 | tf_op jit(solution)/shard_map/ppermute | solution.py:401
  7.8 37.2 %collective-permute-start.2 = (bf16[2,6,4,2,64,128]{5,4,3,2,1,0:T(8,128)(2,1)}, bf16[2,6,4,2,64,128]{5,4,3,2,1,0:T(8,128)(2,1)}, u32[]{:S(2)}, u32[]{:S(2)}) collective-permute-start(bf16[2,6,4,2,64,128]{5,4,3,2,1,0:T(8,128)(2,1)} %pack.2.mine_ref.rest_0_), channel_id=1, source_target_pairs={{4,0},{8,4},{12,8},{5,1},{9,5},{13,9},{6,2},{10,6},{14,10},{7,3},{... | collective-permute-start | bytes 4718600 | tf_op jit(solution)/shard_map/ppermute | solution.py:401
  13.5 3.5 %collective-permute-start = (bf16[16,8,4,768]{3,2,1,0:T(4,128)(2,1)}, bf16[16,8,4,768]{3,2,1,0:T(4,128)(2,1)}, u32[]{:S(2)}, u32[]{:S(2)}) collective-permute-start(bf16[16,8,4,768]{3,2,1,0:T(4,128)(2,1)} %get-tuple-element.19), channel_id=1, source_target_pairs={{0,2},{2,0},{1,3},{3,1},{4,6},{6,4},{5,7},{7,5},{8,10},{10,8},{9,1... | collective-permute-start | bytes 2359304 | tf_op jit(solution)/shard_map/ppermute | solution.py:390
  14.8 3.4 %collective-permute-start.4 = (bf16[2,3,4,2,64,128]{5,4,3,2,1,0:T(8,128)(2,1)}, bf16[2,3,4,2,64,128]{5,4,3,2,1,0:T(8,128)(2,1)}, u32[]{:S(2)}, u32[]{:S(2)}) collective-permute-start(bf16[2,3,4,2,64,128]{5,4,3,2,1,0:T(8,128)(2,1)} %get-tuple-element.22), channel_id=1, source_target_pairs={{0,2},{2,0},{1,3},{3,1},{4,6},{6,4},{5,7},{7,5},{8,10},{10,8},{9,1... | collective-permute-start | bytes 2359304 | tf_op jit(solution)/shard_map/ppermute | solution.py:390
  14.8 4.5 %collective-permute-start.3 = (bf16[2,3,4,2,64,128]{5,4,3,2,1,0:T(8,128)(2,1)}, bf16[2,3,4,2,64,128]{5,4,3,2,1,0:T(8,128)(2,1)}, u32[]{:S(2)}, u32[]{:S(2)}) collective-permute-start(bf16[2,3,4,2,64,128]{5,4,3,2,1,0:T(8,128)(2,1)} %get-tuple-element.20), channel_id=1, source_target_pairs={{0,2},{2,0},{1,3},{3,1},{4,6},{6,4},{5,7},{7,5},{8,10},{10,8},{9,1... | collective-permute-start | bytes 2359304 | tf_op jit(solution)/shard_map/ppermute | solution.py:390
  27.7 27.1 %collective-permute-start.5 = (bf16[7,256,128]{2,1,0:T(8,128)(2,1)}, bf16[7,256,128]{2,1,0:T(8,128)(2,1)}, u32[]{:S(2)}, u32[]{:S(2)}) collective-permute-start(bf16[7,256,128]{2,1,0:T(8,128)(2,1)} %get-tuple-element.26), channel_id=1, source_target_pairs={{0,4},{12,8},{1,5},{13,9},{2,6},{14,10},{3,7},{15,11},{16,20},{28,... | collective-permute-start | bytes 1376264 | tf_op jit(solution)/shard_map/ppermute | solution.py:412
  29.0 35.8 %collective-permute-start.8 = (bf16[2,3,4,2,64,128]{5,4,3,2,1,0:T(8,128)(2,1)}, bf16[2,3,4,2,64,128]{5,4,3,2,1,0:T(8,128)(2,1)}, u32[]{:S(2)}, u32[]{:S(2)}) collective-permute-start(bf16[2,3,4,2,64,128]{5,4,3,2,1,0:T(8,128)(2,1)} %collective-permute-done.4.rest_0_.rest_3_), channel_id=1, source_target_pairs={{0,4},{4,8},{8,12},{1,5},{5,9},{9,13},{2,6},{6,10},{10,14},{3,7},{... | collective-permute-start | bytes 2359304 | tf_op jit(solution)/shard_map/ppermute | solution.py:401
  34.1 37.5 %collective-permute-start.9 = (bf16[2,3,4,2,64,128]{5,4,3,2,1,0:T(8,128)(2,1)}, bf16[2,3,4,2,64,128]{5,4,3,2,1,0:T(8,128)(2,1)}, u32[]{:S(2)}, u32[]{:S(2)}) collective-permute-start(bf16[2,3,4,2,64,128]{5,4,3,2,1,0:T(8,128)(2,1)} %collective-permute-done.4.rest_0_.rest_3_), channel_id=1, source_target_pairs={{4,0},{8,4},{12,8},{5,1},{9,5},{13,9},{6,2},{10,6},{14,10},{7,3},{... | collective-permute-start | bytes 2359304 | tf_op jit(solution)/shard_map/ppermute | solution.py:401
  57.6 26.6 %collective-permute-start.11 = (bf16[7,256,128]{2,1,0:T(8,128)(2,1)}, bf16[7,256,128]{2,1,0:T(8,128)(2,1)}, u32[]{:S(2)}, u32[]{:S(2)}) collective-permute-start(bf16[7,256,128]{2,1,0:T(8,128)(2,1)} %join.1.own_ref), channel_id=1, source_target_pairs={{4,8},{8,4},{5,9},{9,5},{6,10},{10,6},{7,11},{11,7},{20,24},{24,20... | collective-permute-start | bytes 1376264 | tf_op jit(solution)/shard_map/ppermute | solution.py:414
  59.5 30.0 %collective-permute-start.6 = (bf16[2,3,4,2,64,128]{5,4,3,2,1,0:T(8,128)(2,1)}, bf16[2,3,4,2,64,128]{5,4,3,2,1,0:T(8,128)(2,1)}, u32[]{:S(2)}, u32[]{:S(2)}) collective-permute-start(bf16[2,3,4,2,64,128]{5,4,3,2,1,0:T(8,128)(2,1)} %collective-permute-done.3.rest_1_.rest_3_), channel_id=1, source_target_pairs={{0,4},{4,8},{8,12},{1,5},{5,9},{9,13},{2,6},{6,10},{10,14},{3,7},{... | collective-permute-start | bytes 2359304 | tf_op jit(solution)/shard_map/ppermute | solution.py:401
  61.4 28.0 %collective-permute-start.7 = (bf16[2,3,4,2,64,128]{5,4,3,2,1,0:T(8,128)(2,1)}, bf16[2,3,4,2,64,128]{5,4,3,2,1,0:T(8,128)(2,1)}, u32[]{:S(2)}, u32[]{:S(2)}) collective-permute-start(bf16[2,3,4,2,64,128]{5,4,3,2,1,0:T(8,128)(2,1)} %collective-permute-done.3.rest_1_.rest_3_), channel_id=1, source_target_pairs={{4,0},{8,4},{12,8},{5,1},{9,5},{13,9},{6,2},{10,6},{14,10},{7,3},{... | collective-permute-start | bytes 2359304 | tf_op jit(solution)/shard_map/ppermute | solution.py:401
  87.4 14.6 %collective-permute-start.12 = (bf16[256,768]{1,0:T(8,128)(2,1)}, bf16[256,768]{1,0:T(8,128)(2,1)}, u32[]{:S(2)}, u32[]{:S(2)}) collective-permute-start(bf16[256,768]{1,0:T(8,128)(2,1)} %finish.1), channel_id=1, source_target_pairs={{4,0},{8,12},{5,1},{9,13},{6,2},{10,14},{7,3},{11,15},{20,16},{24,... | collective-permute-start | bytes 1179656 | tf_op jit(solution)/shard_map/ppermute | solution.py:429
  103.0 5.0 %collective-permute-start.13 = (bf16[256,768]{1,0:T(8,128)(2,1)S(1)}, bf16[256,768]{1,0:T(8,128)(2,1)S(1)}, u32[]{:S(2)}, u32[]{:S(2)}) collective-permute-start(bf16[256,768]{1,0:T(8,128)(2,1)S(1)} %broadcast_select_fusion), channel_id=1, source_target_pairs={{0,2},{2,0},{1,3},{3,1},{4,6},{6,4},{5,7},{7,5},{8,10},{10,8},{9,1... | collective-permute-start | bytes 1179656 | tf_op jit(solution)/shard_map/ppermute | solution.py:390
  106.7 2.7 %collective-permute-start.10 = (bf16[16,8,4,768]{3,2,1,0:T(4,128)(2,1)}, bf16[16,8,4,768]{3,2,1,0:T(4,128)(2,1)S(1)}, u32[]{:S(2)}, u32[]{:S(2)}) collective-permute-start(bf16[16,8,4,768]{3,2,1,0:T(4,128)(2,1)} %get-tuple-element.31), channel_id=1, source_target_pairs={{0,2},{2,0},{1,3},{3,1},{4,6},{6,4},{5,7},{7,5},{8,10},{10,8},{9,1... | collective-permute-start | bytes 2359304 | tf_op jit(solution)/shard_map/ppermute | solution.py:390
  106.7 2.6 %copy-start = (bf16[16,8,4,1536]{3,2,1,0:T(4,128)(2,1)S(1)}, bf16[16,8,4,1536]{3,2,1,0:T(4,128)(2,1)}, u32[]{:S(2)}) copy-start(bf16[16,8,4,1536]{3,2,1,0:T(4,128)(2,1)} %get-tuple-element.30) | copy-start | bytes 4718596
  109.8 1.1 %copy-start.1 = (bf16[16,8,4,1536]{3,2,1,0:T(4,128)(2,1)}, bf16[16,8,4,1536]{3,2,1,0:T(4,128)(2,1)S(1)}, u32[]{:S(2)}) copy-start(bf16[16,8,4,1536]{3,2,1,0:T(4,128)(2,1)S(1)} %constant_dynamic-update-slice_fusion) | copy-start | bytes 4718596
